TPU v7x, 32 devices: a whole 2x2x4 slice. The times are simulated.
32 devices in a mesh: shard: 4 (over y, x), mp: 4 (over z), segment: 2 (over core).
Axes of the slice: x: 2, y: 2, z: 4, core: 2. Of those that a mesh axis runs over, the one named last changes fastest.
Arguments:
- store_tokens: int32 [256, 48], P('shard'), may hold values from 0 to 16383
- retrieved: int32 [4, 12], replicated, may hold values from 0 to 63
- owner_shard: int32 [48, 1], replicated, may hold values from 0 to 3; in each aligned block of 12 rows (0 to 11, 12 to 23, ...) at most 3 rows name the same one
- targets: int32 [4, 64], P('shard'), may hold values from 0 to 16383
- vocab_table: bfloat16 [16384, 4096], P(None, ('mp', 'segment')), may hold values from -6 to 6
- norm_gains: float32 [3, 4096], replicated, may hold values from 0.1 to 1.9
- layer_weights: bfloat16 [2, 4, 4096, 4096], P('segment', None, 'shard', 'mp'), may hold values from -0.09375 to 0.09375
Outputs:
- encoded: bfloat16 [2304, 4096], P('shard', ('mp', 'segment'))
- decoded: bfloat16 [256, 4096], P('shard', ('mp', 'segment'))
Inputs may be any that keep to these rules, and one draw needn't show every extreme that they name: `owner_shard`: within the 12 passages of one question no shard owns more than 3; in every draw some question has exactly 3 passages from one shard.
All inputs are finite; a program needn't handle non-finite values.
Results may differ from a plain program's by a relative error of at most 0.015.
Values may be sent and summed in bfloat16 or wider, within the bound.
A program may use at most 128 MiB of HBM per device.

v0:
```python
import jax
import jax.numpy as jnp
from jax import lax
from jax.sharding import PartitionSpec as P

D = 4096
DH = 64


epsilon = 1e-06


def attend(query_rows, key_rows, value_rows, head_count):
    batch_size = query_rows.shape[0]
    head_size = query_rows.shape[2] // head_count
    query_heads = query_rows.reshape(batch_size, query_rows.shape[1], head_count, head_size)
    key_heads = key_rows.reshape(batch_size, key_rows.shape[1], head_count, head_size)
    value_heads = value_rows.reshape(batch_size, value_rows.shape[1], head_count, head_size)
    scores = jnp.einsum(
        "brhd,bshd->bhrs", query_heads, key_heads, preferred_element_type=jnp.float32
    ) * head_size ** (-0.5)
    shifted = jnp.exp(scores - jnp.max(scores, axis=-1, keepdims=True))
    attention = (shifted / jnp.sum(shifted, axis=-1, keepdims=True)).astype(jnp.bfloat16)
    mixture = jnp.einsum(
        "bhrs,bshd->brhd", attention, value_heads, preferred_element_type=jnp.float32
    )
    return mixture.astype(jnp.bfloat16).reshape(
        batch_size * query_rows.shape[1], head_count * head_size
    )


def swap_segments(block):
    segments = lax.axis_size("segment")
    me = lax.axis_index("segment")
    half = block.shape[3] // segments
    kept = lax.dynamic_slice_in_dim(block[0], me * half, half, axis=2)
    sent = lax.dynamic_slice_in_dim(block[0], (1 - me) * half, half, axis=2)
    other = lax.ppermute(sent, "segment", [(0, 1), (1, 0)])
    return jnp.where(me == 0, kept, other), jnp.where(me == 0, other, kept)


def shard_pieces(block):
    count = lax.axis_size("shard")
    me = lax.axis_index("shard")
    rows = block.shape[1]
    if count != 4:
        whole = lax.all_gather(block, "shard", axis=1, tiled=True)
        return [(i, 0, whole[:, i * rows : (i + 1) * rows]) for i in range(count)]
    across_x = [(i, i ^ 1) for i in range(4)]
    across_y = [(i, i ^ 2) for i in range(4)]
    from_x = lax.ppermute(block, "shard", across_x)
    from_y = lax.ppermute(block, "shard", across_y)
    top = lax.ppermute(from_y[:, : rows // 2], "shard", across_x)
    bottom = lax.ppermute(from_x[:, rows // 2 :], "shard", across_y)
    return [
        (me, 0, block),
        (me ^ 1, 0, from_x),
        (me ^ 2, 0, from_y),
        (me ^ 3, 0, top),
        (me ^ 3, rows // 2, bottom),
    ]


def after(value, pieces):
    return lax.optimization_barrier((value, pieces[-1][2], pieces[-2][2]))[0]


def project(rows_in, pieces, shard_rows):
    total = None
    for owner, first, block in pieces:
        depth = block.shape[1]
        part = lax.dynamic_slice_in_dim(rows_in, owner * shard_rows + first, depth, axis=1)
        term = jnp.einsum("rn,knh->rkh", part, block, preferred_element_type=jnp.float32)
        total = term if total is None else total + term
    return total


def in_order(pieces, shard_rows):
    columns = pieces[0][2].shape[2]
    whole = jnp.zeros((D, columns), jnp.bfloat16)
    for owner, first, block in pieces:
        whole = lax.dynamic_update_slice_in_dim(
            whole, block[0], owner * shard_rows + first, axis=0
        )
    return whole


def body(store_tokens, retrieved, owner_shard, targets, vocab_table, norm_gains, layer_weights):
    shard_count = lax.axis_size("shard")
    my_shard = lax.axis_index("shard")
    per_question = retrieved.shape[1]
    length = store_tokens.shape[1]
    slot_cap = max(2, (per_question + shard_count - 1) // shard_count)
    owners = owner_shard.reshape(retrieved.shape)
    positions = jnp.arange(per_question)
    before = positions[None, :] < positions[:, None]
    matches = owners[:, :, None] == owners[:, None, :]
    slot_rank = jnp.sum(jnp.where(matches & before[None], 1, 0), axis=2).astype(jnp.int32)
    slot_numbers = jnp.arange(slot_cap)
    chosen = (owners[:, None, :] == my_shard) & (
        slot_rank[:, None, :] == slot_numbers[None, :, None]
    )
    local_rows = jnp.sum(jnp.where(chosen, retrieved[:, None, :], 0), axis=2)
    send_ids = jnp.take(store_tokens, local_rows.reshape(-1), axis=0).reshape(
        shard_count, slot_cap, length
    )
    arrived = lax.all_to_all(send_ids, "shard", split_axis=0, concat_axis=0, tiled=True)
    mine_owner = lax.dynamic_index_in_dim(owners, my_shard, 0, keepdims=False)
    mine_rank = lax.dynamic_index_in_dim(slot_rank, my_shard, 0, keepdims=False)
    arrived_rows = arrived.reshape(shard_count * slot_cap, length)
    passage_ids = jnp.take(arrived_rows, mine_owner * slot_cap + mine_rank, axis=0).reshape(-1)
    enc_qkv, dec_qkv = swap_segments(layer_weights[:, 0:3])
    enc_out, dec_out = swap_segments(layer_weights[:, 3:4])
    shard_rows = layer_weights.shape[2]
    enc_pieces = shard_pieces(enc_qkv)
    enc_out_pieces = shard_pieces(after(enc_out, enc_pieces))
    dec_pieces = shard_pieces(after(dec_qkv, enc_out_pieces))
    dec_out_pieces = shard_pieces(after(dec_out, dec_pieces))
    head_block = enc_qkv.shape[2]
    head_count = head_block // DH
    pass_rows = passage_ids.shape[0]
    all_ids = jnp.concatenate([passage_ids, targets.reshape(-1)])
    embedded_part = jnp.take(vocab_table, all_ids, axis=0)
    piece = lax.all_gather(embedded_part, ("mp", "segment"), axis=1, tiled=True)
    passage_part = embedded_part[:pass_rows]
    target_part = embedded_part[pass_rows:]
    rows_f32 = piece.astype(jnp.float32)
    scale = lax.rsqrt(jnp.sum(rows_f32 * rows_f32, axis=1) / D + epsilon)
    pass_normed = (rows_f32[:pass_rows] * norm_gains[0]).astype(jnp.bfloat16)
    targ_normed = (rows_f32[pass_rows:] * norm_gains[1]).astype(jnp.bfloat16)

    accum = project(pass_normed, enc_pieces, shard_rows)
    projected = (accum * scale[:pass_rows, None, None]).astype(jnp.bfloat16)
    shaped = projected.reshape(per_question, length, 3, head_block)
    context = attend(shaped[:, :, 0], shaped[:, :, 1], shaped[:, :, 2], head_count)
    enc_partial = lax.dot_general(
        context,
        in_order(enc_out_pieces, shard_rows),
        (((1,), (1,)), ((), ())),
        preferred_element_type=jnp.float32,
    )
    encoded = (
        passage_part.astype(jnp.float32)
        + lax.psum_scatter(
            enc_partial.astype(jnp.bfloat16), ("mp", "segment"), scatter_dimension=1, tiled=True
        ).astype(jnp.float32)
    ).astype(jnp.bfloat16)

    enc_f32 = lax.all_gather(encoded, ("mp", "segment"), axis=1, tiled=True).astype(jnp.float32)
    enc_scale = lax.rsqrt(jnp.sum(enc_f32 * enc_f32, axis=1) / D + epsilon)
    enc_normed = (enc_f32 * norm_gains[2]).astype(jnp.bfloat16)
    query_pieces = [(o, f, b[0:1]) for o, f, b in dec_pieces]
    cross_pieces = [(o, f, b[1:3]) for o, f, b in dec_pieces]
    targ_accum = project(targ_normed, query_pieces, shard_rows)[:, 0]
    queries = (targ_accum * scale[pass_rows:, None]).astype(jnp.bfloat16)[None]
    cross_accum = project(enc_normed, cross_pieces, shard_rows)
    key_values = (cross_accum * enc_scale[:, None, None]).astype(jnp.bfloat16)
    dec_context = attend(queries, key_values[None, :, 0], key_values[None, :, 1], head_count)
    dec_partial = lax.dot_general(
        dec_context,
        in_order(dec_out_pieces, shard_rows),
        (((1,), (1,)), ((), ())),
        preferred_element_type=jnp.float32,
    )
    decoded = (
        target_part.astype(jnp.float32)
        + lax.psum_scatter(
            dec_partial.astype(jnp.bfloat16), ("mp", "segment"), scatter_dimension=1, tiled=True
        ).astype(jnp.float32)
    ).astype(jnp.bfloat16)
    return (encoded, decoded)


def solution(mesh):
    placed = (
        P("shard", None),
        P(),
        P(),
        P("shard", None),
        P(None, ("mp", "segment")),
        P(),
        P("segment", None, "shard", "mp"),
    )
    return jax.shard_map(
        body,
        mesh=mesh,
        in_specs=placed,
        out_specs=(P("shard", ("mp", "segment")), P("shard", ("mp", "segment"))),
        check_vma=False,
    )
```

profile of v0, /device:TPU:0, one launch (start us, length us, event | category | flops | bytes accessed | tf_op | source)
XLA Modules:
  0.0 493.6 jit_solution(7201991522954827821)
XLA Ops:
  7.2 6.1 %slice.105 = bf16[1,3,1024,1024]{3,2,1,0:T(8,128)(2,1)} slice(bf16[1,4,1024,1024]{3,2,1,0:T(8,128)(2,1)} %param.13), slice={[0:1], [0:3], [0:1024], [0:1024]} | slice | bytes 12582912 | tf_op jit(solution)/shard_map/slice | solution.py:112
  13.3 2.1 dynamic-slice_bitcast_fusion
  19.7 4.7 all-to-all-start
  24.7 4.5 all-to-all-done
  31.3 11.2 %gather_fusion.2 = bf16[640,512]{1,0:T(8,128)(2,1)} fusion(bf16[16384,512]{1,0:T(8,128)(2,1)} %param.11, s32[1024]{0:T(1024)S(1)} %pad_clamp_fusion), kind=kCustom, calls=%fused_computation.2 | custom fusion | bytes 1313280 | tf_op jit(solution)/shard_map/jit(_take)/gather | solution.py:123
  42.6 2.1 broadcast_select_fusion
  45.0 5.9 %bitcast_select_fusion = (bf16[3,1024,512]{2,1,0:T(8,128)(2,1)}, bf16[3,1024,512]{2,1,0:T(8,128)(2,1)S(1)}) fusion(bf16[3,1024,512]{2,1,0:T(8,128)(2,1)} %collective-permute-done, pred[]{:T(512)S(6)} %eq.51, bf16[1,3,1024,1024]{3,2,1,0:T(8,128)(2,1)} %slice.105, s32[]{:T(128)S(6)} %select_n.172), kind=kLoop, calls=%fused_computation.15 | loop fusion | flops 3145728 | bytes 12582917 | tf_op jit(solution)/shard_map/jit(_where)/select_n | solution.py:39
  52.0 67.9 %collective-permute-done.2 = bf16[3,1024,512]{2,1,0:T(8,128)(2,1)S(1)} collective-permute-done((bf16[3,1024,512]{2,1,0:T(8,128)(2,1)S(1)}, bf16[3,1024,512]{2,1,0:T(8,128)(2,1)S(1)}, u32[]{:S(2)}, u32[]{:S(2)}) %collective-permute-start.2) | collective-permute-done | bytes 3145760 | tf_op jit(solution)/shard_map/ppermute | solution.py:52
  124.9 1.8 slice.112
  126.9 2.8 collective-permute-done.5
  129.6 1.7 bitcast_select_fusion.2
  131.3 24.7 %collective-permute-done.3 = bf16[3,512,512]{2,1,0:T(8,128)(2,1)} collective-permute-done((bf16[3,512,512]{2,1,0:T(8,128)(2,1)}, bf16[3,512,512]{2,1,0:T(8,128)(2,1)}, u32[]{:S(2)}, u32[]{:S(2)}) %collective-permute-start.3) | collective-permute-done | bytes 1572896 | tf_op jit(solution)/shard_map/ppermute | solution.py:53
  156.0 2.5 collective-permute-done.4
  158.5 1.4 collective-permute-start.6
  160.6 2.2 broadcast.170.clone
  163.9 17.8 %collective-permute-done.7 = bf16[1,1024,512]{2,1,0:T(8,128)(2,1)S(1)} collective-permute-done((bf16[1,1024,512]{2,1,0:T(8,128)(2,1)S(1)}, bf16[1,1024,512]{2,1,0:T(8,128)(2,1)S(1)}, u32[]{:S(2)}, u32[]{:S(2)}) %collective-permute-start.7) | collective-permute-done | bytes 1048608 | tf_op jit(solution)/shard_map/ppermute | solution.py:52
  187.5 4.0 convert_element_type.73
  191.6 3.8 fusion.4
  195.3 1.6 copy-done
  196.9 4.4 fusion.24
  203.7 2.0 fusion.20
  205.7 2.0 fusion.22
  207.7 2.5 fusion.56
  210.2 3.0 multiply_convert_fusion
  215.0 1.7 reshape_squeeze.10
  217.5 2.1 fusion.101
  220.2 2.2 fusion.16
  223.5 1.9 bitcast_dynamic-update-slice_fusion.9
  225.4 1.9 bitcast_dynamic-update-slice_fusion.8
  227.3 6.4 %convolution_convert_fusion = bf16[576,4096]{1,0:T(8,128)(2,1)} fusion(bf16[576,512]{1,0:T(8,128)(2,1)S(1)} %reshape.317, bf16[4096,512]{1,0:T(8,128)(2,1)} %bitcast_dynamic-update-slice_fusion.8), kind=kOutput, calls=%fused_computation.12 | convolution fusion | flops 2418278400 | bytes 9502720 | tf_op jit(solution)/shard_map/dot_general | solution.py:136
  233.8 55.3 %reduce-scatter.3.cloned.1.call-done = bf16[576,512]{1,0:T(8,128)(2,1)} async-done(((bf16[576,4096]{1,0:T(8,128)(2,1)}), bf16[576,512]{1,0:T(8,128)(2,1)}) %reduce-scatter.3.cloned.1.call-update) | async-done | bytes 589840 | tf_op jit(solution)/shard_map/reduce_scatter | solution.py:144
  289.1 2.0 add_convert_fusion
  291.5 1.5 collective-permute-start.11
  293.0 1.5 collective-permute-start.10
  294.5 64.9 %collective-permute-done.11 = bf16[3,1024,512]{2,1,0:T(8,128)(2,1)S(1)} collective-permute-done((bf16[3,1024,512]{2,1,0:T(8,128)(2,1)}, bf16[3,1024,512]{2,1,0:T(8,128)(2,1)S(1)}, u32[]{:S(2)}, u32[]{:S(2)}) %collective-permute-start.11) | collective-permute-done | bytes 3145760 | tf_op jit(solution)/shard_map/ppermute | solution.py:52
  359.5 1.5 collective-permute-start.12
  362.8 1.8 fusion.40
  364.6 1.5 fusion.47
  366.2 28.2 %collective-permute-done.12 = bf16[3,512,512]{2,1,0:T(8,128)(2,1)S(1)} collective-permute-done((bf16[3,512,512]{2,1,0:T(8,128)(2,1)S(1)}, bf16[3,512,512]{2,1,0:T(8,128)(2,1)S(1)}, u32[]{:S(2)}, u32[]{:S(2)}) %collective-permute-start.12) | collective-permute-done | bytes 1572896 | tf_op jit(solution)/shard_map/ppermute | solution.py:53
  394.3 1.5 collective-permute-start.14
  399.0 2.2 broadcast.170.clone.1
  402.3 16.0 %collective-permute-done.15 = bf16[1,1024,512]{2,1,0:T(8,128)(2,1)} collective-permute-done((bf16[1,1024,512]{2,1,0:T(8,128)(2,1)S(1)}, bf16[1,1024,512]{2,1,0:T(8,128)(2,1)}, u32[]{:S(2)}, u32[]{:S(2)}) %collective-permute-start.15) | collective-permute-done | bytes 1048608 | tf_op jit(solution)/shard_map/ppermute | solution.py:52
  421.4 2.3 bitcast_dynamic-update-slice_fusion
  423.7 5.9 %collective-permute-done.16 = bf16[1,512,512]{2,1,0:T(8,128)(2,1)S(1)} collective-permute-done((bf16[1,512,512]{2,1,0:T(8,128)(2,1)S(1)}, bf16[1,512,512]{2,1,0:T(8,128)(2,1)S(1)}, u32[]{:S(2)}, u32[]{:S(2)}) %collective-permute-start.16) | collective-permute-done | bytes 524320 | tf_op jit(solution)/shard_map/ppermute | solution.py:53
  431.2 4.4 fusion.3
  445.2 4.4 convolution_convert_fusion.1
  449.6 35.9 %reduce-scatter.5.cloned.1.call-done = bf16[64,512]{1,0:T(8,128)(2,1)} async-done(((bf16[64,4096]{1,0:T(8,128)(2,1)}), bf16[64,512]{1,0:T(8,128)(2,1)}) %reduce-scatter.5.cloned.1.call-update) | async-done | bytes 65552 | tf_op jit(solution)/shard_map/reduce_scatter | solution.py:167
  485.5 1.5 add_convert_fusion.1
  (161 shorter events, 47.7 us)
Async XLA Ops:
  13.3 3.2 copy-start.23
  13.3 4.5 copy-start.22
  13.3 4.8 copy-start.20
  13.3 17.9 %copy-start.21 = (s32[1,64]{1,0:T(1,128)S(1)}, s32[1,64]{1,0:T(1,128)}, u32[]{:S(2)}) copy-start(s32[1,64]{1,0:T(1,128)} %param.10) | copy-start | bytes 772
  15.5 29.5 %collective-permute-start = (bf16[3,1024,512]{2,1,0:T(8,128)(2,1)S(1)}, bf16[3,1024,512]{2,1,0:T(8,128)(2,1)}, u32[]{:S(2)}, u32[]{:S(2)}) collective-permute-start(bf16[3,1024,512]{2,1,0:T(8,128)(2,1)S(1)} %dynamic-slice_bitcast_fusion), channel_id=1, source_target_pairs={{0,1},{1,0},{2,3},{3,2},{4,5},{5,4},{6,7},{7,6},{8,9},{9,8},{10,11... | collective-permute-start | bytes 9437192 | tf_op jit(solution)/shard_map/ppermute | solution.py:38
  19.7 9.4 %all-to-all-start = ((s32[4,1,144]{2,1,0:T(1,128)}), s32[4,1,144]{2,1,0:T(1,128)S(1)}, u32[]{:S(2)}, u32[]{:S(2)}) async-start(s32[4,1,144]{2,1,0:T(1,128)} %reshape.372), calls=%async_computation | async-start | bytes 8192 | tf_op jit(solution)/shard_map/all_to_all | solution.py:107
  24.4 163.0 %all-gather.3.cloned.1.call-start = ((), (), s32[]{:S(2)}) async-start(), calls=%async_computation.3 | async-start | bytes 5898240 | tf_op jit(solution)/shard_map/all_gather | solution.py:124
  44.7 244.4 %reduce-scatter.3.cloned.1.call-start = ((), (), s32[]{:S(2)}) async-start(), calls=%async_computation.4 | async-start | bytes 5308416 | tf_op jit(solution)/shard_map/reduce_scatter | solution.py:144
  50.8 72.4 %copy-start.4 = (bf16[3,1024,512]{2,1,0:T(8,128)(2,1)}, bf16[3,1024,512]{2,1,0:T(8,128)(2,1)S(1)}, u32[]{:S(2)}) copy-start(bf16[3,1024,512]{2,1,0:T(8,128)(2,1)S(1)} %get-tuple-element.9) | copy-start | bytes 9437188
  50.8 69.1 %collective-permute-start.2 = (bf16[3,1024,512]{2,1,0:T(8,128)(2,1)S(1)}, bf16[3,1024,512]{2,1,0:T(8,128)(2,1)S(1)}, u32[]{:S(2)}, u32[]{:S(2)}) collective-permute-start(bf16[3,1024,512]{2,1,0:T(8,128)(2,1)S(1)} %get-tuple-element.9), channel_id=1, source_target_pairs={{0,16},{8,24},{16,0},{24,8},{1,17},{9,25},{17,1},{25,9},{2,18},{10... | collective-permute-start | bytes 9437192 | tf_op jit(solution)/shard_map/ppermute | solution.py:52
  51.4 70.4 %collective-permute-start.1 = (bf16[3,1024,512]{2,1,0:T(8,128)(2,1)S(1)}, bf16[3,1024,512]{2,1,0:T(8,128)(2,1)S(1)}, u32[]{:S(2)}, u32[]{:S(2)}) collective-permute-start(bf16[3,1024,512]{2,1,0:T(8,128)(2,1)S(1)} %get-tuple-element.9), channel_id=1, source_target_pairs={{0,8},{8,0},{16,24},{24,16},{1,9},{9,1},{17,25},{25,17},{2,10},{10... | collective-permute-start | bytes 9437192 | tf_op jit(solution)/shard_map/ppermute | solution.py:51
  119.9 3.3 copy-start.15
  121.3 34.8 %collective-permute-start.3 = (bf16[3,512,512]{2,1,0:T(8,128)(2,1)}, bf16[3,512,512]{2,1,0:T(8,128)(2,1)}, u32[]{:S(2)}, u32[]{:S(2)}) collective-permute-start(bf16[3,512,512]{2,1,0:T(8,128)(2,1)} %slice.144), channel_id=1, source_target_pairs={{0,8},{8,0},{16,24},{24,16},{1,9},{9,1},{17,25},{25,17},{2,10},{10... | collective-permute-start | bytes 4718600 | tf_op jit(solution)/shard_map/ppermute | solution.py:53
  121.8 2.2 copy-start.17
  124.0 34.5 %collective-permute-start.4 = (bf16[3,512,512]{2,1,0:T(8,128)(2,1)}, bf16[3,512,512]{2,1,0:T(8,128)(2,1)}, u32[]{:S(2)}, u32[]{:S(2)}) collective-permute-start(bf16[3,512,512]{2,1,0:T(8,128)(2,1)} %slice.145), channel_id=1, source_target_pairs={{0,16},{8,24},{16,0},{24,8},{1,17},{9,25},{17,1},{25,9},{2,18},{10... | collective-permute-start | bytes 4718600 | tf_op jit(solution)/shard_map/ppermute | solution.py:54
  126.6 33.9 %copy-start.19 = (f32[3,4096]{1,0:T(4,128)S(1)}, f32[3,4096]{1,0:T(4,128)}, u32[]{:S(2)}) copy-start(f32[3,4096]{1,0:T(4,128)} %param.12) | copy-start | bytes 147460
  126.8 2.9 collective-permute-start.5
  158.5 24.7 %collective-permute-start.6 = (bf16[1,1024,512]{2,1,0:T(8,128)(2,1)S(1)}, bf16[1,1024,512]{2,1,0:T(8,128)(2,1)S(1)}, u32[]{:S(2)}, u32[]{:S(2)}) collective-permute-start(bf16[1,1024,512]{2,1,0:T(8,128)(2,1)S(1)} %get-tuple-element.5), channel_id=1, source_target_pairs={{0,8},{8,0},{16,24},{24,16},{1,9},{9,1},{17,25},{25,17},{2,10},{10... | collective-permute-start | bytes 3145736 | tf_op jit(solution)/shard_map/ppermute | solution.py:51
  160.0 21.7 %collective-permute-start.7 = (bf16[1,1024,512]{2,1,0:T(8,128)(2,1)S(1)}, bf16[1,1024,512]{2,1,0:T(8,128)(2,1)S(1)}, u32[]{:S(2)}, u32[]{:S(2)}) collective-permute-start(bf16[1,1024,512]{2,1,0:T(8,128)(2,1)S(1)} %get-tuple-element.5), channel_id=1, source_target_pairs={{0,16},{8,24},{16,0},{24,8},{1,17},{9,25},{17,1},{25,9},{2,18},{10... | collective-permute-start | bytes 3145736 | tf_op jit(solution)/shard_map/ppermute | solution.py:52
  182.5 41.0 %collective-permute-start.8 = (bf16[1,512,512]{2,1,0:T(8,128)(2,1)}, bf16[1,512,512]{2,1,0:T(8,128)(2,1)}, u32[]{:S(2)}, u32[]{:S(2)}) collective-permute-start(bf16[1,512,512]{2,1,0:T(8,128)(2,1)} %slice.149), channel_id=1, source_target_pairs={{0,8},{8,0},{16,24},{24,16},{1,9},{9,1},{17,25},{25,17},{2,10},{10... | collective-permute-start | bytes 1572872 | tf_op jit(solution)/shard_map/ppermute | solution.py:53
  184.0 41.4 %collective-permute-start.9 = (bf16[1,512,512]{2,1,0:T(8,128)(2,1)}, bf16[1,512,512]{2,1,0:T(8,128)(2,1)}, u32[]{:S(2)}, u32[]{:S(2)}) collective-permute-start(bf16[1,512,512]{2,1,0:T(8,128)(2,1)} %slice.150), channel_id=1, source_target_pairs={{0,16},{8,24},{16,0},{24,8},{1,17},{9,25},{17,1},{25,9},{2,18},{10... | collective-permute-start | bytes 1572872 | tf_op jit(solution)/shard_map/ppermute | solution.py:54
  187.5 13.8 %slice-start = ((s8[5242880]{0:T(1024)(128)(4,1)}), s8[4194304]{0:T(1024)(128)(4,1)S(1)}, s32[]{:S(2)}) async-start(s8[5242880]{0:T(1024)(128)(4,1)} %bitcast.125), calls=%async_computation.7 | async-start | bytes 8388608
  191.5 5.4 %copy-start = (f32[640,4096]{1,0:T(8,128)}, f32[640,4096]{1,0:T(8,128)S(1)}, u32[]{:S(2)}) copy-start(f32[640,4096]{1,0:T(8,128)S(1)} %convert_element_type.73) | copy-start | bytes 31457284
  191.6 9.8 %slice-start.1 = ((s8[5242880]{0:T(1024)(128)(4,1)}), s8[1048576]{0:T(1024)(128)(4,1)S(1)}, s32[]{:S(2)}) async-start(s8[5242880]{0:T(1024)(128)(4,1)} %bitcast.125), calls=%async_computation.8 | async-start | bytes 2097152
  196.9 5.5 %copy-start.16 = (bf16[3,1024,512]{2,1,0:T(8,128)(2,1)S(1)}, bf16[3,1024,512]{2,1,0:T(8,128)(2,1)}, u32[]{:S(2)}) copy-start(bf16[3,1024,512]{2,1,0:T(8,128)(2,1)} %copy-done.15) | copy-start | bytes 9437188
  201.3 2.3 copy-start.1
  203.7 2.0 copy-start.18
  217.5 2.2 copy-start.5
  233.7 55.4 %copy-start.2 = (bf16[640,512]{1,0:T(8,128)(2,1)S(1)}, bf16[640,512]{1,0:T(8,128)(2,1)}, u32[]{:S(2)}) copy-start(bf16[640,512]{1,0:T(8,128)(2,1)} %broadcast_select_fusion) | copy-start | bytes 1966084
  233.7 197.5 %all-gather.5.cloned.1.call-start = ((), (), s32[]{:S(2)}) async-start(), calls=%async_computation.5 | async-start | bytes 5308416 | tf_op jit(solution)/shard_map/all_gather | solution.py:149
  291.1 194.4 %reduce-scatter.5.cloned.1.call-start = ((), (), s32[]{:S(2)}) async-start(), calls=%async_computation.6 | async-start | bytes 589824 | tf_op jit(solution)/shard_map/reduce_scatter | solution.py:167
  291.5 68.0 %collective-permute-start.11 = (bf16[3,1024,512]{2,1,0:T(8,128)(2,1)}, bf16[3,1024,512]{2,1,0:T(8,128)(2,1)S(1)}, u32[]{:S(2)}, u32[]{:S(2)}) collective-permute-start(bf16[3,1024,512]{2,1,0:T(8,128)(2,1)} %get-tuple-element.6), channel_id=1, source_target_pairs={{0,16},{8,24},{16,0},{24,8},{1,17},{9,25},{17,1},{25,9},{2,18},{10... | collective-permute-start | bytes 9437192 | tf_op jit(solution)/shard_map/ppermute | solution.py:52
  293.0 69.2 %collective-permute-start.10 = (bf16[3,1024,512]{2,1,0:T(8,128)(2,1)}, bf16[3,1024,512]{2,1,0:T(8,128)(2,1)S(1)}, u32[]{:S(2)}, u32[]{:S(2)}) collective-permute-start(bf16[3,1024,512]{2,1,0:T(8,128)(2,1)} %get-tuple-element.6), channel_id=1, source_target_pairs={{0,8},{8,0},{16,24},{24,16},{1,9},{9,1},{17,25},{25,17},{2,10},{10... | collective-permute-start | bytes 9437192 | tf_op jit(solution)/shard_map/ppermute | solution.py:51
  359.4 38.4 %copy-start.6 = (bf16[3,1024,512]{2,1,0:T(8,128)(2,1)}, bf16[3,1024,512]{2,1,0:T(8,128)(2,1)S(1)}, u32[]{:S(2)}) copy-start(bf16[3,1024,512]{2,1,0:T(8,128)(2,1)S(1)} %collective-permute-done.11) | copy-start | bytes 9437188
  359.5 34.8 %collective-permute-start.12 = (bf16[3,512,512]{2,1,0:T(8,128)(2,1)S(1)}, bf16[3,512,512]{2,1,0:T(8,128)(2,1)S(1)}, u32[]{:S(2)}, u32[]{:S(2)}) collective-permute-start(bf16[3,512,512]{2,1,0:T(8,128)(2,1)S(1)} %slice.154), channel_id=1, source_target_pairs={{0,8},{8,0},{16,24},{24,16},{1,9},{9,1},{17,25},{25,17},{2,10},{10... | collective-permute-start | bytes 4718600 | tf_op jit(solution)/shard_map/ppermute | solution.py:53
  362.2 35.2 %copy-start.8 = (bf16[3,1024,512]{2,1,0:T(8,128)(2,1)}, bf16[3,1024,512]{2,1,0:T(8,128)(2,1)S(1)}, u32[]{:S(2)}) copy-start(bf16[3,1024,512]{2,1,0:T(8,128)(2,1)S(1)} %collective-permute-done.10) | copy-start | bytes 9437188
  362.3 32.0 %collective-permute-start.13 = (bf16[3,512,512]{2,1,0:T(8,128)(2,1)S(1)}, bf16[3,512,512]{2,1,0:T(8,128)(2,1)S(1)}, u32[]{:S(2)}, u32[]{:S(2)}) collective-permute-start(bf16[3,512,512]{2,1,0:T(8,128)(2,1)S(1)} %slice.156), channel_id=1, source_target_pairs={{0,16},{8,24},{16,0},{24,8},{1,17},{9,25},{17,1},{25,9},{2,18},{10... | collective-permute-start | bytes 4718600 | tf_op jit(solution)/shard_map/ppermute | solution.py:54
  394.3 3.3 copy-start.10
  394.3 3.5 copy-start.12
  394.3 25.6 %collective-permute-start.14 = (bf16[1,1024,512]{2,1,0:T(8,128)(2,1)S(1)}, bf16[1,1024,512]{2,1,0:T(8,128)(2,1)S(1)}, u32[]{:S(2)}, u32[]{:S(2)}) collective-permute-start(bf16[1,1024,512]{2,1,0:T(8,128)(2,1)S(1)} %get-tuple-element.7), channel_id=1, source_target_pairs={{0,8},{8,0},{16,24},{24,16},{1,9},{9,1},{17,25},{25,17},{2,10},{10... | collective-permute-start | bytes 3145736 | tf_op jit(solution)/shard_map/ppermute | solution.py:51
  395.9 22.4 %collective-permute-start.15 = (bf16[1,1024,512]{2,1,0:T(8,128)(2,1)S(1)}, bf16[1,1024,512]{2,1,0:T(8,128)(2,1)}, u32[]{:S(2)}, u32[]{:S(2)}) collective-permute-start(bf16[1,1024,512]{2,1,0:T(8,128)(2,1)S(1)} %get-tuple-element.7), channel_id=1, source_target_pairs={{0,16},{8,24},{16,0},{24,8},{1,17},{9,25},{17,1},{25,9},{2,18},{10... | collective-permute-start | bytes 3145736 | tf_op jit(solution)/shard_map/ppermute | solution.py:52
  419.4 10.2 %collective-permute-start.16 = (bf16[1,512,512]{2,1,0:T(8,128)(2,1)S(1)}, bf16[1,512,512]{2,1,0:T(8,128)(2,1)S(1)}, u32[]{:S(2)}, u32[]{:S(2)}) collective-permute-start(bf16[1,512,512]{2,1,0:T(8,128)(2,1)S(1)} %slice.165), channel_id=1, source_target_pairs={{0,8},{8,0},{16,24},{24,16},{1,9},{9,1},{17,25},{25,17},{2,10},{10... | collective-permute-start | bytes 1572872 | tf_op jit(solution)/shard_map/ppermute | solution.py:53
  420.0 10.4 %collective-permute-start.17 = (bf16[1,512,512]{2,1,0:T(8,128)(2,1)S(1)}, bf16[1,512,512]{2,1,0:T(8,128)(2,1)S(1)}, u32[]{:S(2)}, u32[]{:S(2)}) collective-permute-start(bf16[1,512,512]{2,1,0:T(8,128)(2,1)S(1)} %slice.166), channel_id=1, source_target_pairs={{0,16},{8,24},{16,0},{24,8},{1,17},{9,25},{17,1},{25,9},{2,18},{10... | collective-permute-start | bytes 1572872 | tf_op jit(solution)/shard_map/ppermute | solution.py:54
  431.2 4.4 copy-start.3
  435.7 1.4 copy-start.11
  437.1 1.9 copy-start.7
  439.0 1.9 copy-start.9
  440.8 1.4 copy-start.13
  (1 other events, 1.0 us)
Sparse Core Ops, SparseCore 0:
  44.8 55.3 all-gather.2
  233.8 55.2 reduce-scatter.2
  291.3 50.0 all-gather.4
  449.8 35.7 reduce-scatter.4
where the time goes:
time: 495 us; the launch traced here: 494 us
  waiting for transfers between devices  328 us (66%)
  local copies, waits for them, and re-layouts  60.5 us (12%)
  matrix products  37.1 us (7%)
  other arithmetic  32.8 us (7%)
  starting transfers between devices  21.1 us (4%)
  between operations  14.3 us (3%)
    ppermute x4, waiting for transfers between devices, shard_pieces(): from_y = lax.ppermute(block, 'shard', across_y)  167 us
    ppermute x4, waiting for transfers between devices, shard_pieces(): top = lax.ppermute(from_y[:, :rows // 2], 'shard', across_x)  58.8 us
    reduce_scatter x1, waiting for transfers between devices, body(): lax.psum_scatter(enc_partial.astype(jnp.bfloat16), ('mp', 'segment'), sca...  55.3 us
    reduce_scatter x1, waiting for transfers between devices, body(): lax.psum_scatter(dec_partial.astype(jnp.bfloat16), ('mp', 'segment'), sca...  35.9 us
    dot_general x15, matrix products, project(): jnp.einsum('rn,knh->rkh', part, block, preferred_element_type=jnp.float32)  22.2 us
    dynamic_update_slice x10, local copies, waits for them, and re-layouts, in_order(): lax.dynamic_update_slice_in_dim(whole, block[0], owner * shard_rows + fir...  12.9 us
    gather x1, local copies, waits for them, and re-layouts, body(): embedded_part = jnp.take(vocab_table, all_ids, axis=0)  11.2 us
  transfers between devices with their start and end apart: 23, of which 13 were waited for; matrix products, arithmetic and copies ran while one was open for 18% of the time, Pallas kernels for 0%

commit v1 on v0

--- a/solution.py
+++ b/solution.py
@@ -29,44 +29,63 @@
     )
 
 
-def swap_segments(block):
-    segments = lax.axis_size("segment")
+def after(value, *others):
+    return lax.optimization_barrier((value,) + others)[0]
+
+
+def swap_segments(weights, first, count):
     me = lax.axis_index("segment")
-    half = block.shape[3] // segments
-    kept = lax.dynamic_slice_in_dim(block[0], me * half, half, axis=2)
-    sent = lax.dynamic_slice_in_dim(block[0], (1 - me) * half, half, axis=2)
+    rows, half = weights.shape[2], weights.shape[3] // 2
+    size = (1, count, rows, half)
+    kept = lax.dynamic_slice(weights, (0, first, 0, me * half), size)[0]
+    sent = lax.dynamic_slice(weights, (0, first, 0, (1 - me) * half), size)[0]
     other = lax.ppermute(sent, "segment", [(0, 1), (1, 0)])
-    return jnp.where(me == 0, kept, other), jnp.where(me == 0, other, kept)
-
-
-def shard_pieces(block):
+    encoder = jnp.where(me == 0, kept, other)
+
+    def decoder(*others):
+        late_kept, late_other = lax.optimization_barrier((kept, other) + others)[:2]
+        return jnp.where(me == 0, late_other, late_kept)
+
+    return encoder, decoder
+
+
+X_PAIRS = [(i, i ^ 1) for i in range(4)]
+Y_PAIRS = [(i, i ^ 2) for i in range(4)]
+
+
+def near(block):
     count = lax.axis_size("shard")
     me = lax.axis_index("shard")
     rows = block.shape[1]
     if count != 4:
         whole = lax.all_gather(block, "shard", axis=1, tiled=True)
         return [(i, 0, whole[:, i * rows : (i + 1) * rows]) for i in range(count)]
-    across_x = [(i, i ^ 1) for i in range(4)]
-    across_y = [(i, i ^ 2) for i in range(4)]
-    from_x = lax.ppermute(block, "shard", across_x)
-    from_y = lax.ppermute(block, "shard", across_y)
-    top = lax.ppermute(from_y[:, : rows // 2], "shard", across_x)
-    bottom = lax.ppermute(from_x[:, rows // 2 :], "shard", across_y)
     return [
         (me, 0, block),
-        (me ^ 1, 0, from_x),
-        (me ^ 2, 0, from_y),
-        (me ^ 3, 0, top),
-        (me ^ 3, rows // 2, bottom),
+        (me ^ 1, 0, lax.ppermute(block, "shard", X_PAIRS)),
+        (me ^ 2, 0, lax.ppermute(block, "shard", Y_PAIRS)),
     ]
 
 
-def after(value, pieces):
-    return lax.optimization_barrier((value, pieces[-1][2], pieces[-2][2]))[0]
-
-
-def project(rows_in, pieces, shard_rows):
-    total = None
+def far(pieces):
+    if lax.axis_size("shard") != 4:
+        return []
+    me = lax.axis_index("shard")
+    rows = pieces[0][2].shape[1]
+    top = lax.ppermute(pieces[2][2][:, : rows // 2], "shard", X_PAIRS)
+    bottom = lax.ppermute(pieces[1][2][:, rows // 2 :], "shard", Y_PAIRS)
+    return [(me ^ 3, 0, top), (me ^ 3, rows // 2, bottom)]
+
+
+def blocks(pieces):
+    return [piece[2] for piece in pieces]
+
+
+def pick(pieces, first, stop):
+    return [(owner, row, block[first:stop]) for owner, row, block in pieces]
+
+
+def project(rows_in, pieces, shard_rows, total=None):
     for owner, first, block in pieces:
         depth = block.shape[1]
         part = lax.dynamic_slice_in_dim(rows_in, owner * shard_rows + first, depth, axis=1)
@@ -88,6 +107,7 @@
 def body(store_tokens, retrieved, owner_shard, targets, vocab_table, norm_gains, layer_weights):
     shard_count = lax.axis_size("shard")
     my_shard = lax.axis_index("shard")
+    enc_qkv, dec_qkv = swap_segments(layer_weights, 0, 3)
     per_question = retrieved.shape[1]
     length = store_tokens.shape[1]
     slot_cap = max(2, (per_question + shard_count - 1) // shard_count)
@@ -104,18 +124,14 @@
     send_ids = jnp.take(store_tokens, local_rows.reshape(-1), axis=0).reshape(
         shard_count, slot_cap, length
     )
+    send_ids = after(send_ids, enc_qkv)
     arrived = lax.all_to_all(send_ids, "shard", split_axis=0, concat_axis=0, tiled=True)
     mine_owner = lax.dynamic_index_in_dim(owners, my_shard, 0, keepdims=False)
     mine_rank = lax.dynamic_index_in_dim(slot_rank, my_shard, 0, keepdims=False)
     arrived_rows = arrived.reshape(shard_count * slot_cap, length)
     passage_ids = jnp.take(arrived_rows, mine_owner * slot_cap + mine_rank, axis=0).reshape(-1)
-    enc_qkv, dec_qkv = swap_segments(layer_weights[:, 0:3])
-    enc_out, dec_out = swap_segments(layer_weights[:, 3:4])
+    enc_out, dec_out = swap_segments(layer_weights, 3, 1)
     shard_rows = layer_weights.shape[2]
-    enc_pieces = shard_pieces(enc_qkv)
-    enc_out_pieces = shard_pieces(after(enc_out, enc_pieces))
-    dec_pieces = shard_pieces(after(dec_qkv, enc_out_pieces))
-    dec_out_pieces = shard_pieces(after(dec_out, dec_pieces))
     head_block = enc_qkv.shape[2]
     head_count = head_block // DH
     pass_rows = passage_ids.shape[0]
@@ -129,45 +145,55 @@
     pass_normed = (rows_f32[:pass_rows] * norm_gains[0]).astype(jnp.bfloat16)
     targ_normed = (rows_f32[pass_rows:] * norm_gains[1]).astype(jnp.bfloat16)
 
-    accum = project(pass_normed, enc_pieces, shard_rows)
+    enc_near = near(enc_qkv)
+    accum = project(pass_normed, enc_near, shard_rows)
+    enc_far = far(enc_near)
+    out_near = near(after(enc_out, accum))
+    accum = project(pass_normed, enc_far, shard_rows, accum)
+    cross_near = near(dec_qkv(*blocks(out_near))[1:3])
+    out_far = far(out_near)
     projected = (accum * scale[:pass_rows, None, None]).astype(jnp.bfloat16)
     shaped = projected.reshape(per_question, length, 3, head_block)
     context = attend(shaped[:, :, 0], shaped[:, :, 1], shaped[:, :, 2], head_count)
     enc_partial = lax.dot_general(
         context,
-        in_order(enc_out_pieces, shard_rows),
+        in_order(out_near + out_far, shard_rows),
         (((1,), (1,)), ((), ())),
         preferred_element_type=jnp.float32,
-    )
-    encoded = (
-        passage_part.astype(jnp.float32)
-        + lax.psum_scatter(
-            enc_partial.astype(jnp.bfloat16), ("mp", "segment"), scatter_dimension=1, tiled=True
-        ).astype(jnp.float32)
     ).astype(jnp.bfloat16)
-
-    enc_f32 = lax.all_gather(encoded, ("mp", "segment"), axis=1, tiled=True).astype(jnp.float32)
+    enc_sum = lax.psum_scatter(
+        enc_partial, ("mp", "segment"), scatter_dimension=1, tiled=True
+    ).astype(jnp.float32)
+    enc_sum = after(enc_sum, *blocks(cross_near))
+    encoded = (passage_part.astype(jnp.float32) + enc_sum).astype(jnp.bfloat16)
+
+    whole_encoded = lax.all_gather(encoded, ("mp", "segment"), axis=1, tiled=True)
+    cross_far = far(cross_near)
+    late = jnp.concatenate(
+        [dec_qkv(*blocks(cross_near))[0:1], dec_out(*blocks(cross_near))], axis=0
+    )
+    late_near = near(late)
+    whole_encoded = after(whole_encoded, *blocks(cross_far), *blocks(late_near))
+    late_far = far(late_near)
+    enc_f32 = whole_encoded.astype(jnp.float32)
     enc_scale = lax.rsqrt(jnp.sum(enc_f32 * enc_f32, axis=1) / D + epsilon)
     enc_normed = (enc_f32 * norm_gains[2]).astype(jnp.bfloat16)
-    query_pieces = [(o, f, b[0:1]) for o, f, b in dec_pieces]
-    cross_pieces = [(o, f, b[1:3]) for o, f, b in dec_pieces]
-    targ_accum = project(targ_normed, query_pieces, shard_rows)[:, 0]
+    cross_accum = project(enc_normed, cross_near + cross_far, shard_rows)
+    key_values = (cross_accum * enc_scale[:, None, None]).astype(jnp.bfloat16)
+    targ_accum = project(targ_normed, pick(late_near + late_far, 0, 1), shard_rows)[:, 0]
     queries = (targ_accum * scale[pass_rows:, None]).astype(jnp.bfloat16)[None]
-    cross_accum = project(enc_normed, cross_pieces, shard_rows)
-    key_values = (cross_accum * enc_scale[:, None, None]).astype(jnp.bfloat16)
     dec_context = attend(queries, key_values[None, :, 0], key_values[None, :, 1], head_count)
     dec_partial = lax.dot_general(
         dec_context,
-        in_order(dec_out_pieces, shard_rows),
+        in_order(pick(late_near + late_far, 1, 2), shard_rows),
         (((1,), (1,)), ((), ())),
         preferred_element_type=jnp.float32,
-    )
-    decoded = (
-        target_part.astype(jnp.float32)
-        + lax.psum_scatter(
-            dec_partial.astype(jnp.bfloat16), ("mp", "segment"), scatter_dimension=1, tiled=True
-        ).astype(jnp.float32)
     ).astype(jnp.bfloat16)
+    terms = lax.all_to_all(
+        dec_partial, ("mp", "segment"), split_axis=1, concat_axis=0, tiled=True
+    )
+    terms = terms.reshape(-1, target_part.shape[0], target_part.shape[1]).astype(jnp.float32)
+    decoded = (target_part.astype(jnp.float32) + jnp.sum(terms, axis=0)).astype(jnp.bfloat16)
     return (encoded, decoded)
 
 

time: 495 us -> 417 us (0.84)
  waiting for transfers between devices: 328 us -> 210 us
  blocking collectives: 0 us -> 19.4 us
  other arithmetic: 32.8 us -> 41.4 us
  matrix products: 37.1 us -> 44.8 us
    ppermute x16, waiting for transfers between devices: 229 us -> 150 us  [the longest x4 59.6 us: near(): lax.ppermute(block, 'shard', Y_PAIRS)]
    reduce_scatter x2 -> x1, waiting for transfers between devices: 91.2 us -> 49.9 us  [body(): lax.psum_scatter(enc_partial, ('mp', 'segment'), scatter_dimension=1, til...]
    all_to_all x0 -> x1, blocking collectives: none -> 19.4 us  [body(): lax.all_to_all(dec_partial, ('mp', 'segment'), split_axis=1, concat_axis=...]
    dot_general x15, matrix products: 22.2 us -> 31.7 us  [project(): jnp.einsum('rn,knh->rkh', part, block, preferred_element_type=jnp.float32)]
    select_n x2 -> x4, other arithmetic: 7.53 us -> 13.3 us  [the longest x2 8.71 us: swap_segments(): encoder = jnp.where(me == 0, kept, other)]
    squeeze x1 -> x3, local copies, waits for them, and re-layouts: 0.82 us -> 6.13 us  [the longest x2 6.03 us: swap_segments(): sent = lax.dynamic_slice(weights, (0, first, 0, (1 - me) * half), size)[0]]
    dynamic_update_slice x10 -> x9, local copies, waits for them, and re-layouts: 12.9 us -> 9.91 us  [in_order(): lax.dynamic_update_slice_in_dim(whole, block[0], owner * shard_rows + fir...]
    slice x10 -> x8, local copies, waits for them, and re-layouts: 13.6 us -> 12.3 us  [the longest x4 6.16 us: far(): top = lax.ppermute(pieces[2][2][:, :rows // 2], 'shard', X_PAIRS)]
  transfers between devices with their start and end apart: 23 -> 22, of which waited for: 13 -> 11; matrix products, arithmetic and copies ran while one was open for 18% -> 21% of each run, Pallas kernels for 0% -> 0%
where the time goes in v1:
time: 417 us; the launch traced here: 415 us
  waiting for transfers between devices  210 us (50%)
  local copies, waits for them, and re-layouts  63.9 us (15%)
  matrix products  44.8 us (11%)
  other arithmetic  41.4 us (10%)
  starting transfers between devices  21.8 us (5%)
  blocking collectives  19.4 us (5%)
  between operations  14.2 us (3%)
    ppermute x4, waiting for transfers between devices, near(): lax.ppermute(block, 'shard', Y_PAIRS)  59.6 us
    reduce_scatter x1, waiting for transfers between devices, body(): lax.psum_scatter(enc_partial, ('mp', 'segment'), scatter_dimension=1, til...  49.9 us
    ppermute x4, waiting for transfers between devices, far(): bottom = lax.ppermute(pieces[1][2][:, rows // 2:], 'shard', Y_PAIRS)  39 us
    ppermute x4, waiting for transfers between devices, near(): lax.ppermute(block, 'shard', X_PAIRS)  38.6 us
    dot_general x15, matrix products, project(): jnp.einsum('rn,knh->rkh', part, block, preferred_element_type=jnp.float32)  31.7 us
    all_to_all x1, blocking collectives, body(): lax.all_to_all(dec_partial, ('mp', 'segment'), split_axis=1, concat_axis=...  19.4 us
    ppermute x4, waiting for transfers between devices, far(): top = lax.ppermute(pieces[2][2][:, :rows // 2], 'shard', X_PAIRS)  13.1 us
    gather x1, local copies, waits for them, and re-layouts, body(): embedded_part = jnp.take(vocab_table, all_ids, axis=0)  11.2 us
  transfers between devices with their start and end apart: 22, of which 11 were waited for; matrix products, arithmetic and copies ran while one was open for 21% of the time, Pallas kernels for 0%

profile of v1, /device:TPU:0, one launch (start us, length us, event | category | flops | bytes accessed | tf_op | source)
XLA Modules:
  0.0 415.5 jit_solution(2503603504219693196)
XLA Ops:
  7.2 3.7 dynamic-slice_bitcast_fusion
  14.6 2.2 collective-permute-done
  16.9 5.7 %broadcast_select_fusion = (bf16[3,1024,512]{2,1,0:T(8,128)(2,1)}, bf16[3,1024,512]{2,1,0:T(8,128)(2,1)}) fusion(bf16[3,1024,512]{2,1,0:T(8,128)(2,1)S(1)} %collective-permute-done, pred[]{:T(512)S(6)} %eq.52, bf16[1,4,1024,1024]{3,2,1,0:T(8,128)(2,1)} %param.13, s32[]{:T(128)S(6)} %select_n.169), kind=kLoop, calls=%fused_computation.18 | loop fusion | flops 1572864 | bytes 12582917 | tf_op jit(solution)/shard_map/jit(_where)/select_n | solution.py:43
  23.3 5.1 %all-to-all-start = ((s32[4,1,144]{2,1,0:T(1,128)}), s32[4,1,144]{2,1,0:T(1,128)S(1)}, u32[]{:S(2)}, u32[]{:S(2)}) async-start(s32[4,1,144]{2,1,0:T(1,128)} %reshape.373), calls=%async_computation | async-start | bytes 8192 | tf_op jit(solution)/shard_map/all_to_all | solution.py:128
  28.4 4.7 %all-to-all-done = s32[4,1,144]{2,1,0:T(1,128)S(1)} async-done(((s32[4,1,144]{2,1,0:T(1,128)}), s32[4,1,144]{2,1,0:T(1,128)S(1)}, u32[]{:S(2)}, u32[]{:S(2)}) %all-to-all-start) | async-done | bytes 2336 | tf_op jit(solution)/shard_map/all_to_all | solution.py:128
  35.2 11.2 %gather_fusion.2 = bf16[640,512]{1,0:T(8,128)(2,1)} fusion(bf16[16384,512]{1,0:T(8,128)(2,1)} %param.11, s32[1024]{0:T(1024)S(1)} %pad_clamp_fusion), kind=kCustom, calls=%fused_computation.2 | custom fusion | bytes 1313280 | tf_op jit(solution)/shard_map/jit(_take)/gather | solution.py:139
  46.5 2.1 broadcast_select_fusion.3
  50.0 2.3 dynamic-slice_bitcast_fusion.2
  52.4 3.0 collective-permute-done.5
  55.3 3.0 broadcast_select_fusion.2
  58.3 59.6 %collective-permute-done.2 = bf16[3,1024,512]{2,1,0:T(8,128)(2,1)} collective-permute-done((bf16[3,1024,512]{2,1,0:T(8,128)(2,1)}, bf16[3,1024,512]{2,1,0:T(8,128)(2,1)}, u32[]{:S(2)}, u32[]{:S(2)}) %collective-permute-start.2) | collective-permute-done | bytes 3145760 | tf_op jit(solution)/shard_map/ppermute | solution.py:66
  117.9 2.7 slice.136
  121.2 2.7 slice.137
  124.5 3.9 convert_element_type.74
  129.6 2.8 copy-done
  132.4 3.9 fusion.23
  136.3 4.0 fusion.21
  140.3 4.1 add_add_fusion
  148.5 9.8 %collective-permute-done.3 = bf16[3,512,512]{2,1,0:T(8,128)(2,1)} collective-permute-done((bf16[3,512,512]{2,1,0:T(8,128)(2,1)}, bf16[3,512,512]{2,1,0:T(8,128)(2,1)}, u32[]{:S(2)}, u32[]{:S(2)}) %collective-permute-start.3) | collective-permute-done | bytes 1572896 | tf_op jit(solution)/shard_map/ppermute | solution.py:75
  158.3 2.5 fusion.54
  161.6 2.7 multiply_convert_fusion
  165.6 2.5 reshape_squeeze.11
  168.0 2.5 reshape_squeeze.10
  170.6 2.5 reshape_squeeze.9
  173.0 2.4 fusion.26
  175.4 4.2 %fusion.101 = (f32[12,8,48]{2,1,0:T(8,128)S(1)}, f32[12,8,48,48]{2,3,1,0:T(8,128)S(1)}) fusion(f32[12,8,48,48]{2,3,1,0:T(8,128)S(1)} %fusion.26), kind=kOutput, calls=%fused_computation.162 | output fusion | flops 884783 | bytes 1787904 | tf_op jit(solution)/shard_map/sub | solution.py:22
  181.6 2.7 reshape.318
  192.9 3.3 collective-permute-done.8
  196.3 2.6 collective-permute-done.9
  198.9 4.3 %convolution_convert_fusion = bf16[576,4096]{1,0:T(8,128)(2,1)} fusion(bf16[576,512]{1,0:T(8,128)(2,1)S(1)} %copy-done.5, bf16[4096,512]{1,0:T(8,128)(2,1)S(1)} %bitcast_dynamic-update-slice_fusion.4), kind=kOutput, calls=%fused_computation.12 | convolution fusion | flops 2418278400 | bytes 9502720 | tf_op jit(solution)/shard_map/dot_general | solution.py:158
  203.5 3.2 slice_select_fusion
  207.9 49.9 %reduce-scatter.2.cloned.1.call-done = bf16[576,512]{1,0:T(8,128)(2,1)} async-done(((bf16[576,4096]{1,0:T(8,128)(2,1)}), bf16[576,512]{1,0:T(8,128)(2,1)}) %reduce-scatter.2.cloned.1.call-update) | async-done | bytes 589840 | tf_op jit(solution)/shard_map/reduce_scatter | solution.py:164
  259.0 2.1 add_convert_fusion
  262.5 2.3 broadcast.170.clone.1
  264.7 2.6 bitcast_dynamic-update-slice_fusion
  271.8 2.3 slice.146
  274.7 2.3 slice.147
  277.6 38.6 %collective-permute-done.14 = bf16[2,1024,512]{2,1,0:T(8,128)(2,1)S(1)} collective-permute-done((bf16[2,1024,512]{2,1,0:T(8,128)(2,1)S(1)}, bf16[2,1024,512]{2,1,0:T(8,128)(2,1)S(1)}, u32[]{:S(2)}, u32[]{:S(2)}) %collective-permute-start.14) | collective-permute-done | bytes 2097184 | tf_op jit(solution)/shard_map/ppermute | solution.py:65
  322.0 35.6 %collective-permute-done.17 = bf16[2,512,512]{2,1,0:T(8,128)(2,1)S(1)} collective-permute-done((bf16[2,512,512]{2,1,0:T(8,128)(2,1)S(1)}, bf16[2,512,512]{2,1,0:T(8,128)(2,1)S(1)}, u32[]{:S(2)}, u32[]{:S(2)}) %collective-permute-start.17) | collective-permute-done | bytes 1048608 | tf_op jit(solution)/shard_map/ppermute | solution.py:76
  361.3 1.9 fusion.60
  363.1 4.3 %fusion.3 = (f32[576]{0:T(1024)S(1)}, bf16[576,4096]{1,0:T(8,128)(2,1)S(1)}) fusion(bf16[576,4096]{1,0:T(8,128)(2,1)} %all-gather.5.cloned.1.call-done, f32[4096]{0:T(1024)S(1)} %bitcast.154), kind=kLoop, calls=%fused_computation.9 | loop fusion | flops 11795904 | bytes 9455872 | tf_op jit(solution)/shard_map/reduce_sum | solution.py:179
  367.4 3.0 fusion.15
  370.4 2.0 fusion.48
  372.4 3.0 fusion.11
  375.4 3.0 fusion.13
  378.4 2.3 multiply_convert_fusion.1
  384.4 3.6 convolution_convert_fusion.1
  388.0 19.4 %all_to_all.18 = bf16[64,8,512]{2,0,1:T(8,128)(2,1)S(1)} all-to-all(bf16[64,8,512]{2,0,1:T(8,128)(2,1)S(1)} %bitcast.151), channel_id=1, replica_groups=mesh['shard'=4,'mp'=4,'segment'=2] {'mp','segment'}, dimensions={1} | all-to-all | bytes 1048576 | tf_op jit(solution)/shard_map/all_to_all | solution.py:192
  (137 shorter events, 51.6 us)
Async XLA Ops:
  7.2 4.2 %copy-start.7 = (s32[64,48]{0,1:T(8,128)S(1)}, s32[64,48]{0,1:T(8,128)}, u32[]{:S(2)}) copy-start(s32[64,48]{0,1:T(8,128)} %param.7) | copy-start | bytes 36868
  7.2 4.8 %copy-start.10 = (s32[48,1]{0,1:T(1,128)S(1)}, s32[48,1]{0,1:T(1,128)}, u32[]{:S(2)}) copy-start(s32[48,1]{0,1:T(1,128)} %param.9) | copy-start | bytes 580
  7.2 6.1 %copy-start.9 = (s32[4,12]{1,0:T(4,128)S(1)}, s32[4,12]{1,0:T(4,128)}, u32[]{:S(2)}) copy-start(s32[4,12]{1,0:T(4,128)} %param.8) | copy-start | bytes 580
  10.9 6.0 %collective-permute-start = (bf16[3,1024,512]{2,1,0:T(8,128)(2,1)}, bf16[3,1024,512]{2,1,0:T(8,128)(2,1)S(1)}, u32[]{:S(2)}, u32[]{:S(2)}) collective-permute-start(bf16[3,1024,512]{2,1,0:T(8,128)(2,1)} %dynamic-slice_bitcast_fusion), channel_id=1, source_target_pairs={{0,1},{1,0},{2,3},{3,2},{4,5},{5,4},{6,7},{7,6},{8,9},{9,8},{10,11... | collective-permute-start | bytes 9437192 | tf_op jit(solution)/shard_map/ppermute | solution.py:42
  14.6 20.5 %copy-start.8 = (s32[1,64]{1,0:T(1,128)S(1)}, s32[1,64]{1,0:T(1,128)}, u32[]{:S(2)}) copy-start(s32[1,64]{1,0:T(1,128)} %param.10) | copy-start | bytes 772
  23.3 9.8 %all-to-all-start = ((s32[4,1,144]{2,1,0:T(1,128)}), s32[4,1,144]{2,1,0:T(1,128)S(1)}, u32[]{:S(2)}, u32[]{:S(2)}) async-start(s32[4,1,144]{2,1,0:T(1,128)} %reshape.373), calls=%async_computation | async-start | bytes 8192 | tf_op jit(solution)/shard_map/all_to_all | solution.py:128
  28.4 96.1 %all-gather.3.cloned.1.call-start = ((), (), s32[]{:S(2)}) async-start(), calls=%async_computation.3 | async-start | bytes 5898240 | tf_op jit(solution)/shard_map/all_gather | solution.py:140
  46.4 5.9 %copy-start.6 = (f32[3,4096]{1,0:T(4,128)S(1)}, f32[3,4096]{1,0:T(4,128)}, u32[]{:S(2)}) copy-start(f32[3,4096]{1,0:T(4,128)} %param.12) | copy-start | bytes 147460
  48.6 209.1 %reduce-scatter.2.cloned.1.call-start = ((), (), s32[]{:S(2)}) async-start(), calls=%async_computation.4 | async-start | bytes 5308416 | tf_op jit(solution)/shard_map/reduce_scatter | solution.py:164
  48.8 69.1 %collective-permute-start.2 = (bf16[3,1024,512]{2,1,0:T(8,128)(2,1)}, bf16[3,1024,512]{2,1,0:T(8,128)(2,1)}, u32[]{:S(2)}, u32[]{:S(2)}) collective-permute-start(bf16[3,1024,512]{2,1,0:T(8,128)(2,1)} %get-tuple-element.26), channel_id=1, source_target_pairs={{0,16},{8,24},{16,0},{24,8},{1,17},{9,25},{17,1},{25,9},{2,18},{10... | collective-permute-start | bytes 9437192 | tf_op jit(solution)/shard_map/ppermute | solution.py:66
  49.5 71.8 %collective-permute-start.1 = (bf16[3,1024,512]{2,1,0:T(8,128)(2,1)}, bf16[3,1024,512]{2,1,0:T(8,128)(2,1)}, u32[]{:S(2)}, u32[]{:S(2)}) collective-permute-start(bf16[3,1024,512]{2,1,0:T(8,128)(2,1)} %get-tuple-element.26), channel_id=1, source_target_pairs={{0,8},{8,0},{16,24},{24,16},{1,9},{9,1},{17,25},{25,17},{2,10},{10... | collective-permute-start | bytes 9437192 | tf_op jit(solution)/shard_map/ppermute | solution.py:65
  52.3 3.0 collective-permute-start.5
  120.7 37.6 %collective-permute-start.3 = (bf16[3,512,512]{2,1,0:T(8,128)(2,1)}, bf16[3,512,512]{2,1,0:T(8,128)(2,1)}, u32[]{:S(2)}, u32[]{:S(2)}) collective-permute-start(bf16[3,512,512]{2,1,0:T(8,128)(2,1)} %slice.136), channel_id=1, source_target_pairs={{0,8},{8,0},{16,24},{24,16},{1,9},{9,1},{17,25},{25,17},{2,10},{10... | collective-permute-start | bytes 4718600 | tf_op jit(solution)/shard_map/ppermute | solution.py:75
  123.9 37.6 %collective-permute-start.4 = (bf16[3,512,512]{2,1,0:T(8,128)(2,1)}, bf16[3,512,512]{2,1,0:T(8,128)(2,1)}, u32[]{:S(2)}, u32[]{:S(2)}) collective-permute-start(bf16[3,512,512]{2,1,0:T(8,128)(2,1)} %slice.137), channel_id=1, source_target_pairs={{0,16},{8,24},{16,0},{24,8},{1,17},{9,25},{17,1},{25,9},{2,18},{10... | collective-permute-start | bytes 4718600 | tf_op jit(solution)/shard_map/ppermute | solution.py:76
  128.4 4.0 copy-start
  136.3 11.2 %slice-start = ((s8[5242880]{0:T(1024)(128)(4,1)}), s8[4194304]{0:T(1024)(128)(4,1)S(1)}, s32[]{:S(2)}) async-start(s8[5242880]{0:T(1024)(128)(4,1)} %bitcast.146), calls=%async_computation.6 | async-start | bytes 8388608
  140.3 7.1 %slice-start.1 = ((s8[5242880]{0:T(1024)(128)(4,1)}), s8[1048576]{0:T(1024)(128)(4,1)S(1)}, s32[]{:S(2)}) async-start(s8[5242880]{0:T(1024)(128)(4,1)} %bitcast.146), calls=%async_computation.7 | async-start | bytes 2097152
  144.4 44.1 %collective-permute-start.6 = (bf16[1,1024,512]{2,1,0:T(8,128)(2,1)}, bf16[1,1024,512]{2,1,0:T(8,128)(2,1)}, u32[]{:S(2)}, u32[]{:S(2)}) collective-permute-start(bf16[1,1024,512]{2,1,0:T(8,128)(2,1)} %get-tuple-element.13), channel_id=1, source_target_pairs={{0,8},{8,0},{16,24},{24,16},{1,9},{9,1},{17,25},{25,17},{2,10},{10... | collective-permute-start | bytes 3145736 | tf_op jit(solution)/shard_map/ppermute | solution.py:65
  146.0 40.0 %collective-permute-start.7 = (bf16[1,1024,512]{2,1,0:T(8,128)(2,1)}, bf16[1,1024,512]{2,1,0:T(8,128)(2,1)}, u32[]{:S(2)}, u32[]{:S(2)}) collective-permute-start(bf16[1,1024,512]{2,1,0:T(8,128)(2,1)} %get-tuple-element.13), channel_id=1, source_target_pairs={{0,16},{8,24},{16,0},{24,8},{1,17},{9,25},{17,1},{25,9},{2,18},{10... | collective-permute-start | bytes 3145736 | tf_op jit(solution)/shard_map/ppermute | solution.py:66
  175.4 4.3 %copy-start.2 = (bf16[12,48,8,64]{3,2,1,0:T(8,128)(2,1)S(1)}, bf16[12,48,8,64]{3,2,1,0:T(8,128)(2,1)}, u32[]{:S(2)}) copy-start(bf16[12,48,8,64]{3,2,1,0:T(8,128)(2,1)} %reshape_squeeze.9) | copy-start | bytes 1769476
  187.0 9.2 %collective-permute-start.8 = (bf16[1,512,512]{2,1,0:T(8,128)(2,1)S(1)}, bf16[1,512,512]{2,1,0:T(8,128)(2,1)S(1)}, u32[]{:S(2)}, u32[]{:S(2)}) collective-permute-start(bf16[1,512,512]{2,1,0:T(8,128)(2,1)S(1)} %slice.141), channel_id=1, source_target_pairs={{0,8},{8,0},{16,24},{24,16},{1,9},{9,1},{17,25},{25,17},{2,10},{10... | collective-permute-start | bytes 1572872 | tf_op jit(solution)/shard_map/ppermute | solution.py:75
  189.6 9.3 %copy-start.5 = (bf16[576,512]{1,0:T(8,128)(2,1)S(1)}, bf16[576,512]{1,0:T(8,128)(2,1)}, u32[]{:S(2)}) copy-start(bf16[576,512]{1,0:T(8,128)(2,1)} %reshape.318) | copy-start | bytes 1769476
  189.6 9.2 %collective-permute-start.9 = (bf16[1,512,512]{2,1,0:T(8,128)(2,1)S(1)}, bf16[1,512,512]{2,1,0:T(8,128)(2,1)S(1)}, u32[]{:S(2)}, u32[]{:S(2)}) collective-permute-start(bf16[1,512,512]{2,1,0:T(8,128)(2,1)S(1)} %slice.142), channel_id=1, source_target_pairs={{0,16},{8,24},{16,0},{24,8},{1,17},{9,25},{17,1},{25,9},{2,18},{10... | collective-permute-start | bytes 1572872 | tf_op jit(solution)/shard_map/ppermute | solution.py:76
  203.2 159.9 %all-gather.5.cloned.1.call-start = ((), (), s32[]{:S(2)}) async-start(), calls=%async_computation.5 | async-start | bytes 5308416 | tf_op jit(solution)/shard_map/all_gather | solution.py:170
  206.7 52.2 %collective-permute-start.10 = (bf16[2,1024,512]{2,1,0:T(8,128)(2,1)}, bf16[2,1024,512]{2,1,0:T(8,128)(2,1)}, u32[]{:S(2)}, u32[]{:S(2)}) collective-permute-start(bf16[2,1024,512]{2,1,0:T(8,128)(2,1)} %slice_select_fusion), channel_id=1, source_target_pairs={{0,8},{8,0},{16,24},{24,16},{1,9},{9,1},{17,25},{25,17},{2,10},{10... | collective-permute-start | bytes 6291464 | tf_op jit(solution)/shard_map/ppermute | solution.py:65
  207.3 51.6 %collective-permute-start.11 = (bf16[2,1024,512]{2,1,0:T(8,128)(2,1)}, bf16[2,1024,512]{2,1,0:T(8,128)(2,1)}, u32[]{:S(2)}, u32[]{:S(2)}) collective-permute-start(bf16[2,1024,512]{2,1,0:T(8,128)(2,1)} %slice_select_fusion), channel_id=1, source_target_pairs={{0,16},{8,24},{16,0},{24,8},{1,17},{9,25},{17,1},{25,9},{2,18},{10... | collective-permute-start | bytes 6291464 | tf_op jit(solution)/shard_map/ppermute | solution.py:66
  261.0 3.7 copy-start.1
  267.5 48.6 %collective-permute-start.14 = (bf16[2,1024,512]{2,1,0:T(8,128)(2,1)S(1)}, bf16[2,1024,512]{2,1,0:T(8,128)(2,1)S(1)}, u32[]{:S(2)}, u32[]{:S(2)}) collective-permute-start(bf16[2,1024,512]{2,1,0:T(8,128)(2,1)S(1)} %pad_maximum_fusion), channel_id=1, source_target_pairs={{0,8},{8,0},{16,24},{24,16},{1,9},{9,1},{17,25},{25,17},{2,10},{10... | collective-permute-start | bytes 6291464 | tf_op jit(solution)/shard_map/ppermute | solution.py:65
  269.0 49.0 %collective-permute-start.15 = (bf16[2,1024,512]{2,1,0:T(8,128)(2,1)S(1)}, bf16[2,1024,512]{2,1,0:T(8,128)(2,1)S(1)}, u32[]{:S(2)}, u32[]{:S(2)}) collective-permute-start(bf16[2,1024,512]{2,1,0:T(8,128)(2,1)S(1)} %pad_maximum_fusion), channel_id=1, source_target_pairs={{0,16},{8,24},{16,0},{24,8},{1,17},{9,25},{17,1},{25,9},{2,18},{10... | collective-permute-start | bytes 6291464 | tf_op jit(solution)/shard_map/ppermute | solution.py:66
  274.1 89.0 %collective-permute-start.12 = (bf16[2,512,512]{2,1,0:T(8,128)(2,1)}, bf16[2,512,512]{2,1,0:T(8,128)(2,1)}, u32[]{:S(2)}, u32[]{:S(2)}) collective-permute-start(bf16[2,512,512]{2,1,0:T(8,128)(2,1)} %slice.146), channel_id=1, source_target_pairs={{0,8},{8,0},{16,24},{24,16},{1,9},{9,1},{17,25},{25,17},{2,10},{10... | collective-permute-start | bytes 3145736 | tf_op jit(solution)/shard_map/ppermute | solution.py:75
  277.0 86.1 %collective-permute-start.13 = (bf16[2,512,512]{2,1,0:T(8,128)(2,1)}, bf16[2,512,512]{2,1,0:T(8,128)(2,1)}, u32[]{:S(2)}, u32[]{:S(2)}) collective-permute-start(bf16[2,512,512]{2,1,0:T(8,128)(2,1)} %slice.147), channel_id=1, source_target_pairs={{0,16},{8,24},{16,0},{24,8},{1,17},{9,25},{17,1},{25,9},{2,18},{10... | collective-permute-start | bytes 3145736 | tf_op jit(solution)/shard_map/ppermute | solution.py:76
  316.2 41.4 %collective-permute-start.17 = (bf16[2,512,512]{2,1,0:T(8,128)(2,1)S(1)}, bf16[2,512,512]{2,1,0:T(8,128)(2,1)S(1)}, u32[]{:S(2)}, u32[]{:S(2)}) collective-permute-start(bf16[2,512,512]{2,1,0:T(8,128)(2,1)S(1)} %slice.156), channel_id=1, source_target_pairs={{0,16},{8,24},{16,0},{24,8},{1,17},{9,25},{17,1},{25,9},{2,18},{10... | collective-permute-start | bytes 3145736 | tf_op jit(solution)/shard_map/ppermute | solution.py:76
  318.1 39.8 %collective-permute-start.16 = (bf16[2,512,512]{2,1,0:T(8,128)(2,1)S(1)}, bf16[2,512,512]{2,1,0:T(8,128)(2,1)S(1)}, u32[]{:S(2)}, u32[]{:S(2)}) collective-permute-start(bf16[2,512,512]{2,1,0:T(8,128)(2,1)S(1)} %slice.154), channel_id=1, source_target_pairs={{0,8},{8,0},{16,24},{24,16},{1,9},{9,1},{17,25},{25,17},{2,10},{10... | collective-permute-start | bytes 3145736 | tf_op jit(solution)/shard_map/ppermute | solution.py:75
  357.7 1.0 copy-start.3
  357.9 1.1 copy-start.4
Sparse Core Ops, SparseCore 0:
  48.7 55.3 all-gather.2
  203.3 54.3 reduce-scatter.1
  261.2 50.0 all-gather.4

commit v2 on v1

--- a/solution.py
+++ b/solution.py
@@ -79,10 +79,6 @@
 
 def blocks(pieces):
     return [piece[2] for piece in pieces]
-
-
-def pick(pieces, first, stop):
-    return [(owner, row, block[first:stop]) for owner, row, block in pieces]
 
 
 def project(rows_in, pieces, shard_rows, total=None):
@@ -154,7 +150,8 @@
     out_far = far(out_near)
     projected = (accum * scale[:pass_rows, None, None]).astype(jnp.bfloat16)
     shaped = projected.reshape(per_question, length, 3, head_block)
-    context = attend(shaped[:, :, 0], shaped[:, :, 1], shaped[:, :, 2], head_count)
+    values = after(shaped[:, :, 2], *blocks(out_near))
+    context = attend(shaped[:, :, 0], shaped[:, :, 1], values, head_count)
     enc_partial = lax.dot_general(
         context,
         in_order(out_near + out_far, shard_rows),
@@ -164,15 +161,21 @@
     enc_sum = lax.psum_scatter(
         enc_partial, ("mp", "segment"), scatter_dimension=1, tiled=True
     ).astype(jnp.float32)
-    enc_sum = after(enc_sum, *blocks(cross_near))
+    query_rows = lax.all_to_all(
+        after(targ_normed, enc_partial), "shard", split_axis=1, concat_axis=0, tiled=True
+    )
+    query_terms = jnp.dot(
+        query_rows, dec_qkv(enc_partial)[0], preferred_element_type=jnp.float32
+    )
+    query_terms = lax.all_to_all(query_terms, "shard", split_axis=0, concat_axis=0, tiled=True)
+    targ_accum = jnp.sum(query_terms.reshape(shard_count, -1, head_block), axis=0)
+    queries = (targ_accum * scale[pass_rows:, None]).astype(jnp.bfloat16)[None]
+    enc_sum = after(enc_sum, queries, *blocks(cross_near))
     encoded = (passage_part.astype(jnp.float32) + enc_sum).astype(jnp.bfloat16)
 
     whole_encoded = lax.all_gather(encoded, ("mp", "segment"), axis=1, tiled=True)
     cross_far = far(cross_near)
-    late = jnp.concatenate(
-        [dec_qkv(*blocks(cross_near))[0:1], dec_out(*blocks(cross_near))], axis=0
-    )
-    late_near = near(late)
+    late_near = near(dec_out(*blocks(cross_near)))
     whole_encoded = after(whole_encoded, *blocks(cross_far), *blocks(late_near))
     late_far = far(late_near)
     enc_f32 = whole_encoded.astype(jnp.float32)
@@ -180,12 +183,10 @@
     enc_normed = (enc_f32 * norm_gains[2]).astype(jnp.bfloat16)
     cross_accum = project(enc_normed, cross_near + cross_far, shard_rows)
     key_values = (cross_accum * enc_scale[:, None, None]).astype(jnp.bfloat16)
-    targ_accum = project(targ_normed, pick(late_near + late_far, 0, 1), shard_rows)[:, 0]
-    queries = (targ_accum * scale[pass_rows:, None]).astype(jnp.bfloat16)[None]
     dec_context = attend(queries, key_values[None, :, 0], key_values[None, :, 1], head_count)
     dec_partial = lax.dot_general(
         dec_context,
-        in_order(pick(late_near + late_far, 1, 2), shard_rows),
+        in_order(late_near + late_far, shard_rows),
         (((1,), (1,)), ((), ())),
         preferred_element_type=jnp.float32,
     ).astype(jnp.bfloat16)

time: 417 us -> 401 us (0.962)
  waiting for transfers between devices: 210 us -> 177 us
  starting transfers between devices: 21.8 us -> 30.8 us
  local copies, waits for them, and re-layouts: 63.9 us -> 71 us
    ppermute x4, waiting for transfers between devices: 38.6 us -> 0.01 us  [near(): lax.ppermute(block, 'shard', X_PAIRS)]
    ppermute x4, waiting for transfers between devices: 39 us -> 2.01 us  [far(): bottom = lax.ppermute(pieces[1][2][:, rows // 2:], 'shard', Y_PAIRS)]
    all_to_all x0 -> x2, waiting for transfers between devices: none -> 19.6 us  [the longest x1 19.6 us: body(): lax.all_to_all(query_terms, 'shard', split_axis=0, concat_axis=0, tiled=T...]
    ppermute x4, waiting for transfers between devices: 13.1 us -> 30.2 us  [far(): top = lax.ppermute(pieces[2][2][:, :rows // 2], 'shard', X_PAIRS)]
    all_to_all x0 -> x2, starting transfers between devices: none -> 7.87 us  [the longest x1 4.14 us: body(): lax.all_to_all(after(targ_normed, enc_partial), 'shard', split_axis=1, co...]
    dynamic_update_slice x9, local copies, waits for them, and re-layouts: 9.91 us -> 16 us  [in_order(): lax.dynamic_update_slice_in_dim(whole, block[0], owner * shard_rows + fir...]
    ppermute x4, waiting for transfers between devices: 59.6 us -> 64.7 us  [near(): lax.ppermute(block, 'shard', Y_PAIRS)]
    dot_general x15 -> x10, matrix products: 31.7 us -> 29.3 us  [project(): jnp.einsum('rn,knh->rkh', part, block, preferred_element_type=jnp.float32)]
  transfers between devices with their start and end apart: 22 -> 24, of which waited for: 11 -> 11; matrix products, arithmetic and copies ran while one was open for 21% -> 23% of each run, Pallas kernels for 0% -> 0%
where the time goes in v2:
time: 401 us; the launch traced here: 399 us
  waiting for transfers between devices  177 us (44%)
  local copies, waits for them, and re-layouts  71 us (18%)
  matrix products  46.5 us (12%)
  other arithmetic  38.4 us (10%)
  starting transfers between devices  30.8 us (8%)
  blocking collectives  21.8 us (5%)
  between operations  14.2 us (4%)
    ppermute x4, waiting for transfers between devices, near(): lax.ppermute(block, 'shard', Y_PAIRS)  64.7 us
    reduce_scatter x1, waiting for transfers between devices, body(): lax.psum_scatter(enc_partial, ('mp', 'segment'), scatter_dimension=1, til...  50.2 us
    ppermute x4, waiting for transfers between devices, far(): top = lax.ppermute(pieces[2][2][:, :rows // 2], 'shard', X_PAIRS)  30.2 us
    dot_general x10, matrix products, project(): jnp.einsum('rn,knh->rkh', part, block, preferred_element_type=jnp.float32)  29.3 us
    all_to_all x1, blocking collectives, body(): lax.all_to_all(dec_partial, ('mp', 'segment'), split_axis=1, concat_axis=...  21.8 us
    all_to_all x1, waiting for transfers between devices, body(): lax.all_to_all(query_terms, 'shard', split_axis=0, concat_axis=0, tiled=T...  19.6 us
    dynamic_update_slice x9, local copies, waits for them, and re-layouts, in_order(): lax.dynamic_update_slice_in_dim(whole, block[0], owner * shard_rows + fir...  16 us
    gather x1, local copies, waits for them, and re-layouts, body(): embedded_part = jnp.take(vocab_table, all_ids, axis=0)  11.2 us
  transfers between devices with their start and end apart: 24, of which 11 were waited for; matrix products, arithmetic and copies ran while one was open for 23% of the time, Pallas kernels for 0%

profile of v2, /device:TPU:0, one launch (start us, length us, event | category | flops | bytes accessed | tf_op | source)
XLA Modules:
  0.0 399.5 jit_solution(7183047396796194843)
XLA Ops:
  7.2 3.7 dynamic-slice_bitcast_fusion
  14.6 2.2 collective-permute-done
  16.9 5.7 %broadcast_select_fusion = (bf16[3,1024,512]{2,1,0:T(8,128)(2,1)}, bf16[3,1024,512]{2,1,0:T(8,128)(2,1)}) fusion(bf16[3,1024,512]{2,1,0:T(8,128)(2,1)S(1)} %collective-permute-done, pred[]{:T(512)S(6)} %eq.52, bf16[1,4,1024,1024]{3,2,1,0:T(8,128)(2,1)} %param.13, s32[]{:T(128)S(6)} %select_n.164), kind=kLoop, calls=%fused_computation.18 | loop fusion | flops 1572864 | bytes 12582917 | tf_op jit(solution)/shard_map/jit(_where)/select_n | solution.py:43
  23.3 5.1 %all-to-all-start = ((s32[4,1,144]{2,1,0:T(1,128)}), s32[4,1,144]{2,1,0:T(1,128)S(1)}, u32[]{:S(2)}, u32[]{:S(2)}) async-start(s32[4,1,144]{2,1,0:T(1,128)} %reshape.357), calls=%async_computation | async-start | bytes 8192 | tf_op jit(solution)/shard_map/all_to_all | solution.py:124
  28.4 4.7 %all-to-all-done = s32[4,1,144]{2,1,0:T(1,128)S(1)} async-done(((s32[4,1,144]{2,1,0:T(1,128)}), s32[4,1,144]{2,1,0:T(1,128)S(1)}, u32[]{:S(2)}, u32[]{:S(2)}) %all-to-all-start) | async-done | bytes 2336 | tf_op jit(solution)/shard_map/all_to_all | solution.py:124
  35.3 11.2 %gather_fusion.2 = bf16[640,512]{1,0:T(8,128)(2,1)} fusion(bf16[16384,512]{1,0:T(8,128)(2,1)} %param.11, s32[1024]{0:T(1024)S(1)} %pad_clamp_fusion), kind=kCustom, calls=%fused_computation.2 | custom fusion | bytes 1313280 | tf_op jit(solution)/shard_map/jit(_take)/gather | solution.py:135
  46.5 2.2 broadcast_select_fusion.3
  50.1 2.3 dynamic-slice_bitcast_fusion.2
  52.5 3.0 collective-permute-done.5
  55.4 3.0 broadcast_select_fusion.2
  58.4 59.6 %collective-permute-done.2 = bf16[3,1024,512]{2,1,0:T(8,128)(2,1)} collective-permute-done((bf16[3,1024,512]{2,1,0:T(8,128)(2,1)}, bf16[3,1024,512]{2,1,0:T(8,128)(2,1)}, u32[]{:S(2)}, u32[]{:S(2)}) %collective-permute-start.2) | collective-permute-done | bytes 3145760 | tf_op jit(solution)/shard_map/ppermute | solution.py:66
  118.0 2.8 slice.104
  121.3 2.7 slice.105
  124.5 3.9 convert_element_type.74
  129.6 2.8 copy-done
  132.4 3.9 fusion.23
  136.3 4.0 %fusion.21 = f32[576,3,512]{2,0,1:T(8,128)S(1)} fusion(bf16[3,1024,512]{2,1,0:T(8,128)(2,1)} %collective-permute-done.1, bf16[576,4096]{1,0:T(8,128)(2,1)S(1)} %fusion.4, s32[]{:T(128)S(6)} %select_n.174), kind=kOutput, calls=%fused_computation.39 | convolution fusion | flops 1811939328 | bytes 7864324 | tf_op jit(solution)/shard_map/rn,knh->rkh/dot_general | solution.py:88
  140.4 4.1 %add_add_fusion = f32[576,3,512]{2,0,1:T(8,128)S(1)} fusion(f32[576,3,512]{2,0,1:T(8,128)S(1)} %fusion.23, f32[576,3,512]{2,0,1:T(8,128)S(1)} %fusion.21, bf16[3,1024,512]{2,1,0:T(8,128)(2,1)} %collective-permute-done.2, bf16[576,4096]{1,0:T(8,128)(2,1)S(1)} %fusion.4, s32[]{:T(128)S(6)} %select_n.175), kind=kOutput, calls=%fused_computation.15 | convolution fusion | flops 1813708800 | bytes 14942212 | tf_op jit(solution)/shard_map/rn,knh->rkh/dot_general | solution.py:88
  148.6 9.8 %collective-permute-done.3 = bf16[3,512,512]{2,1,0:T(8,128)(2,1)} collective-permute-done((bf16[3,512,512]{2,1,0:T(8,128)(2,1)}, bf16[3,512,512]{2,1,0:T(8,128)(2,1)}, u32[]{:S(2)}, u32[]{:S(2)}) %collective-permute-start.3) | collective-permute-done | bytes 1572896 | tf_op jit(solution)/shard_map/ppermute | solution.py:75
  158.4 2.5 fusion.53
  161.6 2.7 multiply_convert_fusion
  165.7 2.5 reshape_squeeze.7
  168.1 2.5 reshape_squeeze.6
  175.5 5.1 %collective-permute-done.7 = bf16[1,1024,512]{2,1,0:T(8,128)(2,1)} collective-permute-done((bf16[1,1024,512]{2,1,0:T(8,128)(2,1)}, bf16[1,1024,512]{2,1,0:T(8,128)(2,1)}, u32[]{:S(2)}, u32[]{:S(2)}) %collective-permute-start.7) | collective-permute-done | bytes 1048608 | tf_op jit(solution)/shard_map/ppermute | solution.py:66
  186.4 2.5 reshape.305
  188.8 2.6 fusion.10
  192.8 2.7 reshape.306
  195.5 2.3 bitcast_dynamic-update-slice_fusion.4
  197.8 2.3 bitcast_dynamic-update-slice_fusion.3
  203.8 6.6 %convolution_convert_fusion = bf16[576,4096]{1,0:T(8,128)(2,1)} fusion(bf16[576,512]{1,0:T(8,128)(2,1)S(1)} %copy-done.7, bf16[4096,512]{1,0:T(8,128)(2,1)} %bitcast_dynamic-update-slice_fusion.8), kind=kOutput, calls=%fused_computation.12 | convolution fusion | flops 2418278400 | bytes 9502720 | tf_op jit(solution)/shard_map/dot_general | solution.py:155
  210.5 3.1 slice_select_fusion
  215.7 50.2 %reduce-scatter.2.cloned.1.call-done = bf16[576,512]{1,0:T(8,128)(2,1)} async-done(((bf16[576,4096]{1,0:T(8,128)(2,1)}), bf16[576,512]{1,0:T(8,128)(2,1)}) %reduce-scatter.2.cloned.1.call-update) | async-done | bytes 589840 | tf_op jit(solution)/shard_map/reduce_scatter | solution.py:161
  271.3 4.1 %all-to-all-start.1 = ((bf16[64,4,1024]{2,0,1:T(8,128)(2,1)}), bf16[64,4,1024]{2,0,1:T(8,128)(2,1)}, u32[]{:S(2)}, u32[]{:S(2)}) async-start(bf16[64,4,1024]{2,0,1:T(8,128)(2,1)} %bitcast.138), calls=%async_computation.2 | async-start | bytes 1048576 | tf_op jit(solution)/shard_map/all_to_all | solution.py:164
  275.5 2.2 broadcast.170.clone.1
  277.7 2.9 bitcast_dynamic-update-slice_fusion.2
  284.0 2.7 fusion.38
  286.7 3.7 all-to-all-start.2
  290.5 19.6 %all-to-all-done.2 = f32[4,64,512]{2,1,0:T(8,128)S(1)} async-done(((f32[4,64,512]{2,1,0:T(8,128)}), f32[4,64,512]{2,1,0:T(8,128)S(1)}, u32[]{:S(2)}, u32[]{:S(2)}) %all-to-all-start.2) | async-done | bytes 524320 | tf_op jit(solution)/shard_map/all_to_all | solution.py:170
  319.5 2.3 bitcast_dynamic-update-slice_fusion.1
  321.8 2.3 bitcast_dynamic-update-slice_fusion
  324.1 20.4 %collective-permute-done.16 = bf16[1,512,512]{2,1,0:T(8,128)(2,1)S(1)} collective-permute-done((bf16[1,512,512]{2,1,0:T(8,128)(2,1)S(1)}, bf16[1,512,512]{2,1,0:T(8,128)(2,1)S(1)}, u32[]{:S(2)}, u32[]{:S(2)}) %collective-permute-start.16) | collective-permute-done | bytes 524320 | tf_op jit(solution)/shard_map/ppermute | solution.py:75
  347.4 4.6 %fusion.3 = (f32[576]{0:T(1024)S(1)}, bf16[576,4096]{1,0:T(8,128)(2,1)S(1)}) fusion(bf16[576,4096]{1,0:T(8,128)(2,1)} %all-gather.5.cloned.1.call-done, f32[4096]{0:T(1024)S(1)} %bitcast.142), kind=kLoop, calls=%fused_computation.9 | loop fusion | flops 11795904 | bytes 9455872 | tf_op jit(solution)/shard_map/reduce_sum | solution.py:182
  352.0 3.0 fusion.15
  355.0 3.0 fusion.11
  358.0 3.1 fusion.13
  361.9 2.3 multiply_convert_fusion.1
  365.9 3.6 convolution_convert_fusion.1
  369.6 21.8 %all_to_all.40 = bf16[64,8,512]{2,0,1:T(8,128)(2,1)S(1)} all-to-all(bf16[64,8,512]{2,0,1:T(8,128)(2,1)S(1)} %bitcast.139), channel_id=1, replica_groups=mesh['shard'=4,'mp'=4,'segment'=2] {'mp','segment'}, dimensions={1} | all-to-all | bytes 1048576 | tf_op jit(solution)/shard_map/all_to_all | solution.py:193
  (142 shorter events, 59.5 us)
Async XLA Ops:
  7.2 4.7 %copy-start.12 = (s32[48,1]{0,1:T(1,128)S(1)}, s32[48,1]{0,1:T(1,128)}, u32[]{:S(2)}) copy-start(s32[48,1]{0,1:T(1,128)} %param.9) | copy-start | bytes 580
  7.2 6.0 %copy-start.11 = (s32[4,12]{1,0:T(4,128)S(1)}, s32[4,12]{1,0:T(4,128)}, u32[]{:S(2)}) copy-start(s32[4,12]{1,0:T(4,128)} %param.8) | copy-start | bytes 580
  7.2 6.5 %copy-start.9 = (s32[64,48]{0,1:T(8,128)S(1)}, s32[64,48]{0,1:T(8,128)}, u32[]{:S(2)}) copy-start(s32[64,48]{0,1:T(8,128)} %param.7) | copy-start | bytes 36868
  10.9 6.0 %collective-permute-start = (bf16[3,1024,512]{2,1,0:T(8,128)(2,1)}, bf16[3,1024,512]{2,1,0:T(8,128)(2,1)S(1)}, u32[]{:S(2)}, u32[]{:S(2)}) collective-permute-start(bf16[3,1024,512]{2,1,0:T(8,128)(2,1)} %dynamic-slice_bitcast_fusion), channel_id=1, source_target_pairs={{0,1},{1,0},{2,3},{3,2},{4,5},{5,4},{6,7},{7,6},{8,9},{9,8},{10,11... | collective-permute-start | bytes 9437192 | tf_op jit(solution)/shard_map/ppermute | solution.py:42
  14.6 20.4 %copy-start.10 = (s32[1,64]{1,0:T(1,128)S(1)}, s32[1,64]{1,0:T(1,128)}, u32[]{:S(2)}) copy-start(s32[1,64]{1,0:T(1,128)} %param.10) | copy-start | bytes 772
  23.3 9.8 %all-to-all-start = ((s32[4,1,144]{2,1,0:T(1,128)}), s32[4,1,144]{2,1,0:T(1,128)S(1)}, u32[]{:S(2)}, u32[]{:S(2)}) async-start(s32[4,1,144]{2,1,0:T(1,128)} %reshape.357), calls=%async_computation | async-start | bytes 8192 | tf_op jit(solution)/shard_map/all_to_all | solution.py:124
  28.3 96.2 %all-gather.3.cloned.1.call-start = ((), (), s32[]{:S(2)}) async-start(), calls=%async_computation.5 | async-start | bytes 5898240 | tf_op jit(solution)/shard_map/all_gather | solution.py:136
  46.5 5.9 %copy-start.8 = (f32[3,4096]{1,0:T(4,128)S(1)}, f32[3,4096]{1,0:T(4,128)}, u32[]{:S(2)}) copy-start(f32[3,4096]{1,0:T(4,128)} %param.12) | copy-start | bytes 147460
  48.7 217.2 %reduce-scatter.2.cloned.1.call-start = ((), (), s32[]{:S(2)}) async-start(), calls=%async_computation.6 | async-start | bytes 5308416 | tf_op jit(solution)/shard_map/reduce_scatter | solution.py:161
  48.9 69.1 %collective-permute-start.2 = (bf16[3,1024,512]{2,1,0:T(8,128)(2,1)}, bf16[3,1024,512]{2,1,0:T(8,128)(2,1)}, u32[]{:S(2)}, u32[]{:S(2)}) collective-permute-start(bf16[3,1024,512]{2,1,0:T(8,128)(2,1)} %get-tuple-element.30), channel_id=1, source_target_pairs={{0,16},{8,24},{16,0},{24,8},{1,17},{9,25},{17,1},{25,9},{2,18},{10... | collective-permute-start | bytes 9437192 | tf_op jit(solution)/shard_map/ppermute | solution.py:66
  49.6 71.8 %collective-permute-start.1 = (bf16[3,1024,512]{2,1,0:T(8,128)(2,1)}, bf16[3,1024,512]{2,1,0:T(8,128)(2,1)}, u32[]{:S(2)}, u32[]{:S(2)}) collective-permute-start(bf16[3,1024,512]{2,1,0:T(8,128)(2,1)} %get-tuple-element.30), channel_id=1, source_target_pairs={{0,8},{8,0},{16,24},{24,16},{1,9},{9,1},{17,25},{25,17},{2,10},{10... | collective-permute-start | bytes 9437192 | tf_op jit(solution)/shard_map/ppermute | solution.py:65
  52.4 3.0 collective-permute-start.5
  120.8 37.6 %collective-permute-start.3 = (bf16[3,512,512]{2,1,0:T(8,128)(2,1)}, bf16[3,512,512]{2,1,0:T(8,128)(2,1)}, u32[]{:S(2)}, u32[]{:S(2)}) collective-permute-start(bf16[3,512,512]{2,1,0:T(8,128)(2,1)} %slice.104), channel_id=1, source_target_pairs={{0,8},{8,0},{16,24},{24,16},{1,9},{9,1},{17,25},{25,17},{2,10},{10... | collective-permute-start | bytes 4718600 | tf_op jit(solution)/shard_map/ppermute | solution.py:75
  124.0 37.6 %collective-permute-start.4 = (bf16[3,512,512]{2,1,0:T(8,128)(2,1)}, bf16[3,512,512]{2,1,0:T(8,128)(2,1)}, u32[]{:S(2)}, u32[]{:S(2)}) collective-permute-start(bf16[3,512,512]{2,1,0:T(8,128)(2,1)} %slice.105), channel_id=1, source_target_pairs={{0,16},{8,24},{16,0},{24,8},{1,17},{9,25},{17,1},{25,9},{2,18},{10... | collective-permute-start | bytes 4718600 | tf_op jit(solution)/shard_map/ppermute | solution.py:76
  128.5 4.0 copy-start
  136.3 11.2 %slice-start = ((s8[5242880]{0:T(1024)(128)(4,1)}), s8[4194304]{0:T(1024)(128)(4,1)S(1)}, s32[]{:S(2)}) async-start(s8[5242880]{0:T(1024)(128)(4,1)} %bitcast.132), calls=%async_computation.8 | async-start | bytes 8388608
  140.4 7.1 %slice-start.1 = ((s8[5242880]{0:T(1024)(128)(4,1)}), s8[1048576]{0:T(1024)(128)(4,1)S(1)}, s32[]{:S(2)}) async-start(s8[5242880]{0:T(1024)(128)(4,1)} %bitcast.132), calls=%async_computation.9 | async-start | bytes 2097152
  144.5 36.1 %collective-permute-start.7 = (bf16[1,1024,512]{2,1,0:T(8,128)(2,1)}, bf16[1,1024,512]{2,1,0:T(8,128)(2,1)}, u32[]{:S(2)}, u32[]{:S(2)}) collective-permute-start(bf16[1,1024,512]{2,1,0:T(8,128)(2,1)} %get-tuple-element.15), channel_id=1, source_target_pairs={{0,16},{8,24},{16,0},{24,8},{1,17},{9,25},{17,1},{25,9},{2,18},{10... | collective-permute-start | bytes 3145736 | tf_op jit(solution)/shard_map/ppermute | solution.py:66
  146.0 37.9 %collective-permute-start.6 = (bf16[1,1024,512]{2,1,0:T(8,128)(2,1)}, bf16[1,1024,512]{2,1,0:T(8,128)(2,1)}, u32[]{:S(2)}, u32[]{:S(2)}) collective-permute-start(bf16[1,1024,512]{2,1,0:T(8,128)(2,1)} %get-tuple-element.15), channel_id=1, source_target_pairs={{0,8},{8,0},{16,24},{24,16},{1,9},{9,1},{17,25},{25,17},{2,10},{10... | collective-permute-start | bytes 3145736 | tf_op jit(solution)/shard_map/ppermute | solution.py:65
  170.6 1.8 copy-start.1
  170.6 1.9 copy-start.2
  172.6 2.9 copy-start.4
  182.5 17.6 %collective-permute-start.8 = (bf16[1,512,512]{2,1,0:T(8,128)(2,1)}, bf16[1,512,512]{2,1,0:T(8,128)(2,1)}, u32[]{:S(2)}, u32[]{:S(2)}) collective-permute-start(bf16[1,512,512]{2,1,0:T(8,128)(2,1)} %slice.109), channel_id=1, source_target_pairs={{0,8},{8,0},{16,24},{24,16},{1,9},{9,1},{17,25},{25,17},{2,10},{10... | collective-permute-start | bytes 1572872 | tf_op jit(solution)/shard_map/ppermute | solution.py:75
  185.8 16.2 %collective-permute-start.9 = (bf16[1,512,512]{2,1,0:T(8,128)(2,1)}, bf16[1,512,512]{2,1,0:T(8,128)(2,1)}, u32[]{:S(2)}, u32[]{:S(2)}) collective-permute-start(bf16[1,512,512]{2,1,0:T(8,128)(2,1)} %slice.110), channel_id=1, source_target_pairs={{0,16},{8,24},{16,0},{24,8},{1,17},{9,25},{17,1},{25,9},{2,18},{10... | collective-permute-start | bytes 1572872 | tf_op jit(solution)/shard_map/ppermute | solution.py:76
  195.5 8.4 %copy-start.7 = (bf16[576,512]{1,0:T(8,128)(2,1)S(1)}, bf16[576,512]{1,0:T(8,128)(2,1)}, u32[]{:S(2)}) copy-start(bf16[576,512]{1,0:T(8,128)(2,1)} %reshape.306) | copy-start | bytes 1769476
  210.5 136.9 %all-gather.5.cloned.1.call-start = ((), (), s32[]{:S(2)}) async-start(), calls=%async_computation.7 | async-start | bytes 5308416 | tf_op jit(solution)/shard_map/all_gather | solution.py:176
  213.6 53.5 %collective-permute-start.11 = (bf16[2,1024,512]{2,1,0:T(8,128)(2,1)}, bf16[2,1024,512]{2,1,0:T(8,128)(2,1)}, u32[]{:S(2)}, u32[]{:S(2)}) collective-permute-start(bf16[2,1024,512]{2,1,0:T(8,128)(2,1)} %slice_select_fusion), channel_id=1, source_target_pairs={{0,16},{8,24},{16,0},{24,8},{1,17},{9,25},{17,1},{25,9},{2,18},{10... | collective-permute-start | bytes 6291464 | tf_op jit(solution)/shard_map/ppermute | solution.py:66
  215.1 52.0 %collective-permute-start.10 = (bf16[2,1024,512]{2,1,0:T(8,128)(2,1)}, bf16[2,1024,512]{2,1,0:T(8,128)(2,1)}, u32[]{:S(2)}, u32[]{:S(2)}) collective-permute-start(bf16[2,1024,512]{2,1,0:T(8,128)(2,1)} %slice_select_fusion), channel_id=1, source_target_pairs={{0,8},{8,0},{16,24},{24,16},{1,9},{9,1},{17,25},{25,17},{2,10},{10... | collective-permute-start | bytes 6291464 | tf_op jit(solution)/shard_map/ppermute | solution.py:65
  271.3 12.7 %all-to-all-start.1 = ((bf16[64,4,1024]{2,0,1:T(8,128)(2,1)}), bf16[64,4,1024]{2,0,1:T(8,128)(2,1)}, u32[]{:S(2)}, u32[]{:S(2)}) async-start(bf16[64,4,1024]{2,0,1:T(8,128)(2,1)} %bitcast.138), calls=%async_computation.2 | async-start | bytes 1048576 | tf_op jit(solution)/shard_map/all_to_all | solution.py:164
  275.5 2.2 copy-start.3
  280.7 34.7 %collective-permute-start.15 = (bf16[1,1024,512]{2,1,0:T(8,128)(2,1)}, bf16[1,1024,512]{2,1,0:T(8,128)(2,1)}, u32[]{:S(2)}, u32[]{:S(2)}) collective-permute-start(bf16[1,1024,512]{2,1,0:T(8,128)(2,1)} %get-tuple-element.27), channel_id=1, source_target_pairs={{0,16},{8,24},{16,0},{24,8},{1,17},{9,25},{17,1},{25,9},{2,18},{10... | collective-permute-start | bytes 3145736 | tf_op jit(solution)/shard_map/ppermute | solution.py:66
  282.6 35.3 %collective-permute-start.14 = (bf16[1,1024,512]{2,1,0:T(8,128)(2,1)}, bf16[1,1024,512]{2,1,0:T(8,128)(2,1)}, u32[]{:S(2)}, u32[]{:S(2)}) collective-permute-start(bf16[1,1024,512]{2,1,0:T(8,128)(2,1)} %get-tuple-element.27), channel_id=1, source_target_pairs={{0,8},{8,0},{16,24},{24,16},{1,9},{9,1},{17,25},{25,17},{2,10},{10... | collective-permute-start | bytes 3145736 | tf_op jit(solution)/shard_map/ppermute | solution.py:65
  286.7 23.4 %all-to-all-start.2 = ((f32[4,64,512]{2,1,0:T(8,128)}), f32[4,64,512]{2,1,0:T(8,128)S(1)}, u32[]{:S(2)}, u32[]{:S(2)}) async-start(f32[4,64,512]{2,1,0:T(8,128)} %fusion.38), calls=%async_computation.3 | async-start | bytes 1048576 | tf_op jit(solution)/shard_map/all_to_all | solution.py:170
  311.7 35.6 %collective-permute-start.12 = (bf16[2,512,512]{2,1,0:T(8,128)(2,1)S(1)}, bf16[2,512,512]{2,1,0:T(8,128)(2,1)S(1)}, u32[]{:S(2)}, u32[]{:S(2)}) collective-permute-start(bf16[2,512,512]{2,1,0:T(8,128)(2,1)S(1)} %slice.114), channel_id=1, source_target_pairs={{0,8},{8,0},{16,24},{24,16},{1,9},{9,1},{17,25},{25,17},{2,10},{10... | collective-permute-start | bytes 3145736 | tf_op jit(solution)/shard_map/ppermute | solution.py:75
  314.5 32.8 %collective-permute-start.13 = (bf16[2,512,512]{2,1,0:T(8,128)(2,1)S(1)}, bf16[2,512,512]{2,1,0:T(8,128)(2,1)}, u32[]{:S(2)}, u32[]{:S(2)}) collective-permute-start(bf16[2,512,512]{2,1,0:T(8,128)(2,1)S(1)} %slice.115), channel_id=1, source_target_pairs={{0,16},{8,24},{16,0},{24,8},{1,17},{9,25},{17,1},{25,9},{2,18},{10... | collective-permute-start | bytes 3145736 | tf_op jit(solution)/shard_map/ppermute | solution.py:76
  316.4 28.0 %collective-permute-start.16 = (bf16[1,512,512]{2,1,0:T(8,128)(2,1)S(1)}, bf16[1,512,512]{2,1,0:T(8,128)(2,1)S(1)}, u32[]{:S(2)}, u32[]{:S(2)}) collective-permute-start(bf16[1,512,512]{2,1,0:T(8,128)(2,1)S(1)} %slice.121), channel_id=1, source_target_pairs={{0,8},{8,0},{16,24},{24,16},{1,9},{9,1},{17,25},{25,17},{2,10},{10... | collective-permute-start | bytes 1572872 | tf_op jit(solution)/shard_map/ppermute | solution.py:75
  319.0 27.5 %collective-permute-start.17 = (bf16[1,512,512]{2,1,0:T(8,128)(2,1)S(1)}, bf16[1,512,512]{2,1,0:T(8,128)(2,1)S(1)}, u32[]{:S(2)}, u32[]{:S(2)}) collective-permute-start(bf16[1,512,512]{2,1,0:T(8,128)(2,1)S(1)} %slice.122), channel_id=1, source_target_pairs={{0,16},{8,24},{16,0},{24,8},{1,17},{9,25},{17,1},{25,9},{2,18},{10... | collective-permute-start | bytes 1572872 | tf_op jit(solution)/shard_map/ppermute | solution.py:76
  347.3 4.7 %copy-start.5 = (bf16[2,512,512]{2,1,0:T(8,128)(2,1)}, bf16[2,512,512]{2,1,0:T(8,128)(2,1)S(1)}, u32[]{:S(2)}) copy-start(bf16[2,512,512]{2,1,0:T(8,128)(2,1)S(1)} %collective-permute-done.12) | copy-start | bytes 3145732
  358.0 3.1 copy-start.6
Sparse Core Ops, SparseCore 0:
  48.8 55.3 all-gather.2
  210.6 55.2 reduce-scatter.1
  269.3 50.0 all-gather.4

commit v3 on v2

--- a/solution.py
+++ b/solution.py
@@ -120,7 +120,6 @@
     send_ids = jnp.take(store_tokens, local_rows.reshape(-1), axis=0).reshape(
         shard_count, slot_cap, length
     )
-    send_ids = after(send_ids, enc_qkv)
     arrived = lax.all_to_all(send_ids, "shard", split_axis=0, concat_axis=0, tiled=True)
     mine_owner = lax.dynamic_index_in_dim(owners, my_shard, 0, keepdims=False)
     mine_rank = lax.dynamic_index_in_dim(slot_rank, my_shard, 0, keepdims=False)
@@ -131,7 +130,7 @@
     head_block = enc_qkv.shape[2]
     head_count = head_block // DH
     pass_rows = passage_ids.shape[0]
-    all_ids = jnp.concatenate([passage_ids, targets.reshape(-1)])
+    all_ids = after(jnp.concatenate([passage_ids, targets.reshape(-1)]), enc_qkv)
     embedded_part = jnp.take(vocab_table, all_ids, axis=0)
     piece = lax.all_gather(embedded_part, ("mp", "segment"), axis=1, tiled=True)
     passage_part = embedded_part[:pass_rows]
@@ -175,11 +174,11 @@
 
     whole_encoded = lax.all_gather(encoded, ("mp", "segment"), axis=1, tiled=True)
     cross_far = far(cross_near)
-    late_near = near(dec_out(*blocks(cross_near)))
+    late_near = near(dec_out(*blocks(cross_far)))
     whole_encoded = after(whole_encoded, *blocks(cross_far), *blocks(late_near))
-    late_far = far(late_near)
     enc_f32 = whole_encoded.astype(jnp.float32)
     enc_scale = lax.rsqrt(jnp.sum(enc_f32 * enc_f32, axis=1) / D + epsilon)
+    late_far = far([(o, f, after(b, enc_scale)) for o, f, b in late_near])
     enc_normed = (enc_f32 * norm_gains[2]).astype(jnp.bfloat16)
     cross_accum = project(enc_normed, cross_near + cross_far, shard_rows)
     key_values = (cross_accum * enc_scale[:, None, None]).astype(jnp.bfloat16)

time: 401 us -> 401 us (level)
  waiting for transfers between devices: 177 us -> 169 us
  local copies, waits for them, and re-layouts: 71 us -> 76.6 us
    ppermute x4, waiting for transfers between devices: 30.2 us -> 24.2 us  [far(): top = lax.ppermute(pieces[2][2][:, :rows // 2], 'shard', X_PAIRS)]
  transfers between devices with their start and end apart: 24 -> 24, of which waited for: 11 -> 10; matrix products, arithmetic and copies ran while one was open for 23% -> 27% of each run, Pallas kernels for 0% -> 0%
where the time goes in v3:
time: 401 us; the launch traced here: 399 us
  waiting for transfers between devices  169 us (42%)
  local copies, waits for them, and re-layouts  76.6 us (19%)
  matrix products  47.6 us (12%)
  other arithmetic  38 us (9%)
  starting transfers between devices  30 us (7%)
  blocking collectives  24 us (6%)
  between operations  14.2 us (4%)
    ppermute x4, waiting for transfers between devices, near(): lax.ppermute(block, 'shard', Y_PAIRS)  65.5 us
    reduce_scatter x1, waiting for transfers between devices, body(): lax.psum_scatter(enc_partial, ('mp', 'segment'), scatter_dimension=1, til...  50.2 us
    dot_general x10, matrix products, project(): jnp.einsum('rn,knh->rkh', part, block, preferred_element_type=jnp.float32)  30.4 us
    ppermute x4, waiting for transfers between devices, far(): top = lax.ppermute(pieces[2][2][:, :rows // 2], 'shard', X_PAIRS)  24.2 us
    all_to_all x1, blocking collectives, body(): lax.all_to_all(dec_partial, ('mp', 'segment'), split_axis=1, concat_axis=...  24 us
    dynamic_update_slice x9, local copies, waits for them, and re-layouts, in_order(): lax.dynamic_update_slice_in_dim(whole, block[0], owner * shard_rows + fir...  18.2 us
    all_to_all x1, waiting for transfers between devices, body(): lax.all_to_all(query_terms, 'shard', split_axis=0, concat_axis=0, tiled=T...  15.8 us
    gather x1, local copies, waits for them, and re-layouts, body(): embedded_part = jnp.take(vocab_table, all_ids, axis=0)  11.2 us
  transfers between devices with their start and end apart: 24, of which 10 were waited for; matrix products, arithmetic and copies ran while one was open for 27% of the time, Pallas kernels for 0%

profile of v3, /device:TPU:0, one launch (start us, length us, event | category | flops | bytes accessed | tf_op | source)
XLA Modules:
  0.0 399.1 jit_solution(18313715478135112084)
XLA Ops:
  7.2 3.8 dynamic-slice_bitcast_fusion
  15.1 4.7 %all-to-all-start = ((s32[4,1,144]{2,1,0:T(1,128)}), s32[4,1,144]{2,1,0:T(1,128)S(1)}, u32[]{:S(2)}, u32[]{:S(2)}) async-start(s32[4,1,144]{2,1,0:T(1,128)} %reshape.263), calls=%async_computation | async-start | bytes 8192 | tf_op jit(solution)/shard_map/all_to_all | solution.py:123
  20.1 4.4 %all-to-all-done = s32[4,1,144]{2,1,0:T(1,128)S(1)} async-done(((s32[4,1,144]{2,1,0:T(1,128)}), s32[4,1,144]{2,1,0:T(1,128)S(1)}, u32[]{:S(2)}, u32[]{:S(2)}) %all-to-all-start) | async-done | bytes 2336 | tf_op jit(solution)/shard_map/all_to_all | solution.py:123
  26.6 5.7 %broadcast_select_fusion = (bf16[3,1024,512]{2,1,0:T(8,128)(2,1)}, bf16[3,1024,512]{2,1,0:T(8,128)(2,1)}) fusion(bf16[3,1024,512]{2,1,0:T(8,128)(2,1)S(1)} %collective-permute-done, pred[]{:T(512)S(6)} %eq.52, bf16[1,4,1024,1024]{3,2,1,0:T(8,128)(2,1)} %param.13, s32[]{:T(128)S(6)} %select_n.144), kind=kLoop, calls=%fused_computation.18 | loop fusion | flops 1572864 | bytes 12582917 | tf_op jit(solution)/shard_map/jit(_where)/select_n | solution.py:43
  32.3 11.2 %gather_fusion.2 = bf16[640,512]{1,0:T(8,128)(2,1)} fusion(bf16[16384,512]{1,0:T(8,128)(2,1)} %param.11, s32[1024]{0:T(1024)S(1)} %pad_clamp_fusion), kind=kCustom, calls=%fused_computation.2 | custom fusion | bytes 1313280 | tf_op jit(solution)/shard_map/jit(_take)/gather | solution.py:134
  47.2 2.3 dynamic-slice_bitcast_fusion.2
  49.5 3.0 collective-permute-done.5
  52.5 3.0 broadcast_select_fusion.2
  55.5 60.0 %collective-permute-done.2 = bf16[3,1024,512]{2,1,0:T(8,128)(2,1)} collective-permute-done((bf16[3,1024,512]{2,1,0:T(8,128)(2,1)}, bf16[3,1024,512]{2,1,0:T(8,128)(2,1)}, u32[]{:S(2)}, u32[]{:S(2)}) %collective-permute-start.2) | collective-permute-done | bytes 3145760 | tf_op jit(solution)/shard_map/ppermute | solution.py:66
  115.4 2.7 slice.104
  118.8 2.7 slice.105
  122.3 3.9 convert_element_type.74
  127.4 2.8 copy-done
  130.2 3.9 fusion.23
  134.1 4.0 %fusion.21 = f32[576,3,512]{2,0,1:T(8,128)S(1)} fusion(bf16[3,1024,512]{2,1,0:T(8,128)(2,1)} %collective-permute-done.1, bf16[576,4096]{1,0:T(8,128)(2,1)S(1)} %fusion.4, s32[]{:T(128)S(6)} %select_n.150), kind=kOutput, calls=%fused_computation.39 | convolution fusion | flops 1811939328 | bytes 7864324 | tf_op jit(solution)/shard_map/rn,knh->rkh/dot_general | solution.py:88
  138.1 4.1 %add_add_fusion = f32[576,3,512]{2,0,1:T(8,128)S(1)} fusion(f32[576,3,512]{2,0,1:T(8,128)S(1)} %fusion.23, f32[576,3,512]{2,0,1:T(8,128)S(1)} %fusion.21, bf16[3,1024,512]{2,1,0:T(8,128)(2,1)} %collective-permute-done.2, bf16[576,4096]{1,0:T(8,128)(2,1)S(1)} %fusion.4, s32[]{:T(128)S(6)} %select_n.151), kind=kOutput, calls=%fused_computation.15 | convolution fusion | flops 1813708800 | bytes 14942212 | tf_op jit(solution)/shard_map/rn,knh->rkh/dot_general | solution.py:88
  146.0 9.8 %collective-permute-done.3 = bf16[3,512,512]{2,1,0:T(8,128)(2,1)} collective-permute-done((bf16[3,512,512]{2,1,0:T(8,128)(2,1)}, bf16[3,512,512]{2,1,0:T(8,128)(2,1)}, u32[]{:S(2)}, u32[]{:S(2)}) %collective-permute-start.3) | collective-permute-done | bytes 1572896 | tf_op jit(solution)/shard_map/ppermute | solution.py:75
  155.8 2.5 fusion.53
  159.1 2.7 multiply_convert_fusion
  163.1 2.5 reshape_squeeze.7
  165.5 2.5 reshape_squeeze.6
  172.8 5.5 %collective-permute-done.7 = bf16[1,1024,512]{2,1,0:T(8,128)(2,1)} collective-permute-done((bf16[1,1024,512]{2,1,0:T(8,128)(2,1)}, bf16[1,1024,512]{2,1,0:T(8,128)(2,1)}, u32[]{:S(2)}, u32[]{:S(2)}) %collective-permute-start.7) | collective-permute-done | bytes 1048608 | tf_op jit(solution)/shard_map/ppermute | solution.py:66
  184.2 2.5 reshape.211
  186.6 2.6 fusion.10
  190.6 2.7 reshape.212
  193.2 2.3 bitcast_dynamic-update-slice_fusion.4
  195.6 2.3 bitcast_dynamic-update-slice_fusion.3
  201.6 6.6 %convolution_convert_fusion = bf16[576,4096]{1,0:T(8,128)(2,1)} fusion(bf16[576,512]{1,0:T(8,128)(2,1)S(1)} %copy-done.5, bf16[4096,512]{1,0:T(8,128)(2,1)} %bitcast_dynamic-update-slice_fusion.8), kind=kOutput, calls=%fused_computation.12 | convolution fusion | flops 2418278400 | bytes 9502720 | tf_op jit(solution)/shard_map/dot_general | solution.py:154
  208.3 3.1 slice_select_fusion
  213.5 50.2 %reduce-scatter.2.cloned.1.call-done = bf16[576,512]{1,0:T(8,128)(2,1)} async-done(((bf16[576,4096]{1,0:T(8,128)(2,1)}), bf16[576,512]{1,0:T(8,128)(2,1)}) %reduce-scatter.2.cloned.1.call-update) | async-done | bytes 589840 | tf_op jit(solution)/shard_map/reduce_scatter | solution.py:160
  267.0 2.3 slice.114
  270.8 2.3 slice.115
  276.6 4.1 %all-to-all-start.1 = ((bf16[64,4,1024]{2,0,1:T(8,128)(2,1)}), bf16[64,4,1024]{2,0,1:T(8,128)(2,1)}, u32[]{:S(2)}, u32[]{:S(2)}) async-start(bf16[64,4,1024]{2,0,1:T(8,128)(2,1)} %bitcast.137), calls=%async_computation.2 | async-start | bytes 1048576 | tf_op jit(solution)/shard_map/all_to_all | solution.py:163
  280.8 14.4 %collective-permute-done.12 = bf16[2,512,512]{2,1,0:T(8,128)(2,1)} collective-permute-done((bf16[2,512,512]{2,1,0:T(8,128)(2,1)}, bf16[2,512,512]{2,1,0:T(8,128)(2,1)}, u32[]{:S(2)}, u32[]{:S(2)}) %collective-permute-start.12) | collective-permute-done | bytes 1048608 | tf_op jit(solution)/shard_map/ppermute | solution.py:75
  295.2 4.8 %collective-permute-done.13 = bf16[2,512,512]{2,1,0:T(8,128)(2,1)} collective-permute-done((bf16[2,512,512]{2,1,0:T(8,128)(2,1)}, bf16[2,512,512]{2,1,0:T(8,128)(2,1)}, u32[]{:S(2)}, u32[]{:S(2)}) %collective-permute-start.13) | collective-permute-done | bytes 1048608 | tf_op jit(solution)/shard_map/ppermute | solution.py:76
  302.3 2.9 bitcast_dynamic-update-slice_fusion.2
  307.2 2.6 fusion.38
  309.8 3.7 all-to-all-start.2
  313.6 15.8 %all-to-all-done.2 = f32[4,64,512]{2,1,0:T(8,128)S(1)} async-done(((f32[4,64,512]{2,1,0:T(8,128)}), f32[4,64,512]{2,1,0:T(8,128)S(1)}, u32[]{:S(2)}, u32[]{:S(2)}) %all-to-all-start.2) | async-done | bytes 524320 | tf_op jit(solution)/shard_map/all_to_all | solution.py:169
  329.7 2.3 bitcast_dynamic-update-slice_fusion.1
  332.0 2.3 bitcast_dynamic-update-slice_fusion
  334.3 4.3 %fusion.3 = (f32[576]{0:T(1024)S(1)}, bf16[576,4096]{1,0:T(8,128)(2,1)S(1)}) fusion(bf16[576,4096]{1,0:T(8,128)(2,1)} %all-gather.5.cloned.1.call-done, f32[4096]{0:T(1024)S(1)} %bitcast.141), kind=kLoop, calls=%fused_computation.9 | loop fusion | flops 11795904 | bytes 9455872 | tf_op jit(solution)/shard_map/reduce_sum | solution.py:180
  342.3 3.0 fusion.15
  347.6 3.0 fusion.11
  350.6 3.0 fusion.13
  355.6 2.3 multiply_convert_fusion.1
  363.4 3.6 convolution_convert_fusion.1
  367.0 24.0 %all_to_all.40 = bf16[64,8,512]{2,0,1:T(8,128)(2,1)S(1)} all-to-all(bf16[64,8,512]{2,0,1:T(8,128)(2,1)S(1)} %bitcast.138), channel_id=1, replica_groups=mesh['shard'=4,'mp'=4,'segment'=2] {'mp','segment'}, dimensions={1} | all-to-all | bytes 1048576 | tf_op jit(solution)/shard_map/all_to_all | solution.py:192
  (138 shorter events, 64.4 us)
Async XLA Ops:
  7.2 4.8 %copy-start.10 = (s32[48,1]{0,1:T(1,128)S(1)}, s32[48,1]{0,1:T(1,128)}, u32[]{:S(2)}) copy-start(s32[48,1]{0,1:T(1,128)} %param.9) | copy-start | bytes 580
  7.2 6.1 %copy-start.8 = (s32[4,12]{1,0:T(4,128)S(1)}, s32[4,12]{1,0:T(4,128)}, u32[]{:S(2)}) copy-start(s32[4,12]{1,0:T(4,128)} %param.8) | copy-start | bytes 580
  7.2 6.5 %copy-start.7 = (s32[64,48]{0,1:T(8,128)S(1)}, s32[64,48]{0,1:T(8,128)}, u32[]{:S(2)}) copy-start(s32[64,48]{0,1:T(8,128)} %param.7) | copy-start | bytes 36868
  7.2 19.3 %copy-start.9 = (s32[1,64]{1,0:T(1,128)S(1)}, s32[1,64]{1,0:T(1,128)}, u32[]{:S(2)}) copy-start(s32[1,64]{1,0:T(1,128)} %param.10) | copy-start | bytes 772
  11.0 15.6 %collective-permute-start = (bf16[3,1024,512]{2,1,0:T(8,128)(2,1)}, bf16[3,1024,512]{2,1,0:T(8,128)(2,1)S(1)}, u32[]{:S(2)}, u32[]{:S(2)}) collective-permute-start(bf16[3,1024,512]{2,1,0:T(8,128)(2,1)} %dynamic-slice_bitcast_fusion), channel_id=1, source_target_pairs={{0,1},{1,0},{2,3},{3,2},{4,5},{5,4},{6,7},{7,6},{8,9},{9,8},{10,11... | collective-permute-start | bytes 9437192 | tf_op jit(solution)/shard_map/ppermute | solution.py:42
  15.1 9.4 %all-to-all-start = ((s32[4,1,144]{2,1,0:T(1,128)}), s32[4,1,144]{2,1,0:T(1,128)S(1)}, u32[]{:S(2)}, u32[]{:S(2)}) async-start(s32[4,1,144]{2,1,0:T(1,128)} %reshape.263), calls=%async_computation | async-start | bytes 8192 | tf_op jit(solution)/shard_map/all_to_all | solution.py:123
  19.9 102.4 %all-gather.3.cloned.1.call-start = ((), (), s32[]{:S(2)}) async-start(), calls=%async_computation.5 | async-start | bytes 5898240 | tf_op jit(solution)/shard_map/all_gather | solution.py:135
  43.6 5.9 %copy-start.6 = (f32[3,4096]{1,0:T(4,128)S(1)}, f32[3,4096]{1,0:T(4,128)}, u32[]{:S(2)}) copy-start(f32[3,4096]{1,0:T(4,128)} %param.12) | copy-start | bytes 147460
  45.8 218.0 %reduce-scatter.2.cloned.1.call-start = ((), (), s32[]{:S(2)}) async-start(), calls=%async_computation.6 | async-start | bytes 5308416 | tf_op jit(solution)/shard_map/reduce_scatter | solution.py:160
  46.0 69.5 %collective-permute-start.2 = (bf16[3,1024,512]{2,1,0:T(8,128)(2,1)}, bf16[3,1024,512]{2,1,0:T(8,128)(2,1)}, u32[]{:S(2)}, u32[]{:S(2)}) collective-permute-start(bf16[3,1024,512]{2,1,0:T(8,128)(2,1)} %get-tuple-element.34), channel_id=1, source_target_pairs={{0,16},{8,24},{16,0},{24,8},{1,17},{9,25},{17,1},{25,9},{2,18},{10... | collective-permute-start | bytes 9437192 | tf_op jit(solution)/shard_map/ppermute | solution.py:66
  46.6 72.2 %collective-permute-start.1 = (bf16[3,1024,512]{2,1,0:T(8,128)(2,1)}, bf16[3,1024,512]{2,1,0:T(8,128)(2,1)}, u32[]{:S(2)}, u32[]{:S(2)}) collective-permute-start(bf16[3,1024,512]{2,1,0:T(8,128)(2,1)} %get-tuple-element.34), channel_id=1, source_target_pairs={{0,8},{8,0},{16,24},{24,16},{1,9},{9,1},{17,25},{25,17},{2,10},{10... | collective-permute-start | bytes 9437192 | tf_op jit(solution)/shard_map/ppermute | solution.py:65
  49.5 3.0 collective-permute-start.5
  118.2 37.6 %collective-permute-start.3 = (bf16[3,512,512]{2,1,0:T(8,128)(2,1)}, bf16[3,512,512]{2,1,0:T(8,128)(2,1)}, u32[]{:S(2)}, u32[]{:S(2)}) collective-permute-start(bf16[3,512,512]{2,1,0:T(8,128)(2,1)} %slice.104), channel_id=1, source_target_pairs={{0,8},{8,0},{16,24},{24,16},{1,9},{9,1},{17,25},{25,17},{2,10},{10... | collective-permute-start | bytes 4718600 | tf_op jit(solution)/shard_map/ppermute | solution.py:75
  121.4 37.6 %collective-permute-start.4 = (bf16[3,512,512]{2,1,0:T(8,128)(2,1)}, bf16[3,512,512]{2,1,0:T(8,128)(2,1)}, u32[]{:S(2)}, u32[]{:S(2)}) collective-permute-start(bf16[3,512,512]{2,1,0:T(8,128)(2,1)} %slice.105), channel_id=1, source_target_pairs={{0,16},{8,24},{16,0},{24,8},{1,17},{9,25},{17,1},{25,9},{2,18},{10... | collective-permute-start | bytes 4718600 | tf_op jit(solution)/shard_map/ppermute | solution.py:76
  126.2 4.0 copy-start
  134.0 10.9 %slice-start = ((s8[5242880]{0:T(1024)(128)(4,1)}), s8[4194304]{0:T(1024)(128)(4,1)S(1)}, s32[]{:S(2)}) async-start(s8[5242880]{0:T(1024)(128)(4,1)} %bitcast.131), calls=%async_computation.8 | async-start | bytes 8388608
  138.1 6.8 %slice-start.1 = ((s8[5242880]{0:T(1024)(128)(4,1)}), s8[1048576]{0:T(1024)(128)(4,1)S(1)}, s32[]{:S(2)}) async-start(s8[5242880]{0:T(1024)(128)(4,1)} %bitcast.131), calls=%async_computation.9 | async-start | bytes 2097152
  142.2 36.2 %collective-permute-start.7 = (bf16[1,1024,512]{2,1,0:T(8,128)(2,1)}, bf16[1,1024,512]{2,1,0:T(8,128)(2,1)}, u32[]{:S(2)}, u32[]{:S(2)}) collective-permute-start(bf16[1,1024,512]{2,1,0:T(8,128)(2,1)} %get-tuple-element.17), channel_id=1, source_target_pairs={{0,16},{8,24},{16,0},{24,8},{1,17},{9,25},{17,1},{25,9},{2,18},{10... | collective-permute-start | bytes 3145736 | tf_op jit(solution)/shard_map/ppermute | solution.py:66
  143.5 38.3 %collective-permute-start.6 = (bf16[1,1024,512]{2,1,0:T(8,128)(2,1)}, bf16[1,1024,512]{2,1,0:T(8,128)(2,1)}, u32[]{:S(2)}, u32[]{:S(2)}) collective-permute-start(bf16[1,1024,512]{2,1,0:T(8,128)(2,1)} %get-tuple-element.17), channel_id=1, source_target_pairs={{0,8},{8,0},{16,24},{24,16},{1,9},{9,1},{17,25},{25,17},{2,10},{10... | collective-permute-start | bytes 3145736 | tf_op jit(solution)/shard_map/ppermute | solution.py:65
  168.0 1.8 copy-start.1
  168.0 1.9 copy-start.2
  170.0 2.9 copy-start.4
  180.3 17.6 %collective-permute-start.8 = (bf16[1,512,512]{2,1,0:T(8,128)(2,1)}, bf16[1,512,512]{2,1,0:T(8,128)(2,1)}, u32[]{:S(2)}, u32[]{:S(2)}) collective-permute-start(bf16[1,512,512]{2,1,0:T(8,128)(2,1)} %slice.109), channel_id=1, source_target_pairs={{0,8},{8,0},{16,24},{24,16},{1,9},{9,1},{17,25},{25,17},{2,10},{10... | collective-permute-start | bytes 1572872 | tf_op jit(solution)/shard_map/ppermute | solution.py:75
  183.6 16.2 %collective-permute-start.9 = (bf16[1,512,512]{2,1,0:T(8,128)(2,1)}, bf16[1,512,512]{2,1,0:T(8,128)(2,1)}, u32[]{:S(2)}, u32[]{:S(2)}) collective-permute-start(bf16[1,512,512]{2,1,0:T(8,128)(2,1)} %slice.110), channel_id=1, source_target_pairs={{0,16},{8,24},{16,0},{24,8},{1,17},{9,25},{17,1},{25,9},{2,18},{10... | collective-permute-start | bytes 1572872 | tf_op jit(solution)/shard_map/ppermute | solution.py:76
  193.2 8.4 %copy-start.5 = (bf16[576,512]{1,0:T(8,128)(2,1)S(1)}, bf16[576,512]{1,0:T(8,128)(2,1)}, u32[]{:S(2)}) copy-start(bf16[576,512]{1,0:T(8,128)(2,1)} %reshape.212) | copy-start | bytes 1769476
  208.3 126.0 %all-gather.5.cloned.1.call-start = ((), (), s32[]{:S(2)}) async-start(), calls=%async_computation.7 | async-start | bytes 5308416 | tf_op jit(solution)/shard_map/all_gather | solution.py:175
  211.5 53.5 %collective-permute-start.11 = (bf16[2,1024,512]{2,1,0:T(8,128)(2,1)}, bf16[2,1024,512]{2,1,0:T(8,128)(2,1)}, u32[]{:S(2)}, u32[]{:S(2)}) collective-permute-start(bf16[2,1024,512]{2,1,0:T(8,128)(2,1)} %slice_select_fusion), channel_id=1, source_target_pairs={{0,16},{8,24},{16,0},{24,8},{1,17},{9,25},{17,1},{25,9},{2,18},{10... | collective-permute-start | bytes 6291464 | tf_op jit(solution)/shard_map/ppermute | solution.py:66
  212.9 52.0 %collective-permute-start.10 = (bf16[2,1024,512]{2,1,0:T(8,128)(2,1)}, bf16[2,1024,512]{2,1,0:T(8,128)(2,1)}, u32[]{:S(2)}, u32[]{:S(2)}) collective-permute-start(bf16[2,1024,512]{2,1,0:T(8,128)(2,1)} %slice_select_fusion), channel_id=1, source_target_pairs={{0,8},{8,0},{16,24},{24,16},{1,9},{9,1},{17,25},{25,17},{2,10},{10... | collective-permute-start | bytes 6291464 | tf_op jit(solution)/shard_map/ppermute | solution.py:65
  269.3 25.9 %collective-permute-start.12 = (bf16[2,512,512]{2,1,0:T(8,128)(2,1)}, bf16[2,512,512]{2,1,0:T(8,128)(2,1)}, u32[]{:S(2)}, u32[]{:S(2)}) collective-permute-start(bf16[2,512,512]{2,1,0:T(8,128)(2,1)} %slice.114), channel_id=1, source_target_pairs={{0,8},{8,0},{16,24},{24,16},{1,9},{9,1},{17,25},{25,17},{2,10},{10... | collective-permute-start | bytes 3145736 | tf_op jit(solution)/shard_map/ppermute | solution.py:75
  273.0 27.0 %collective-permute-start.13 = (bf16[2,512,512]{2,1,0:T(8,128)(2,1)}, bf16[2,512,512]{2,1,0:T(8,128)(2,1)}, u32[]{:S(2)}, u32[]{:S(2)}) collective-permute-start(bf16[2,512,512]{2,1,0:T(8,128)(2,1)} %slice.115), channel_id=1, source_target_pairs={{0,16},{8,24},{16,0},{24,8},{1,17},{9,25},{17,1},{25,9},{2,18},{10... | collective-permute-start | bytes 3145736 | tf_op jit(solution)/shard_map/ppermute | solution.py:76
  276.6 30.6 %all-to-all-start.1 = ((bf16[64,4,1024]{2,0,1:T(8,128)(2,1)}), bf16[64,4,1024]{2,0,1:T(8,128)(2,1)}, u32[]{:S(2)}, u32[]{:S(2)}) async-start(bf16[64,4,1024]{2,0,1:T(8,128)(2,1)} %bitcast.137), calls=%async_computation.2 | async-start | bytes 1048576 | tf_op jit(solution)/shard_map/all_to_all | solution.py:163
  280.8 21.5 %copy-start.3 = (bf16[1,1024,512]{2,1,0:T(8,128)(2,1)S(1)}, bf16[1,1024,512]{2,1,0:T(8,128)(2,1)}, u32[]{:S(2)}) copy-start(bf16[1,1024,512]{2,1,0:T(8,128)(2,1)} %get-tuple-element.23) | copy-start | bytes 3145732
  305.1 24.6 %collective-permute-start.14 = (bf16[1,1024,512]{2,1,0:T(8,128)(2,1)}, bf16[1,1024,512]{2,1,0:T(8,128)(2,1)}, u32[]{:S(2)}, u32[]{:S(2)}) collective-permute-start(bf16[1,1024,512]{2,1,0:T(8,128)(2,1)} %get-tuple-element.31), channel_id=1, source_target_pairs={{0,8},{8,0},{16,24},{24,16},{1,9},{9,1},{17,25},{25,17},{2,10},{10... | collective-permute-start | bytes 3145736 | tf_op jit(solution)/shard_map/ppermute | solution.py:65
  305.7 26.2 %collective-permute-start.15 = (bf16[1,1024,512]{2,1,0:T(8,128)(2,1)}, bf16[1,1024,512]{2,1,0:T(8,128)(2,1)}, u32[]{:S(2)}, u32[]{:S(2)}) collective-permute-start(bf16[1,1024,512]{2,1,0:T(8,128)(2,1)} %get-tuple-element.31), channel_id=1, source_target_pairs={{0,16},{8,24},{16,0},{24,8},{1,17},{9,25},{17,1},{25,9},{2,18},{10... | collective-permute-start | bytes 3145736 | tf_op jit(solution)/shard_map/ppermute | solution.py:66
  309.8 19.6 %all-to-all-start.2 = ((f32[4,64,512]{2,1,0:T(8,128)}), f32[4,64,512]{2,1,0:T(8,128)S(1)}, u32[]{:S(2)}, u32[]{:S(2)}) async-start(f32[4,64,512]{2,1,0:T(8,128)} %fusion.38), calls=%async_computation.3 | async-start | bytes 1048576 | tf_op jit(solution)/shard_map/all_to_all | solution.py:169
  345.3 14.4 %collective-permute-start.16 = (bf16[1,512,512]{2,1,0:T(8,128)(2,1)}, bf16[1,512,512]{2,1,0:T(8,128)(2,1)}, u32[]{:S(2)}, u32[]{:S(2)}) collective-permute-start(bf16[1,512,512]{2,1,0:T(8,128)(2,1)} %slice.94), channel_id=1, source_target_pairs={{0,8},{8,0},{16,24},{24,16},{1,9},{9,1},{17,25},{25,17},{2,10},{10... | collective-permute-start | bytes 1572872 | tf_op jit(solution)/shard_map/ppermute | solution.py:75
  346.2 15.4 %collective-permute-start.17 = (bf16[1,512,512]{2,1,0:T(8,128)(2,1)}, bf16[1,512,512]{2,1,0:T(8,128)(2,1)}, u32[]{:S(2)}, u32[]{:S(2)}) collective-permute-start(bf16[1,512,512]{2,1,0:T(8,128)(2,1)} %slice.95), channel_id=1, source_target_pairs={{0,16},{8,24},{16,0},{24,8},{1,17},{9,25},{17,1},{25,9},{2,18},{10... | collective-permute-start | bytes 1572872 | tf_op jit(solution)/shard_map/ppermute | solution.py:76
Sparse Core Ops, SparseCore 0:
  45.9 55.3 all-gather.2
  208.4 55.2 reduce-scatter.1
  267.2 50.0 all-gather.4

commit v4 on v3

--- a/solution.py
+++ b/solution.py
@@ -174,13 +174,13 @@
 
     whole_encoded = lax.all_gather(encoded, ("mp", "segment"), axis=1, tiled=True)
     cross_far = far(cross_near)
-    late_near = near(dec_out(*blocks(cross_far)))
-    whole_encoded = after(whole_encoded, *blocks(cross_far), *blocks(late_near))
+    late_near = near(dec_out(*blocks(cross_far), queries))
+    whole_encoded = after(whole_encoded, *blocks(cross_far))
     enc_f32 = whole_encoded.astype(jnp.float32)
     enc_scale = lax.rsqrt(jnp.sum(enc_f32 * enc_f32, axis=1) / D + epsilon)
-    late_far = far([(o, f, after(b, enc_scale)) for o, f, b in late_near])
     enc_normed = (enc_f32 * norm_gains[2]).astype(jnp.bfloat16)
     cross_accum = project(enc_normed, cross_near + cross_far, shard_rows)
+    late_far = far([(o, f, after(b, cross_accum)) for o, f, b in late_near])
     key_values = (cross_accum * enc_scale[:, None, None]).astype(jnp.bfloat16)
     dec_context = attend(queries, key_values[None, :, 0], key_values[None, :, 1], head_count)
     dec_partial = lax.dot_general(

time: 401 us -> 396 us (0.988)
  waiting for transfers between devices: 169 us -> 181 us
  local copies, waits for them, and re-layouts: 76.6 us -> 69.5 us
  blocking collectives: 24 us -> 17.8 us
    reduce_scatter x1, waiting for transfers between devices: 50.2 us -> 0.02 us  [body(): lax.psum_scatter(enc_partial, ('mp', 'segment'), scatter_dimension=1, til...]
    all_to_all x1, waiting for transfers between devices: 0.01 us -> 41.2 us  [body(): lax.all_to_all(after(targ_normed, enc_partial), 'shard', split_axis=1, co...]
    ppermute x4, waiting for transfers between devices: 0.01 us -> 16.5 us  [near(): lax.ppermute(block, 'shard', X_PAIRS)]
    ppermute x4, waiting for transfers between devices: 24.2 us -> 36.7 us  [far(): top = lax.ppermute(pieces[2][2][:, :rows // 2], 'shard', X_PAIRS)]
    all_to_all x1, waiting for transfers between devices: 15.8 us -> 6.16 us  [body(): lax.all_to_all(query_terms, 'shard', split_axis=0, concat_axis=0, tiled=T...]
    all_to_all x1, blocking collectives: 24 us -> 17.8 us  [body(): lax.all_to_all(dec_partial, ('mp', 'segment'), split_axis=1, concat_axis=...]
    all_gather x1, waiting for transfers between devices: 0.01 us -> 5.28 us  [body(): lax.all_gather(encoded, ('mp', 'segment'), axis=1, tiled=True)]
    dynamic_update_slice x9, local copies, waits for them, and re-layouts: 18.2 us -> 13.8 us  [in_order(): lax.dynamic_update_slice_in_dim(whole, block[0], owner * shard_rows + fir...]
  transfers between devices with their start and end apart: 24 -> 24, of which waited for: 10 -> 17; matrix products, arithmetic and copies ran while one was open for 27% -> 21% of each run, Pallas kernels for 0% -> 0%
where the time goes in v4:
time: 396 us; the launch traced here: 395 us
  waiting for transfers between devices  181 us (46%)
  local copies, waits for them, and re-layouts  69.5 us (18%)
  matrix products  46.3 us (12%)
  other arithmetic  36.1 us (9%)
  starting transfers between devices  30.1 us (8%)
  blocking collectives  17.8 us (4%)
  between operations  14.2 us (4%)
    ppermute x4, waiting for transfers between devices, near(): lax.ppermute(block, 'shard', Y_PAIRS)  62.9 us
    all_to_all x1, waiting for transfers between devices, body(): lax.all_to_all(after(targ_normed, enc_partial), 'shard', split_axis=1, co...  41.2 us
    ppermute x4, waiting for transfers between devices, far(): top = lax.ppermute(pieces[2][2][:, :rows // 2], 'shard', X_PAIRS)  36.7 us
    dot_general x10, matrix products, project(): jnp.einsum('rn,knh->rkh', part, block, preferred_element_type=jnp.float32)  28 us
    all_to_all x1, blocking collectives, body(): lax.all_to_all(dec_partial, ('mp', 'segment'), split_axis=1, concat_axis=...  17.8 us
    ppermute x4, waiting for transfers between devices, near(): lax.ppermute(block, 'shard', X_PAIRS)  16.5 us
    dynamic_update_slice x9, local copies, waits for them, and re-layouts, in_order(): lax.dynamic_update_slice_in_dim(whole, block[0], owner * shard_rows + fir...  13.8 us
    gather x1, local copies, waits for them, and re-layouts, body(): embedded_part = jnp.take(vocab_table, all_ids, axis=0)  11.2 us
  transfers between devices with their start and end apart: 24, of which 17 were waited for; matrix products, arithmetic and copies ran while one was open for 21% of the time, Pallas kernels for 0%

profile of v4, /device:TPU:0, one launch (start us, length us, event | category | flops | bytes accessed | tf_op | source)
XLA Modules:
  0.0 394.8 jit_solution(14517952175766466162)
XLA Ops:
  7.2 3.8 dynamic-slice_bitcast_fusion
  15.1 4.7 %all-to-all-start = ((s32[4,1,144]{2,1,0:T(1,128)}), s32[4,1,144]{2,1,0:T(1,128)S(1)}, u32[]{:S(2)}, u32[]{:S(2)}) async-start(s32[4,1,144]{2,1,0:T(1,128)} %reshape.289), calls=%async_computation | async-start | bytes 8192 | tf_op jit(solution)/shard_map/all_to_all | solution.py:123
  20.1 4.4 %all-to-all-done = s32[4,1,144]{2,1,0:T(1,128)S(1)} async-done(((s32[4,1,144]{2,1,0:T(1,128)}), s32[4,1,144]{2,1,0:T(1,128)S(1)}, u32[]{:S(2)}, u32[]{:S(2)}) %all-to-all-start) | async-done | bytes 2336 | tf_op jit(solution)/shard_map/all_to_all | solution.py:123
  26.6 5.7 %broadcast_select_fusion = (bf16[3,1024,512]{2,1,0:T(8,128)(2,1)}, bf16[3,1024,512]{2,1,0:T(8,128)(2,1)}) fusion(bf16[3,1024,512]{2,1,0:T(8,128)(2,1)S(1)} %collective-permute-done, pred[]{:T(512)S(6)} %eq.52, bf16[1,4,1024,1024]{3,2,1,0:T(8,128)(2,1)} %param.13, s32[]{:T(128)S(6)} %select_n.144), kind=kLoop, calls=%fused_computation.18 | loop fusion | flops 1572864 | bytes 12582917 | tf_op jit(solution)/shard_map/jit(_where)/select_n | solution.py:43
  32.3 11.2 %gather_fusion.2 = bf16[640,512]{1,0:T(8,128)(2,1)} fusion(bf16[16384,512]{1,0:T(8,128)(2,1)} %param.11, s32[1024]{0:T(1024)S(1)} %pad_clamp_fusion), kind=kCustom, calls=%fused_computation.2 | custom fusion | bytes 1313280 | tf_op jit(solution)/shard_map/jit(_take)/gather | solution.py:134
  47.1 2.3 dynamic-slice_bitcast_fusion.2
  49.5 3.0 collective-permute-done.5
  52.5 3.0 broadcast_select_fusion.2
  55.5 59.9 %collective-permute-done.2 = bf16[3,1024,512]{2,1,0:T(8,128)(2,1)} collective-permute-done((bf16[3,1024,512]{2,1,0:T(8,128)(2,1)}, bf16[3,1024,512]{2,1,0:T(8,128)(2,1)}, u32[]{:S(2)}, u32[]{:S(2)}) %collective-permute-start.2) | collective-permute-done | bytes 3145760 | tf_op jit(solution)/shard_map/ppermute | solution.py:66
  115.4 2.7 slice.104
  118.7 2.7 slice.105
  122.2 3.9 convert_element_type.83
  127.3 2.8 copy-done
  130.2 3.9 fusion.23
  134.1 4.0 %fusion.21 = f32[576,3,512]{2,0,1:T(8,128)S(1)} fusion(bf16[3,1024,512]{2,1,0:T(8,128)(2,1)} %collective-permute-done.1, bf16[576,4096]{1,0:T(8,128)(2,1)S(1)} %fusion.4, s32[]{:T(128)S(6)} %select_n.150), kind=kOutput, calls=%fused_computation.40 | convolution fusion | flops 1811939328 | bytes 7864324 | tf_op jit(solution)/shard_map/rn,knh->rkh/dot_general | solution.py:88
  138.1 4.1 %add_add_fusion = f32[576,3,512]{2,0,1:T(8,128)S(1)} fusion(f32[576,3,512]{2,0,1:T(8,128)S(1)} %fusion.23, f32[576,3,512]{2,0,1:T(8,128)S(1)} %fusion.21, bf16[3,1024,512]{2,1,0:T(8,128)(2,1)} %collective-permute-done.2, bf16[576,4096]{1,0:T(8,128)(2,1)S(1)} %fusion.4, s32[]{:T(128)S(6)} %select_n.151), kind=kOutput, calls=%fused_computation.15 | convolution fusion | flops 1813708800 | bytes 14942212 | tf_op jit(solution)/shard_map/rn,knh->rkh/dot_general | solution.py:88
  146.0 9.8 %collective-permute-done.3 = bf16[3,512,512]{2,1,0:T(8,128)(2,1)} collective-permute-done((bf16[3,512,512]{2,1,0:T(8,128)(2,1)}, bf16[3,512,512]{2,1,0:T(8,128)(2,1)}, u32[]{:S(2)}, u32[]{:S(2)}) %collective-permute-start.3) | collective-permute-done | bytes 1572896 | tf_op jit(solution)/shard_map/ppermute | solution.py:75
  155.8 2.5 fusion.53
  159.0 2.7 multiply_convert_fusion
  163.0 2.5 reshape_squeeze.7
  165.5 2.5 reshape_squeeze.6
  172.8 2.6 collective-permute-done.6
  175.4 3.0 collective-permute-done.7
  178.3 2.5 reshape.237
  180.8 2.6 fusion.10
  184.8 2.7 reshape.238
  191.7 2.3 bitcast_dynamic-update-slice_fusion.4
  194.0 2.3 bitcast_dynamic-update-slice_fusion.3
  196.3 3.0 collective-permute-done.8
  202.5 6.6 %convolution_convert_fusion = bf16[576,4096]{1,0:T(8,128)(2,1)} fusion(bf16[576,512]{1,0:T(8,128)(2,1)S(1)} %copy-done.13, bf16[4096,512]{1,0:T(8,128)(2,1)} %bitcast_dynamic-update-slice_fusion.8), kind=kOutput, calls=%fused_computation.12 | convolution fusion | flops 2418278400 | bytes 9502720 | tf_op jit(solution)/shard_map/dot_general | solution.py:154
  209.1 3.1 slice_select_fusion
  216.5 4.1 %all-to-all-start.1 = ((bf16[64,4,1024]{2,0,1:T(8,128)(2,1)}), bf16[64,4,1024]{2,0,1:T(8,128)(2,1)}, u32[]{:S(2)}, u32[]{:S(2)}) async-start(bf16[64,4,1024]{2,0,1:T(8,128)(2,1)} %bitcast.143), calls=%async_computation.2 | async-start | bytes 1048576 | tf_op jit(solution)/shard_map/all_to_all | solution.py:163
  220.6 41.2 %all-to-all-done.1 = bf16[64,4,1024]{2,0,1:T(8,128)(2,1)} async-done(((bf16[64,4,1024]{2,0,1:T(8,128)(2,1)}), bf16[64,4,1024]{2,0,1:T(8,128)(2,1)}, u32[]{:S(2)}, u32[]{:S(2)}) %all-to-all-start.1) | async-done | bytes 524320 | tf_op jit(solution)/shard_map/all_to_all | solution.py:163
  261.8 2.6 fusion.38
  264.5 3.6 all-to-all-start.2
  268.4 6.2 %all-to-all-done.2 = f32[4,64,512]{2,1,0:T(8,128)S(1)} async-done(((f32[4,64,512]{2,1,0:T(8,128)}), f32[4,64,512]{2,1,0:T(8,128)S(1)}, u32[]{:S(2)}, u32[]{:S(2)}) %all-to-all-start.2) | async-done | bytes 524320 | tf_op jit(solution)/shard_map/all_to_all | solution.py:169
  281.7 15.4 %collective-permute-done.12 = bf16[2,512,512]{2,1,0:T(8,128)(2,1)S(1)} collective-permute-done((bf16[2,512,512]{2,1,0:T(8,128)(2,1)S(1)}, bf16[2,512,512]{2,1,0:T(8,128)(2,1)S(1)}, u32[]{:S(2)}, u32[]{:S(2)}) %collective-permute-start.12) | collective-permute-done | bytes 1048608 | tf_op jit(solution)/shard_map/ppermute | solution.py:75
  300.3 2.3 broadcast.152
  302.6 2.9 bitcast_dynamic-update-slice_fusion.2
  307.8 14.0 %collective-permute-done.14 = bf16[1,1024,512]{2,1,0:T(8,128)(2,1)S(1)} collective-permute-done((bf16[1,1024,512]{2,1,0:T(8,128)(2,1)}, bf16[1,1024,512]{2,1,0:T(8,128)(2,1)S(1)}, u32[]{:S(2)}, u32[]{:S(2)}) %collective-permute-start.14) | collective-permute-done | bytes 1048608 | tf_op jit(solution)/shard_map/ppermute | solution.py:65
  324.0 5.3 %all-gather.5.cloned.1.call-done = bf16[576,4096]{1,0:T(8,128)(2,1)} async-done(((bf16[576,512]{1,0:T(8,128)(2,1)}), bf16[576,4096]{1,0:T(8,128)(2,1)}) %all-gather.5.cloned.1.call-update) | async-done | bytes 4718608 | tf_op jit(solution)/shard_map/all_gather | solution.py:175
  329.3 4.3 %fusion.3 = (f32[576]{0:T(1024)S(1)}, bf16[576,4096]{1,0:T(8,128)(2,1)S(1)}) fusion(bf16[576,4096]{1,0:T(8,128)(2,1)} %all-gather.5.cloned.1.call-done, f32[4096]{0:T(1024)S(1)} %bitcast.147), kind=kLoop, calls=%fused_computation.9 | loop fusion | flops 11795904 | bytes 9455872 | tf_op jit(solution)/shard_map/reduce_sum | solution.py:180
  333.6 3.1 fusion.15
  337.5 3.0 fusion.11
  340.5 3.1 fusion.13
  353.7 8.5 %collective-permute-done.16 = bf16[1,512,512]{2,1,0:T(8,128)(2,1)} collective-permute-done((bf16[1,512,512]{2,1,0:T(8,128)(2,1)}, bf16[1,512,512]{2,1,0:T(8,128)(2,1)}, u32[]{:S(2)}, u32[]{:S(2)}) %collective-permute-start.16) | collective-permute-done | bytes 524320 | tf_op jit(solution)/shard_map/ppermute | solution.py:75
  366.2 3.6 convolution_convert_fusion.1
  369.8 17.8 %all_to_all.40 = bf16[64,8,512]{2,0,1:T(8,128)(2,1)S(1)} all-to-all(bf16[64,8,512]{2,0,1:T(8,128)(2,1)S(1)} %bitcast.144), channel_id=1, replica_groups=mesh['shard'=4,'mp'=4,'segment'=2] {'mp','segment'}, dimensions={1} | all-to-all | bytes 1048576 | tf_op jit(solution)/shard_map/all_to_all | solution.py:192
  (154 shorter events, 67.1 us)
Async XLA Ops:
  7.2 4.2 %copy-start.15 = (s32[64,48]{0,1:T(8,128)S(1)}, s32[64,48]{0,1:T(8,128)}, u32[]{:S(2)}) copy-start(s32[64,48]{0,1:T(8,128)} %param.7) | copy-start | bytes 36868
  7.2 4.8 %copy-start.18 = (s32[48,1]{0,1:T(1,128)S(1)}, s32[48,1]{0,1:T(1,128)}, u32[]{:S(2)}) copy-start(s32[48,1]{0,1:T(1,128)} %param.9) | copy-start | bytes 580
  7.2 6.1 %copy-start.16 = (s32[4,12]{1,0:T(4,128)S(1)}, s32[4,12]{1,0:T(4,128)}, u32[]{:S(2)}) copy-start(s32[4,12]{1,0:T(4,128)} %param.8) | copy-start | bytes 580
  7.2 19.3 %copy-start.17 = (s32[1,64]{1,0:T(1,128)S(1)}, s32[1,64]{1,0:T(1,128)}, u32[]{:S(2)}) copy-start(s32[1,64]{1,0:T(1,128)} %param.10) | copy-start | bytes 772
  11.0 15.6 %collective-permute-start = (bf16[3,1024,512]{2,1,0:T(8,128)(2,1)}, bf16[3,1024,512]{2,1,0:T(8,128)(2,1)S(1)}, u32[]{:S(2)}, u32[]{:S(2)}) collective-permute-start(bf16[3,1024,512]{2,1,0:T(8,128)(2,1)} %dynamic-slice_bitcast_fusion), channel_id=1, source_target_pairs={{0,1},{1,0},{2,3},{3,2},{4,5},{5,4},{6,7},{7,6},{8,9},{9,8},{10,11... | collective-permute-start | bytes 9437192 | tf_op jit(solution)/shard_map/ppermute | solution.py:42
  15.1 9.4 %all-to-all-start = ((s32[4,1,144]{2,1,0:T(1,128)}), s32[4,1,144]{2,1,0:T(1,128)S(1)}, u32[]{:S(2)}, u32[]{:S(2)}) async-start(s32[4,1,144]{2,1,0:T(1,128)} %reshape.289), calls=%async_computation | async-start | bytes 8192 | tf_op jit(solution)/shard_map/all_to_all | solution.py:123
  19.9 102.4 %all-gather.3.cloned.1.call-start = ((), (), s32[]{:S(2)}) async-start(), calls=%async_computation.5 | async-start | bytes 5898240 | tf_op jit(solution)/shard_map/all_gather | solution.py:135
  43.6 5.9 %copy-start.14 = (f32[3,4096]{1,0:T(4,128)S(1)}, f32[3,4096]{1,0:T(4,128)}, u32[]{:S(2)}) copy-start(f32[3,4096]{1,0:T(4,128)} %param.12) | copy-start | bytes 147460
  45.7 229.0 %reduce-scatter.2.cloned.1.call-start = ((), (), s32[]{:S(2)}) async-start(), calls=%async_computation.6 | async-start | bytes 5308416 | tf_op jit(solution)/shard_map/reduce_scatter | solution.py:160
  45.9 69.5 %collective-permute-start.2 = (bf16[3,1024,512]{2,1,0:T(8,128)(2,1)}, bf16[3,1024,512]{2,1,0:T(8,128)(2,1)}, u32[]{:S(2)}, u32[]{:S(2)}) collective-permute-start(bf16[3,1024,512]{2,1,0:T(8,128)(2,1)} %get-tuple-element.34), channel_id=1, source_target_pairs={{0,16},{8,24},{16,0},{24,8},{1,17},{9,25},{17,1},{25,9},{2,18},{10... | collective-permute-start | bytes 9437192 | tf_op jit(solution)/shard_map/ppermute | solution.py:66
  46.6 72.1 %collective-permute-start.1 = (bf16[3,1024,512]{2,1,0:T(8,128)(2,1)}, bf16[3,1024,512]{2,1,0:T(8,128)(2,1)}, u32[]{:S(2)}, u32[]{:S(2)}) collective-permute-start(bf16[3,1024,512]{2,1,0:T(8,128)(2,1)} %get-tuple-element.34), channel_id=1, source_target_pairs={{0,8},{8,0},{16,24},{24,16},{1,9},{9,1},{17,25},{25,17},{2,10},{10... | collective-permute-start | bytes 9437192 | tf_op jit(solution)/shard_map/ppermute | solution.py:65
  49.5 3.0 collective-permute-start.5
  118.1 37.6 %collective-permute-start.3 = (bf16[3,512,512]{2,1,0:T(8,128)(2,1)}, bf16[3,512,512]{2,1,0:T(8,128)(2,1)}, u32[]{:S(2)}, u32[]{:S(2)}) collective-permute-start(bf16[3,512,512]{2,1,0:T(8,128)(2,1)} %slice.104), channel_id=1, source_target_pairs={{0,8},{8,0},{16,24},{24,16},{1,9},{9,1},{17,25},{25,17},{2,10},{10... | collective-permute-start | bytes 4718600 | tf_op jit(solution)/shard_map/ppermute | solution.py:75
  121.4 37.6 %collective-permute-start.4 = (bf16[3,512,512]{2,1,0:T(8,128)(2,1)}, bf16[3,512,512]{2,1,0:T(8,128)(2,1)}, u32[]{:S(2)}, u32[]{:S(2)}) collective-permute-start(bf16[3,512,512]{2,1,0:T(8,128)(2,1)} %slice.105), channel_id=1, source_target_pairs={{0,16},{8,24},{16,0},{24,8},{1,17},{9,25},{17,1},{25,9},{2,18},{10... | collective-permute-start | bytes 4718600 | tf_op jit(solution)/shard_map/ppermute | solution.py:76
  126.1 4.0 %copy-start = (f32[640,4096]{1,0:T(8,128)}, f32[640,4096]{1,0:T(8,128)S(1)}, u32[]{:S(2)}) copy-start(f32[640,4096]{1,0:T(8,128)S(1)} %convert_element_type.83) | copy-start | bytes 31457284
  134.0 10.9 %slice-start = ((s8[5242880]{0:T(1024)(128)(4,1)}), s8[4194304]{0:T(1024)(128)(4,1)S(1)}, s32[]{:S(2)}) async-start(s8[5242880]{0:T(1024)(128)(4,1)} %bitcast.137), calls=%async_computation.8 | async-start | bytes 8388608
  138.1 6.8 %slice-start.1 = ((s8[5242880]{0:T(1024)(128)(4,1)}), s8[1048576]{0:T(1024)(128)(4,1)S(1)}, s32[]{:S(2)}) async-start(s8[5242880]{0:T(1024)(128)(4,1)} %bitcast.137), calls=%async_computation.9 | async-start | bytes 2097152
  142.2 33.2 %collective-permute-start.6 = (bf16[1,1024,512]{2,1,0:T(8,128)(2,1)}, bf16[1,1024,512]{2,1,0:T(8,128)(2,1)}, u32[]{:S(2)}, u32[]{:S(2)}) collective-permute-start(bf16[1,1024,512]{2,1,0:T(8,128)(2,1)} %get-tuple-element.17), channel_id=1, source_target_pairs={{0,8},{8,0},{16,24},{24,16},{1,9},{9,1},{17,25},{25,17},{2,10},{10... | collective-permute-start | bytes 3145736 | tf_op jit(solution)/shard_map/ppermute | solution.py:65
  143.4 34.9 %collective-permute-start.7 = (bf16[1,1024,512]{2,1,0:T(8,128)(2,1)}, bf16[1,1024,512]{2,1,0:T(8,128)(2,1)}, u32[]{:S(2)}, u32[]{:S(2)}) collective-permute-start(bf16[1,1024,512]{2,1,0:T(8,128)(2,1)} %get-tuple-element.17), channel_id=1, source_target_pairs={{0,16},{8,24},{16,0},{24,8},{1,17},{9,25},{17,1},{25,9},{2,18},{10... | collective-permute-start | bytes 3145736 | tf_op jit(solution)/shard_map/ppermute | solution.py:66
  168.0 1.8 copy-start.2
  168.0 1.9 copy-start.3
  169.9 2.9 copy-start.5
  188.5 10.8 %collective-permute-start.8 = (bf16[1,512,512]{2,1,0:T(8,128)(2,1)S(1)}, bf16[1,512,512]{2,1,0:T(8,128)(2,1)S(1)}, u32[]{:S(2)}, u32[]{:S(2)}) collective-permute-start(bf16[1,512,512]{2,1,0:T(8,128)(2,1)S(1)} %slice.109), channel_id=1, source_target_pairs={{0,8},{8,0},{16,24},{24,16},{1,9},{9,1},{17,25},{25,17},{2,10},{10... | collective-permute-start | bytes 1572872 | tf_op jit(solution)/shard_map/ppermute | solution.py:75
  191.1 11.4 %copy-start.13 = (bf16[576,512]{1,0:T(8,128)(2,1)S(1)}, bf16[576,512]{1,0:T(8,128)(2,1)}, u32[]{:S(2)}) copy-start(bf16[576,512]{1,0:T(8,128)(2,1)} %reshape.238) | copy-start | bytes 1769476
  191.1 10.6 %collective-permute-start.9 = (bf16[1,512,512]{2,1,0:T(8,128)(2,1)S(1)}, bf16[1,512,512]{2,1,0:T(8,128)(2,1)S(1)}, u32[]{:S(2)}, u32[]{:S(2)}) collective-permute-start(bf16[1,512,512]{2,1,0:T(8,128)(2,1)S(1)} %slice.110), channel_id=1, source_target_pairs={{0,16},{8,24},{16,0},{24,8},{1,17},{9,25},{17,1},{25,9},{2,18},{10... | collective-permute-start | bytes 1572872 | tf_op jit(solution)/shard_map/ppermute | solution.py:76
  212.3 63.6 %collective-permute-start.10 = (bf16[2,1024,512]{2,1,0:T(8,128)(2,1)}, bf16[2,1024,512]{2,1,0:T(8,128)(2,1)}, u32[]{:S(2)}, u32[]{:S(2)}) collective-permute-start(bf16[2,1024,512]{2,1,0:T(8,128)(2,1)} %slice_select_fusion), channel_id=1, source_target_pairs={{0,8},{8,0},{16,24},{24,16},{1,9},{9,1},{17,25},{25,17},{2,10},{10... | collective-permute-start | bytes 6291464 | tf_op jit(solution)/shard_map/ppermute | solution.py:65
  212.9 63.0 %collective-permute-start.11 = (bf16[2,1024,512]{2,1,0:T(8,128)(2,1)}, bf16[2,1024,512]{2,1,0:T(8,128)(2,1)}, u32[]{:S(2)}, u32[]{:S(2)}) collective-permute-start(bf16[2,1024,512]{2,1,0:T(8,128)(2,1)} %slice_select_fusion), channel_id=1, source_target_pairs={{0,16},{8,24},{16,0},{24,8},{1,17},{9,25},{17,1},{25,9},{2,18},{10... | collective-permute-start | bytes 6291464 | tf_op jit(solution)/shard_map/ppermute | solution.py:66
  216.5 45.3 %all-to-all-start.1 = ((bf16[64,4,1024]{2,0,1:T(8,128)(2,1)}), bf16[64,4,1024]{2,0,1:T(8,128)(2,1)}, u32[]{:S(2)}, u32[]{:S(2)}) async-start(bf16[64,4,1024]{2,0,1:T(8,128)(2,1)} %bitcast.143), calls=%async_computation.2 | async-start | bytes 1048576 | tf_op jit(solution)/shard_map/all_to_all | solution.py:163
  264.5 11.5 %copy-start.1 = (bf16[640,512]{1,0:T(8,128)(2,1)S(1)}, bf16[640,512]{1,0:T(8,128)(2,1)}, u32[]{:S(2)}) copy-start(bf16[640,512]{1,0:T(8,128)(2,1)} %broadcast_select_fusion.3) | copy-start | bytes 1966084
  264.5 10.2 %all-to-all-start.2 = ((f32[4,64,512]{2,1,0:T(8,128)}), f32[4,64,512]{2,1,0:T(8,128)S(1)}, u32[]{:S(2)}, u32[]{:S(2)}) async-start(f32[4,64,512]{2,1,0:T(8,128)} %fusion.38), calls=%async_computation.3 | async-start | bytes 1048576 | tf_op jit(solution)/shard_map/all_to_all | solution.py:169
  268.1 61.2 %all-gather.5.cloned.1.call-start = ((), (), s32[]{:S(2)}) async-start(), calls=%async_computation.7 | async-start | bytes 5308416 | tf_op jit(solution)/shard_map/all_gather | solution.py:175
  278.3 24.3 %copy-start.4 = (bf16[1,1024,512]{2,1,0:T(8,128)(2,1)S(1)}, bf16[1,1024,512]{2,1,0:T(8,128)(2,1)}, u32[]{:S(2)}) copy-start(bf16[1,1024,512]{2,1,0:T(8,128)(2,1)} %get-tuple-element.27) | copy-start | bytes 3145732
  278.3 18.8 %collective-permute-start.12 = (bf16[2,512,512]{2,1,0:T(8,128)(2,1)S(1)}, bf16[2,512,512]{2,1,0:T(8,128)(2,1)S(1)}, u32[]{:S(2)}, u32[]{:S(2)}) collective-permute-start(bf16[2,512,512]{2,1,0:T(8,128)(2,1)S(1)} %slice.117), channel_id=1, source_target_pairs={{0,8},{8,0},{16,24},{24,16},{1,9},{9,1},{17,25},{25,17},{2,10},{10... | collective-permute-start | bytes 3145736 | tf_op jit(solution)/shard_map/ppermute | solution.py:75
  281.1 18.2 %collective-permute-start.13 = (bf16[2,512,512]{2,1,0:T(8,128)(2,1)S(1)}, bf16[2,512,512]{2,1,0:T(8,128)(2,1)S(1)}, u32[]{:S(2)}, u32[]{:S(2)}) collective-permute-start(bf16[2,512,512]{2,1,0:T(8,128)(2,1)S(1)} %slice.118), channel_id=1, source_target_pairs={{0,16},{8,24},{16,0},{24,8},{1,17},{9,25},{17,1},{25,9},{2,18},{10... | collective-permute-start | bytes 3145736 | tf_op jit(solution)/shard_map/ppermute | solution.py:76
  297.1 2.2 copy-start.9
  299.3 1.0 copy-start.11
  305.4 16.3 %collective-permute-start.14 = (bf16[1,1024,512]{2,1,0:T(8,128)(2,1)}, bf16[1,1024,512]{2,1,0:T(8,128)(2,1)S(1)}, u32[]{:S(2)}, u32[]{:S(2)}) collective-permute-start(bf16[1,1024,512]{2,1,0:T(8,128)(2,1)} %get-tuple-element.31), channel_id=1, source_target_pairs={{0,8},{8,0},{16,24},{24,16},{1,9},{9,1},{17,25},{25,17},{2,10},{10... | collective-permute-start | bytes 3145736 | tf_op jit(solution)/shard_map/ppermute | solution.py:65
  306.3 16.6 %collective-permute-start.15 = (bf16[1,1024,512]{2,1,0:T(8,128)(2,1)}, bf16[1,1024,512]{2,1,0:T(8,128)(2,1)S(1)}, u32[]{:S(2)}, u32[]{:S(2)}) collective-permute-start(bf16[1,1024,512]{2,1,0:T(8,128)(2,1)} %get-tuple-element.31), channel_id=1, source_target_pairs={{0,16},{8,24},{16,0},{24,8},{1,17},{9,25},{17,1},{25,9},{2,18},{10... | collective-permute-start | bytes 3145736 | tf_op jit(solution)/shard_map/ppermute | solution.py:66
  321.8 11.8 %copy-start.6 = (bf16[1,1024,512]{2,1,0:T(8,128)(2,1)}, bf16[1,1024,512]{2,1,0:T(8,128)(2,1)S(1)}, u32[]{:S(2)}) copy-start(bf16[1,1024,512]{2,1,0:T(8,128)(2,1)S(1)} %collective-permute-done.14) | copy-start | bytes 3145732
  322.9 10.7 %copy-start.8 = (bf16[1,1024,512]{2,1,0:T(8,128)(2,1)}, bf16[1,1024,512]{2,1,0:T(8,128)(2,1)S(1)}, u32[]{:S(2)}) copy-start(bf16[1,1024,512]{2,1,0:T(8,128)(2,1)S(1)} %collective-permute-done.15) | copy-start | bytes 3145732
  333.6 3.1 copy-start.10
  340.4 3.1 copy-start.12
  344.5 4.8 %copy-start.7 = (bf16[1,1024,512]{2,1,0:T(8,128)(2,1)S(1)}, bf16[1,1024,512]{2,1,0:T(8,128)(2,1)}, u32[]{:S(2)}) copy-start(bf16[1,1024,512]{2,1,0:T(8,128)(2,1)} %copy-done.6) | copy-start | bytes 3145732
  347.8 14.4 %collective-permute-start.16 = (bf16[1,512,512]{2,1,0:T(8,128)(2,1)}, bf16[1,512,512]{2,1,0:T(8,128)(2,1)}, u32[]{:S(2)}, u32[]{:S(2)}) collective-permute-start(bf16[1,512,512]{2,1,0:T(8,128)(2,1)} %slice.94), channel_id=1, source_target_pairs={{0,8},{8,0},{16,24},{24,16},{1,9},{9,1},{17,25},{25,17},{2,10},{10... | collective-permute-start | bytes 1572872 | tf_op jit(solution)/shard_map/ppermute | solution.py:75
  350.2 14.1 %collective-permute-start.17 = (bf16[1,512,512]{2,1,0:T(8,128)(2,1)}, bf16[1,512,512]{2,1,0:T(8,128)(2,1)}, u32[]{:S(2)}, u32[]{:S(2)}) collective-permute-start(bf16[1,512,512]{2,1,0:T(8,128)(2,1)} %slice.95), channel_id=1, source_target_pairs={{0,16},{8,24},{16,0},{24,8},{1,17},{9,25},{17,1},{25,9},{2,18},{10... | collective-permute-start | bytes 1572872 | tf_op jit(solution)/shard_map/ppermute | solution.py:76
Sparse Core Ops, SparseCore 0:
  45.8 55.3 all-gather.2
  209.2 55.2 reduce-scatter.1
  277.1 52.1 all-gather.4

commit v5 on v4

--- a/solution.py
+++ b/solution.py
@@ -149,8 +149,7 @@
     out_far = far(out_near)
     projected = (accum * scale[:pass_rows, None, None]).astype(jnp.bfloat16)
     shaped = projected.reshape(per_question, length, 3, head_block)
-    values = after(shaped[:, :, 2], *blocks(out_near))
-    context = attend(shaped[:, :, 0], shaped[:, :, 1], values, head_count)
+    context = attend(shaped[:, :, 0], shaped[:, :, 1], shaped[:, :, 2], head_count)
     enc_partial = lax.dot_general(
         context,
         in_order(out_near + out_far, shard_rows),

time: 396 us -> 387 us (0.977)
  waiting for transfers between devices: 181 us -> 177 us
  transfers between devices with their start and end apart: 24 -> 24, of which waited for: 17 -> 15; matrix products, arithmetic and copies ran while one was open for 21% -> 24% of each run, Pallas kernels for 0% -> 0%
where the time goes in v5:
time: 387 us; the launch traced here: 386 us
  waiting for transfers between devices  177 us (46%)
  local copies, waits for them, and re-layouts  65.8 us (17%)
  matrix products  43.6 us (11%)
  other arithmetic  38.4 us (10%)
  starting transfers between devices  28.8 us (7%)
  blocking collectives  17.8 us (5%)
  between operations  14.3 us (4%)
    ppermute x4, waiting for transfers between devices, near(): lax.ppermute(block, 'shard', Y_PAIRS)  60 us
    all_to_all x1, waiting for transfers between devices, body(): lax.all_to_all(after(targ_normed, enc_partial), 'shard', split_axis=1, co...  38.4 us
    ppermute x4, waiting for transfers between devices, far(): top = lax.ppermute(pieces[2][2][:, :rows // 2], 'shard', X_PAIRS)  35.6 us
    dot_general x10, matrix products, project(): jnp.einsum('rn,knh->rkh', part, block, preferred_element_type=jnp.float32)  28 us
    all_to_all x1, blocking collectives, body(): lax.all_to_all(dec_partial, ('mp', 'segment'), split_axis=1, concat_axis=...  17.8 us
    ppermute x4, waiting for transfers between devices, near(): lax.ppermute(block, 'shard', X_PAIRS)  13.1 us
    gather x1, local copies, waits for them, and re-layouts, body(): embedded_part = jnp.take(vocab_table, all_ids, axis=0)  11.2 us
    dynamic_update_slice x9, local copies, waits for them, and re-layouts, in_order(): lax.dynamic_update_slice_in_dim(whole, block[0], owner * shard_rows + fir...  10.2 us
  transfers between devices with their start and end apart: 24, of which 15 were waited for; matrix products, arithmetic and copies ran while one was open for 24% of the time, Pallas kernels for 0%

profile of v5, /device:TPU:0, one launch (start us, length us, event | category | flops | bytes accessed | tf_op | source)
XLA Modules:
  0.0 385.7 jit_solution(14812456501296723791)
XLA Ops:
  7.2 3.8 dynamic-slice_bitcast_fusion
  15.2 4.7 %all-to-all-start = ((s32[4,1,144]{2,1,0:T(1,128)}), s32[4,1,144]{2,1,0:T(1,128)S(1)}, u32[]{:S(2)}, u32[]{:S(2)}) async-start(s32[4,1,144]{2,1,0:T(1,128)} %reshape.285), calls=%async_computation | async-start | bytes 8192 | tf_op jit(solution)/shard_map/all_to_all | solution.py:123
  20.1 4.4 %all-to-all-done = s32[4,1,144]{2,1,0:T(1,128)S(1)} async-done(((s32[4,1,144]{2,1,0:T(1,128)}), s32[4,1,144]{2,1,0:T(1,128)S(1)}, u32[]{:S(2)}, u32[]{:S(2)}) %all-to-all-start) | async-done | bytes 2336 | tf_op jit(solution)/shard_map/all_to_all | solution.py:123
  26.6 5.7 %broadcast_select_fusion = (bf16[3,1024,512]{2,1,0:T(8,128)(2,1)}, bf16[3,1024,512]{2,1,0:T(8,128)(2,1)}) fusion(bf16[3,1024,512]{2,1,0:T(8,128)(2,1)S(1)} %collective-permute-done, pred[]{:T(512)S(6)} %eq.52, bf16[1,4,1024,1024]{3,2,1,0:T(8,128)(2,1)} %param.13, s32[]{:T(128)S(6)} %select_n.144), kind=kLoop, calls=%fused_computation.18 | loop fusion | flops 1572864 | bytes 12582917 | tf_op jit(solution)/shard_map/jit(_where)/select_n | solution.py:43
  32.4 11.2 %gather_fusion.2 = bf16[640,512]{1,0:T(8,128)(2,1)} fusion(bf16[16384,512]{1,0:T(8,128)(2,1)} %param.11, s32[1024]{0:T(1024)S(1)} %pad_clamp_fusion), kind=kCustom, calls=%fused_computation.2 | custom fusion | bytes 1313280 | tf_op jit(solution)/shard_map/jit(_take)/gather | solution.py:134
  43.6 2.1 broadcast_select_fusion.3
  47.2 2.3 dynamic-slice_bitcast_fusion.2
  49.5 3.0 collective-permute-done.5
  52.5 3.0 broadcast_select_fusion.2
  55.5 60.0 %collective-permute-done.2 = bf16[3,1024,512]{2,1,0:T(8,128)(2,1)} collective-permute-done((bf16[3,1024,512]{2,1,0:T(8,128)(2,1)}, bf16[3,1024,512]{2,1,0:T(8,128)(2,1)}, u32[]{:S(2)}, u32[]{:S(2)}) %collective-permute-start.2) | collective-permute-done | bytes 3145760 | tf_op jit(solution)/shard_map/ppermute | solution.py:66
  115.4 2.8 slice.104
  118.8 2.6 slice.105
  122.3 3.9 %convert_element_type.83 = f32[640,4096]{1,0:T(8,128)S(1)} convert(bf16[640,4096]{1,0:T(8,128)(2,1)} %all-gather.3.cloned.1.call-done) | non-fusion elementwise | flops 2621440 | bytes 15728640 | tf_op jit(solution)/shard_map/convert_element_type | solution.py:138
  127.4 2.8 copy-done
  130.2 3.9 %fusion.23 = f32[576,3,512]{2,0,1:T(8,128)S(1)} fusion(bf16[3,1024,512]{2,1,0:T(8,128)(2,1)} %get-tuple-element.32, bf16[576,4096]{1,0:T(8,128)(2,1)S(1)} %fusion.4, s32[]{:T(128)S(6)} %select_n.149), kind=kOutput, calls=%fused_computation.42 | convolution fusion | flops 1811939328 | bytes 7864324 | tf_op jit(solution)/shard_map/rn,knh->rkh/dot_general | solution.py:88
  134.1 4.0 %fusion.21 = f32[576,3,512]{2,0,1:T(8,128)S(1)} fusion(bf16[3,1024,512]{2,1,0:T(8,128)(2,1)} %collective-permute-done.1, bf16[576,4096]{1,0:T(8,128)(2,1)S(1)} %fusion.4, s32[]{:T(128)S(6)} %select_n.150), kind=kOutput, calls=%fused_computation.40 | convolution fusion | flops 1811939328 | bytes 7864324 | tf_op jit(solution)/shard_map/rn,knh->rkh/dot_general | solution.py:88
  138.1 4.1 %add_add_fusion = f32[576,3,512]{2,0,1:T(8,128)S(1)} fusion(f32[576,3,512]{2,0,1:T(8,128)S(1)} %fusion.23, f32[576,3,512]{2,0,1:T(8,128)S(1)} %fusion.21, bf16[3,1024,512]{2,1,0:T(8,128)(2,1)} %collective-permute-done.2, bf16[576,4096]{1,0:T(8,128)(2,1)S(1)} %fusion.4, s32[]{:T(128)S(6)} %select_n.151), kind=kOutput, calls=%fused_computation.15 | convolution fusion | flops 1813708800 | bytes 14942212 | tf_op jit(solution)/shard_map/rn,knh->rkh/dot_general | solution.py:88
  146.0 9.8 %collective-permute-done.3 = bf16[3,512,512]{2,1,0:T(8,128)(2,1)} collective-permute-done((bf16[3,512,512]{2,1,0:T(8,128)(2,1)}, bf16[3,512,512]{2,1,0:T(8,128)(2,1)}, u32[]{:S(2)}, u32[]{:S(2)}) %collective-permute-start.3) | collective-permute-done | bytes 1572896 | tf_op jit(solution)/shard_map/ppermute | solution.py:75
  155.9 2.5 fusion.53
  159.1 2.7 multiply_convert_fusion
  163.1 2.5 reshape_squeeze.11
  165.5 2.5 reshape_squeeze.10
  168.0 2.5 reshape_squeeze.9
  170.5 2.4 fusion.26
  172.9 4.2 %fusion.85 = (f32[12,8,48]{2,1,0:T(8,128)S(1)}, f32[12,8,48,48]{2,3,1,0:T(8,128)S(1)}) fusion(f32[12,8,48,48]{2,3,1,0:T(8,128)S(1)} %fusion.26), kind=kOutput, calls=%fused_computation.142 | output fusion | flops 884783 | bytes 1787904 | tf_op jit(solution)/shard_map/sub | solution.py:22
  179.1 2.7 reshape.234
  190.4 3.3 collective-permute-done.8
  193.8 2.6 collective-permute-done.9
  196.4 4.3 %convolution_convert_fusion = bf16[576,4096]{1,0:T(8,128)(2,1)} fusion(bf16[576,512]{1,0:T(8,128)(2,1)S(1)} %copy-done.11, bf16[4096,512]{1,0:T(8,128)(2,1)S(1)} %bitcast_dynamic-update-slice_fusion.8), kind=kOutput, calls=%fused_computation.12 | convolution fusion | flops 2418278400 | bytes 9502720 | tf_op jit(solution)/shard_map/dot_general | solution.py:153
  200.7 3.2 slice_select_fusion
  207.5 4.1 %all-to-all-start.1 = ((bf16[64,4,1024]{2,0,1:T(8,128)(2,1)}), bf16[64,4,1024]{2,0,1:T(8,128)(2,1)}, u32[]{:S(2)}, u32[]{:S(2)}) async-start(bf16[64,4,1024]{2,0,1:T(8,128)(2,1)} %bitcast.145), calls=%async_computation.2 | async-start | bytes 1048576 | tf_op jit(solution)/shard_map/all_to_all | solution.py:162
  211.7 38.4 %all-to-all-done.1 = bf16[64,4,1024]{2,0,1:T(8,128)(2,1)} async-done(((bf16[64,4,1024]{2,0,1:T(8,128)(2,1)}), bf16[64,4,1024]{2,0,1:T(8,128)(2,1)}, u32[]{:S(2)}, u32[]{:S(2)}) %all-to-all-start.1) | async-done | bytes 524320 | tf_op jit(solution)/shard_map/all_to_all | solution.py:162
  250.1 2.7 fusion.38
  252.7 3.6 all-to-all-start.2
  256.7 8.7 %all-to-all-done.2 = f32[4,64,512]{2,1,0:T(8,128)S(1)} async-done(((f32[4,64,512]{2,1,0:T(8,128)}), f32[4,64,512]{2,1,0:T(8,128)S(1)}, u32[]{:S(2)}, u32[]{:S(2)}) %all-to-all-start.2) | async-done | bytes 524320 | tf_op jit(solution)/shard_map/all_to_all | solution.py:168
  272.2 14.0 %collective-permute-done.12 = bf16[2,512,512]{2,1,0:T(8,128)(2,1)S(1)} collective-permute-done((bf16[2,512,512]{2,1,0:T(8,128)(2,1)S(1)}, bf16[2,512,512]{2,1,0:T(8,128)(2,1)S(1)}, u32[]{:S(2)}, u32[]{:S(2)}) %collective-permute-start.12) | collective-permute-done | bytes 1048608 | tf_op jit(solution)/shard_map/ppermute | solution.py:75
  286.2 2.4 collective-permute-done.13
  289.7 2.3 broadcast.152
  292.0 2.9 bitcast_dynamic-update-slice_fusion.2
  296.9 13.1 %collective-permute-done.14 = bf16[1,1024,512]{2,1,0:T(8,128)(2,1)S(1)} collective-permute-done((bf16[1,1024,512]{2,1,0:T(8,128)(2,1)}, bf16[1,1024,512]{2,1,0:T(8,128)(2,1)S(1)}, u32[]{:S(2)}, u32[]{:S(2)}) %collective-permute-start.14) | collective-permute-done | bytes 1048608 | tf_op jit(solution)/shard_map/ppermute | solution.py:65
  312.2 7.9 %all-gather.5.cloned.1.call-done = bf16[576,4096]{1,0:T(8,128)(2,1)} async-done(((bf16[576,512]{1,0:T(8,128)(2,1)}), bf16[576,4096]{1,0:T(8,128)(2,1)}) %all-gather.5.cloned.1.call-update) | async-done | bytes 4718608 | tf_op jit(solution)/shard_map/all_gather | solution.py:174
  320.1 4.3 %fusion.3 = (f32[576]{0:T(1024)S(1)}, bf16[576,4096]{1,0:T(8,128)(2,1)S(1)}) fusion(bf16[576,4096]{1,0:T(8,128)(2,1)} %all-gather.5.cloned.1.call-done, f32[4096]{0:T(1024)S(1)} %bitcast.149), kind=kLoop, calls=%fused_computation.9 | loop fusion | flops 11795904 | bytes 9455872 | tf_op jit(solution)/shard_map/reduce_sum | solution.py:179
  324.4 3.1 fusion.15
  328.3 3.0 fusion.11
  331.3 3.1 fusion.13
  344.6 8.5 %collective-permute-done.16 = bf16[1,512,512]{2,1,0:T(8,128)(2,1)} collective-permute-done((bf16[1,512,512]{2,1,0:T(8,128)(2,1)}, bf16[1,512,512]{2,1,0:T(8,128)(2,1)}, u32[]{:S(2)}, u32[]{:S(2)}) %collective-permute-start.16) | collective-permute-done | bytes 524320 | tf_op jit(solution)/shard_map/ppermute | solution.py:75
  357.0 3.6 convolution_convert_fusion.1
  360.7 17.8 %all_to_all.40 = bf16[64,8,512]{2,0,1:T(8,128)(2,1)S(1)} all-to-all(bf16[64,8,512]{2,0,1:T(8,128)(2,1)S(1)} %bitcast.146), channel_id=1, replica_groups=mesh['shard'=4,'mp'=4,'segment'=2] {'mp','segment'}, dimensions={1} | all-to-all | bytes 1048576 | tf_op jit(solution)/shard_map/all_to_all | solution.py:191
  (150 shorter events, 58.6 us)
Async XLA Ops:
  7.2 4.3 %copy-start.13 = (s32[64,48]{0,1:T(8,128)S(1)}, s32[64,48]{0,1:T(8,128)}, u32[]{:S(2)}) copy-start(s32[64,48]{0,1:T(8,128)} %param.7) | copy-start | bytes 36868
  7.2 4.8 %copy-start.16 = (s32[48,1]{0,1:T(1,128)S(1)}, s32[48,1]{0,1:T(1,128)}, u32[]{:S(2)}) copy-start(s32[48,1]{0,1:T(1,128)} %param.9) | copy-start | bytes 580
  7.2 6.1 %copy-start.14 = (s32[4,12]{1,0:T(4,128)S(1)}, s32[4,12]{1,0:T(4,128)}, u32[]{:S(2)}) copy-start(s32[4,12]{1,0:T(4,128)} %param.8) | copy-start | bytes 580
  7.2 19.3 %copy-start.15 = (s32[1,64]{1,0:T(1,128)S(1)}, s32[1,64]{1,0:T(1,128)}, u32[]{:S(2)}) copy-start(s32[1,64]{1,0:T(1,128)} %param.10) | copy-start | bytes 772
  11.0 15.6 %collective-permute-start = (bf16[3,1024,512]{2,1,0:T(8,128)(2,1)}, bf16[3,1024,512]{2,1,0:T(8,128)(2,1)S(1)}, u32[]{:S(2)}, u32[]{:S(2)}) collective-permute-start(bf16[3,1024,512]{2,1,0:T(8,128)(2,1)} %dynamic-slice_bitcast_fusion), channel_id=1, source_target_pairs={{0,1},{1,0},{2,3},{3,2},{4,5},{5,4},{6,7},{7,6},{8,9},{9,8},{10,11... | collective-permute-start | bytes 9437192 | tf_op jit(solution)/shard_map/ppermute | solution.py:42
  15.2 9.4 %all-to-all-start = ((s32[4,1,144]{2,1,0:T(1,128)}), s32[4,1,144]{2,1,0:T(1,128)S(1)}, u32[]{:S(2)}, u32[]{:S(2)}) async-start(s32[4,1,144]{2,1,0:T(1,128)} %reshape.285), calls=%async_computation | async-start | bytes 8192 | tf_op jit(solution)/shard_map/all_to_all | solution.py:123
  19.9 102.4 %all-gather.3.cloned.1.call-start = ((), (), s32[]{:S(2)}) async-start(), calls=%async_computation.5 | async-start | bytes 5898240 | tf_op jit(solution)/shard_map/all_gather | solution.py:135
  43.6 5.8 %copy-start.12 = (f32[3,4096]{1,0:T(4,128)S(1)}, f32[3,4096]{1,0:T(4,128)}, u32[]{:S(2)}) copy-start(f32[3,4096]{1,0:T(4,128)} %param.12) | copy-start | bytes 147460
  45.8 219.7 %reduce-scatter.2.cloned.1.call-start = ((), (), s32[]{:S(2)}) async-start(), calls=%async_computation.6 | async-start | bytes 5308416 | tf_op jit(solution)/shard_map/reduce_scatter | solution.py:159
  46.0 69.5 %collective-permute-start.2 = (bf16[3,1024,512]{2,1,0:T(8,128)(2,1)}, bf16[3,1024,512]{2,1,0:T(8,128)(2,1)}, u32[]{:S(2)}, u32[]{:S(2)}) collective-permute-start(bf16[3,1024,512]{2,1,0:T(8,128)(2,1)} %get-tuple-element.32), channel_id=1, source_target_pairs={{0,16},{8,24},{16,0},{24,8},{1,17},{9,25},{17,1},{25,9},{2,18},{10... | collective-permute-start | bytes 9437192 | tf_op jit(solution)/shard_map/ppermute | solution.py:66
  46.6 72.2 %collective-permute-start.1 = (bf16[3,1024,512]{2,1,0:T(8,128)(2,1)}, bf16[3,1024,512]{2,1,0:T(8,128)(2,1)}, u32[]{:S(2)}, u32[]{:S(2)}) collective-permute-start(bf16[3,1024,512]{2,1,0:T(8,128)(2,1)} %get-tuple-element.32), channel_id=1, source_target_pairs={{0,8},{8,0},{16,24},{24,16},{1,9},{9,1},{17,25},{25,17},{2,10},{10... | collective-permute-start | bytes 9437192 | tf_op jit(solution)/shard_map/ppermute | solution.py:65
  49.5 3.0 collective-permute-start.5
  118.2 37.6 %collective-permute-start.3 = (bf16[3,512,512]{2,1,0:T(8,128)(2,1)}, bf16[3,512,512]{2,1,0:T(8,128)(2,1)}, u32[]{:S(2)}, u32[]{:S(2)}) collective-permute-start(bf16[3,512,512]{2,1,0:T(8,128)(2,1)} %slice.104), channel_id=1, source_target_pairs={{0,8},{8,0},{16,24},{24,16},{1,9},{9,1},{17,25},{25,17},{2,10},{10... | collective-permute-start | bytes 4718600 | tf_op jit(solution)/shard_map/ppermute | solution.py:75
  121.4 37.6 %collective-permute-start.4 = (bf16[3,512,512]{2,1,0:T(8,128)(2,1)}, bf16[3,512,512]{2,1,0:T(8,128)(2,1)}, u32[]{:S(2)}, u32[]{:S(2)}) collective-permute-start(bf16[3,512,512]{2,1,0:T(8,128)(2,1)} %slice.105), channel_id=1, source_target_pairs={{0,16},{8,24},{16,0},{24,8},{1,17},{9,25},{17,1},{25,9},{2,18},{10... | collective-permute-start | bytes 4718600 | tf_op jit(solution)/shard_map/ppermute | solution.py:76
  126.2 4.0 %copy-start = (f32[640,4096]{1,0:T(8,128)}, f32[640,4096]{1,0:T(8,128)S(1)}, u32[]{:S(2)}) copy-start(f32[640,4096]{1,0:T(8,128)S(1)} %convert_element_type.83) | copy-start | bytes 31457284
  134.1 10.9 %slice-start = ((s8[5242880]{0:T(1024)(128)(4,1)}), s8[4194304]{0:T(1024)(128)(4,1)S(1)}, s32[]{:S(2)}) async-start(s8[5242880]{0:T(1024)(128)(4,1)} %bitcast.139), calls=%async_computation.8 | async-start | bytes 8388608
  138.1 6.8 %slice-start.1 = ((s8[5242880]{0:T(1024)(128)(4,1)}), s8[1048576]{0:T(1024)(128)(4,1)S(1)}, s32[]{:S(2)}) async-start(s8[5242880]{0:T(1024)(128)(4,1)} %bitcast.139), calls=%async_computation.9 | async-start | bytes 2097152
  142.2 43.8 %collective-permute-start.6 = (bf16[1,1024,512]{2,1,0:T(8,128)(2,1)}, bf16[1,1024,512]{2,1,0:T(8,128)(2,1)}, u32[]{:S(2)}, u32[]{:S(2)}) collective-permute-start(bf16[1,1024,512]{2,1,0:T(8,128)(2,1)} %get-tuple-element.16), channel_id=1, source_target_pairs={{0,8},{8,0},{16,24},{24,16},{1,9},{9,1},{17,25},{25,17},{2,10},{10... | collective-permute-start | bytes 3145736 | tf_op jit(solution)/shard_map/ppermute | solution.py:65
  143.5 39.9 %collective-permute-start.7 = (bf16[1,1024,512]{2,1,0:T(8,128)(2,1)}, bf16[1,1024,512]{2,1,0:T(8,128)(2,1)}, u32[]{:S(2)}, u32[]{:S(2)}) collective-permute-start(bf16[1,1024,512]{2,1,0:T(8,128)(2,1)} %get-tuple-element.16), channel_id=1, source_target_pairs={{0,16},{8,24},{16,0},{24,8},{1,17},{9,25},{17,1},{25,9},{2,18},{10... | collective-permute-start | bytes 3145736 | tf_op jit(solution)/shard_map/ppermute | solution.py:66
  172.9 4.3 %copy-start.6 = (bf16[12,48,8,64]{3,2,1,0:T(8,128)(2,1)S(1)}, bf16[12,48,8,64]{3,2,1,0:T(8,128)(2,1)}, u32[]{:S(2)}) copy-start(bf16[12,48,8,64]{3,2,1,0:T(8,128)(2,1)} %reshape_squeeze.9) | copy-start | bytes 1769476
  184.5 9.2 %collective-permute-start.8 = (bf16[1,512,512]{2,1,0:T(8,128)(2,1)S(1)}, bf16[1,512,512]{2,1,0:T(8,128)(2,1)S(1)}, u32[]{:S(2)}, u32[]{:S(2)}) collective-permute-start(bf16[1,512,512]{2,1,0:T(8,128)(2,1)S(1)} %slice.109), channel_id=1, source_target_pairs={{0,8},{8,0},{16,24},{24,16},{1,9},{9,1},{17,25},{25,17},{2,10},{10... | collective-permute-start | bytes 1572872 | tf_op jit(solution)/shard_map/ppermute | solution.py:75
  187.1 9.3 %copy-start.11 = (bf16[576,512]{1,0:T(8,128)(2,1)S(1)}, bf16[576,512]{1,0:T(8,128)(2,1)}, u32[]{:S(2)}) copy-start(bf16[576,512]{1,0:T(8,128)(2,1)} %reshape.234) | copy-start | bytes 1769476
  187.1 9.2 %collective-permute-start.9 = (bf16[1,512,512]{2,1,0:T(8,128)(2,1)S(1)}, bf16[1,512,512]{2,1,0:T(8,128)(2,1)S(1)}, u32[]{:S(2)}, u32[]{:S(2)}) collective-permute-start(bf16[1,512,512]{2,1,0:T(8,128)(2,1)S(1)} %slice.110), channel_id=1, source_target_pairs={{0,16},{8,24},{16,0},{24,8},{1,17},{9,25},{17,1},{25,9},{2,18},{10... | collective-permute-start | bytes 1572872 | tf_op jit(solution)/shard_map/ppermute | solution.py:76
  203.9 62.8 %collective-permute-start.10 = (bf16[2,1024,512]{2,1,0:T(8,128)(2,1)}, bf16[2,1024,512]{2,1,0:T(8,128)(2,1)}, u32[]{:S(2)}, u32[]{:S(2)}) collective-permute-start(bf16[2,1024,512]{2,1,0:T(8,128)(2,1)} %slice_select_fusion), channel_id=1, source_target_pairs={{0,8},{8,0},{16,24},{24,16},{1,9},{9,1},{17,25},{25,17},{2,10},{10... | collective-permute-start | bytes 6291464 | tf_op jit(solution)/shard_map/ppermute | solution.py:65
  204.5 62.3 %collective-permute-start.11 = (bf16[2,1024,512]{2,1,0:T(8,128)(2,1)}, bf16[2,1024,512]{2,1,0:T(8,128)(2,1)}, u32[]{:S(2)}, u32[]{:S(2)}) collective-permute-start(bf16[2,1024,512]{2,1,0:T(8,128)(2,1)} %slice_select_fusion), channel_id=1, source_target_pairs={{0,16},{8,24},{16,0},{24,8},{1,17},{9,25},{17,1},{25,9},{2,18},{10... | collective-permute-start | bytes 6291464 | tf_op jit(solution)/shard_map/ppermute | solution.py:66
  207.5 42.5 %all-to-all-start.1 = ((bf16[64,4,1024]{2,0,1:T(8,128)(2,1)}), bf16[64,4,1024]{2,0,1:T(8,128)(2,1)}, u32[]{:S(2)}, u32[]{:S(2)}) async-start(bf16[64,4,1024]{2,0,1:T(8,128)(2,1)} %bitcast.145), calls=%async_computation.2 | async-start | bytes 1048576 | tf_op jit(solution)/shard_map/all_to_all | solution.py:162
  252.7 14.0 %copy-start.1 = (bf16[640,512]{1,0:T(8,128)(2,1)S(1)}, bf16[640,512]{1,0:T(8,128)(2,1)}, u32[]{:S(2)}) copy-start(bf16[640,512]{1,0:T(8,128)(2,1)} %broadcast_select_fusion.3) | copy-start | bytes 1966084
  252.7 12.7 %all-to-all-start.2 = ((f32[4,64,512]{2,1,0:T(8,128)}), f32[4,64,512]{2,1,0:T(8,128)S(1)}, u32[]{:S(2)}, u32[]{:S(2)}) async-start(f32[4,64,512]{2,1,0:T(8,128)} %fusion.38), calls=%async_computation.3 | async-start | bytes 1048576 | tf_op jit(solution)/shard_map/all_to_all | solution.py:168
  256.3 63.8 %all-gather.5.cloned.1.call-start = ((), (), s32[]{:S(2)}) async-start(), calls=%async_computation.7 | async-start | bytes 5308416 | tf_op jit(solution)/shard_map/all_gather | solution.py:174
  269.1 22.9 %copy-start.2 = (bf16[1,1024,512]{2,1,0:T(8,128)(2,1)S(1)}, bf16[1,1024,512]{2,1,0:T(8,128)(2,1)}, u32[]{:S(2)}) copy-start(bf16[1,1024,512]{2,1,0:T(8,128)(2,1)} %get-tuple-element.25) | copy-start | bytes 3145732
  269.1 17.2 %collective-permute-start.12 = (bf16[2,512,512]{2,1,0:T(8,128)(2,1)S(1)}, bf16[2,512,512]{2,1,0:T(8,128)(2,1)S(1)}, u32[]{:S(2)}, u32[]{:S(2)}) collective-permute-start(bf16[2,512,512]{2,1,0:T(8,128)(2,1)S(1)} %slice.117), channel_id=1, source_target_pairs={{0,8},{8,0},{16,24},{24,16},{1,9},{9,1},{17,25},{25,17},{2,10},{10... | collective-permute-start | bytes 3145736 | tf_op jit(solution)/shard_map/ppermute | solution.py:75
  272.0 16.7 %collective-permute-start.13 = (bf16[2,512,512]{2,1,0:T(8,128)(2,1)S(1)}, bf16[2,512,512]{2,1,0:T(8,128)(2,1)S(1)}, u32[]{:S(2)}, u32[]{:S(2)}) collective-permute-start(bf16[2,512,512]{2,1,0:T(8,128)(2,1)S(1)} %slice.118), channel_id=1, source_target_pairs={{0,16},{8,24},{16,0},{24,8},{1,17},{9,25},{17,1},{25,9},{2,18},{10... | collective-permute-start | bytes 3145736 | tf_op jit(solution)/shard_map/ppermute | solution.py:76
  286.2 2.4 copy-start.7
  288.7 1.1 copy-start.9
  294.9 15.0 %collective-permute-start.14 = (bf16[1,1024,512]{2,1,0:T(8,128)(2,1)}, bf16[1,1024,512]{2,1,0:T(8,128)(2,1)S(1)}, u32[]{:S(2)}, u32[]{:S(2)}) collective-permute-start(bf16[1,1024,512]{2,1,0:T(8,128)(2,1)} %get-tuple-element.29), channel_id=1, source_target_pairs={{0,8},{8,0},{16,24},{24,16},{1,9},{9,1},{17,25},{25,17},{2,10},{10... | collective-permute-start | bytes 3145736 | tf_op jit(solution)/shard_map/ppermute | solution.py:65
  294.9 16.1 %collective-permute-start.15 = (bf16[1,1024,512]{2,1,0:T(8,128)(2,1)}, bf16[1,1024,512]{2,1,0:T(8,128)(2,1)S(1)}, u32[]{:S(2)}, u32[]{:S(2)}) collective-permute-start(bf16[1,1024,512]{2,1,0:T(8,128)(2,1)} %get-tuple-element.29), channel_id=1, source_target_pairs={{0,16},{8,24},{16,0},{24,8},{1,17},{9,25},{17,1},{25,9},{2,18},{10... | collective-permute-start | bytes 3145736 | tf_op jit(solution)/shard_map/ppermute | solution.py:66
  309.9 14.5 %copy-start.3 = (bf16[1,1024,512]{2,1,0:T(8,128)(2,1)}, bf16[1,1024,512]{2,1,0:T(8,128)(2,1)S(1)}, u32[]{:S(2)}) copy-start(bf16[1,1024,512]{2,1,0:T(8,128)(2,1)S(1)} %collective-permute-done.14) | copy-start | bytes 3145732
  311.1 13.3 %copy-start.5 = (bf16[1,1024,512]{2,1,0:T(8,128)(2,1)}, bf16[1,1024,512]{2,1,0:T(8,128)(2,1)S(1)}, u32[]{:S(2)}) copy-start(bf16[1,1024,512]{2,1,0:T(8,128)(2,1)S(1)} %collective-permute-done.15) | copy-start | bytes 3145732
  324.4 3.1 copy-start.8
  331.3 3.1 copy-start.10
  335.3 4.8 %copy-start.4 = (bf16[1,1024,512]{2,1,0:T(8,128)(2,1)S(1)}, bf16[1,1024,512]{2,1,0:T(8,128)(2,1)}, u32[]{:S(2)}) copy-start(bf16[1,1024,512]{2,1,0:T(8,128)(2,1)} %copy-done.3) | copy-start | bytes 3145732
  338.7 14.4 %collective-permute-start.16 = (bf16[1,512,512]{2,1,0:T(8,128)(2,1)}, bf16[1,512,512]{2,1,0:T(8,128)(2,1)}, u32[]{:S(2)}, u32[]{:S(2)}) collective-permute-start(bf16[1,512,512]{2,1,0:T(8,128)(2,1)} %slice.94), channel_id=1, source_target_pairs={{0,8},{8,0},{16,24},{24,16},{1,9},{9,1},{17,25},{25,17},{2,10},{10... | collective-permute-start | bytes 1572872 | tf_op jit(solution)/shard_map/ppermute | solution.py:75
  341.0 14.1 %collective-permute-start.17 = (bf16[1,512,512]{2,1,0:T(8,128)(2,1)}, bf16[1,512,512]{2,1,0:T(8,128)(2,1)}, u32[]{:S(2)}, u32[]{:S(2)}) collective-permute-start(bf16[1,512,512]{2,1,0:T(8,128)(2,1)} %slice.95), channel_id=1, source_target_pairs={{0,16},{8,24},{16,0},{24,8},{1,17},{9,25},{17,1},{25,9},{2,18},{10... | collective-permute-start | bytes 1572872 | tf_op jit(solution)/shard_map/ppermute | solution.py:76
Sparse Core Ops, SparseCore 0:
  45.9 55.3 all-gather.2
  200.9 54.6 reduce-scatter.1
  267.9 52.1 all-gather.4
